TPU v7x, 128 devices: a whole 4x4x4 slice. The times are simulated.
128 devices in a mesh: grp: 8 (over z_lo, x), blk: 16 (over z_hi, y, core).
Axes of the slice: x: 4, y: 4, z: 4 (z_hi: 2, z_lo: 2; z = z_hi * 2 + z_lo), core: 2. Of those that a mesh axis runs over, the one named last changes fastest.
Arguments:
- feats: bfloat16 [131072, 256], P(('grp', 'blk')), may hold values from -6 to 6
- weight: bfloat16 [256, 256], replicated, may hold values from -0.375 to 0.375
- cotangent: bfloat16 [131072, 256], P(('grp', 'blk')), may hold values from -6 to 6
- labels: int32 [131072], P(('grp', 'blk')), may hold values from -86 to 171
- tile_vals: bfloat16 [8, 16, 16, 32, 128, 128], P('grp', 'blk'), may hold values from -0.0625 to 0.0625
- tile_row: int32 [8, 16, 16, 32], P('grp', 'blk'), may hold values from 0 to 7
- tile_col: int32 [8, 16, 16, 32], P('grp', 'blk'), may hold values from 0 to 7
- tile_count: int32 [8, 16, 16], P('grp', 'blk'), may hold values from 1 to 32, as said below
- hub_vals: bfloat16 [8, 16, 16, 128, 128], P('grp', 'blk'), may hold values from -0.0625 to 0.0625
- hub_col: int32 [8, 16, 16], P('grp', 'blk'), may hold values from 0 to 7
- hub_dest: int32 [8, 16, 16, 1], P(None, 'blk'), may hold values from 0 to 7; in each aligned block of 16 rows (0 to 15, 16 to 31, ..., all dimensions but the last counted through in order) at most 4 rows name the same one
- hub_row: int32 [8, 16, 16], P(None, 'blk'), may hold values from 0 to 7
Outputs:
- layer_out: bfloat16 [131072, 256], P(('grp', 'blk'))
- grad_feats: bfloat16 [131072, 256], P(('grp', 'blk'))
- grad_weight: float32 [256, 256], replicated
Inputs may be any that keep to these rules, and one draw needn't show every extreme that they name: Only the first tile_count slots of a device's list for a source block are used; some device uses all 32. `hub_dest`: at most 4 of the 16 hub tiles of one device name the same group, and exactly 4 in some devices.
All inputs are finite; a program needn't handle non-finite values.
Results may differ from a plain program's by a relative error of at most 0.007.
Values may be sent and summed in bfloat16 or wider, within the bound.
A program may use at most 192 MiB of HBM per device.

v0:
```python
import math

import jax
import jax.numpy as jnp
from jax import lax
from jax.sharding import PartitionSpec as P


def shifted(value, axis, by):
    size = lax.axis_size(axis)
    return lax.ppermute(value, axis, [(i, (i + by) % size) for i in range(size)])


def local(
    feats,
    weight,
    cotangent,
    labels,
    tile_vals,
    tile_row,
    tile_col,
    tile_count,
    hub_vals,
    hub_col,
    hub_dest,
    hub_row,
):
    n_blocks = lax.axis_size("blk")
    n_groups = lax.axis_size("grp")
    my_block = lax.axis_index("blk")
    my_group = lax.axis_index("grp")
    rows_dev = feats.shape[0]
    width = feats.shape[1]
    tile_size = tile_vals.shape[-1]
    row_tiles = rows_dev // tile_size
    slot_count = tile_vals.shape[3]
    hub_count = hub_vals.shape[2]
    capacity = max(2, hub_count // 4)
    highest = lax.Precision.HIGHEST
    dev_vals = tile_vals[0, 0]
    dev_rows = tile_row[0, 0]
    dev_cols = tile_col[0, 0]
    dev_count = tile_count[0, 0]
    tile_range = jnp.arange(row_tiles, dtype=jnp.int32)
    slot_range = jnp.arange(slot_count, dtype=jnp.int32)
    proj = jnp.dot(feats, weight, preferred_element_type=jnp.float32).astype(jnp.bfloat16)
    own_panel = proj.reshape(row_tiles, tile_size, width)

    def block_parts(source):
        blk_vals = lax.dynamic_index_in_dim(dev_vals, source, 0, keepdims=False)
        blk_rows = lax.dynamic_index_in_dim(dev_rows, source, 0, keepdims=False)
        blk_cols = lax.dynamic_index_in_dim(dev_cols, source, 0, keepdims=False)
        blk_count = lax.dynamic_index_in_dim(dev_count, source, 0, keepdims=False)
        live_mask = (slot_range < blk_count).astype(jnp.float32)
        return (blk_vals, blk_rows, blk_cols, live_mask)

    def forward_block(source, panel_now):
        blk_vals, blk_rows, blk_cols, live_mask = block_parts(source)
        picked = jnp.take(panel_now, blk_cols, axis=0)
        product = jnp.einsum("tij,tjf->tif", blk_vals, picked, preferred_element_type=jnp.float32)
        placing = (blk_rows[:, None] == tile_range[None, :]).astype(jnp.float32) * live_mask[
            :, None
        ]
        return jnp.einsum("tr,tif->rif", placing, product, precision=highest)

    def backward_block(target, grad_tiles):
        blk_vals, blk_rows, blk_cols, live_mask = block_parts(target)
        picked = jnp.take(grad_tiles, blk_rows, axis=0)
        product = jnp.einsum("tij,tif->tjf", blk_vals, picked, preferred_element_type=jnp.float32)
        placing = (blk_cols[:, None] == tile_range[None, :]).astype(jnp.float32) * live_mask[
            :, None
        ]
        return jnp.einsum("tr,tjf->rjf", placing, product, precision=highest)

    agg_sum = forward_block(my_block, own_panel)

    def forward_turn(k, carry):
        panel_now, running = carry
        panel_now = shifted(panel_now, "blk", 1)
        source = (my_block - k) % n_blocks
        return (panel_now, running + forward_block(source, panel_now))

    _, agg_sum = lax.fori_loop(1, n_blocks, forward_turn, (own_panel, agg_sum))
    dest_all = hub_dest[:, 0, :, 0]
    hub_rows_all = hub_row[:, 0, :]
    hub_range = jnp.arange(hub_count, dtype=jnp.int32)
    earlier = hub_range[None, :] < hub_range[:, None]
    same_dest = dest_all[:, :, None] == dest_all[:, None, :]
    rank_all = jnp.sum((same_dest & earlier[None, :, :]).astype(jnp.int32), axis=-1)
    my_dest = lax.dynamic_index_in_dim(dest_all, my_group, 0, keepdims=False)
    my_rank = lax.dynamic_index_in_dim(rank_all, my_group, 0, keepdims=False)
    slot_of = my_dest * capacity + my_rank
    send_place = (
        slot_of[:, None] == jnp.arange(n_groups * capacity, dtype=jnp.int32)[None, :]
    ).astype(jnp.float32)
    hub_tiles = hub_vals[0, 0]
    hub_cols = hub_col[0, 0]
    hub_src = jnp.take(own_panel, hub_cols, axis=0)
    hub_part = jnp.einsum("hij,hjf->hif", hub_tiles, hub_src, preferred_element_type=jnp.float32)
    send_buf = jnp.einsum("hs,hif->sif", send_place, hub_part, precision=highest)
    send_buf = send_buf.reshape(n_groups, capacity, tile_size, width)
    received = lax.all_to_all(send_buf, "grp", split_axis=0, concat_axis=0, tiled=True)
    chosen = (dest_all == my_group).astype(jnp.float32)
    slot_hot = (rank_all[..., None] == jnp.arange(capacity, dtype=jnp.int32)).astype(
        jnp.float32
    ) * chosen[..., None]
    row_hot = (hub_rows_all[..., None] == tile_range).astype(jnp.float32)
    routing = jnp.einsum("shc,shr->scr", slot_hot, row_hot, precision=highest)
    agg_sum = agg_sum + jnp.einsum("scr,scif->rif", routing, received, precision=highest)
    agg_rows = agg_sum.reshape(rows_dev, width)
    layer_out = jax.nn.silu(agg_rows).astype(jnp.bfloat16)
    sigmoid_z = jax.nn.sigmoid(agg_rows)
    slope = sigmoid_z * (1.0 + agg_rows * (1.0 - sigmoid_z))
    keep = (labels >= 0).astype(jnp.float32)[:, None]
    grad_agg = (cotangent.astype(jnp.float32) * keep * slope).astype(jnp.bfloat16)
    grad_tiles = grad_agg.reshape(row_tiles, tile_size, width)
    grad_sum = backward_block((my_block + n_blocks - 1) % n_blocks, grad_tiles)

    def backward_turn(k, running):
        running = shifted(running, "blk", 1)
        return running + backward_block((my_block + n_blocks - 1 - k) % n_blocks, grad_tiles)

    grad_sum = lax.fori_loop(1, n_blocks, backward_turn, grad_sum)
    back_send = jnp.einsum(
        "scr,rif->scif",
        routing.astype(jnp.bfloat16),
        grad_tiles,
        preferred_element_type=jnp.float32,
    ).astype(jnp.bfloat16)
    back_recv = lax.all_to_all(back_send, "grp", split_axis=0, concat_axis=0, tiled=True)
    back_flat = back_recv.reshape(n_groups * capacity, tile_size, width)
    own_pick = jnp.einsum(
        "hs,sif->hif",
        send_place.astype(jnp.bfloat16),
        back_flat,
        preferred_element_type=jnp.float32,
    ).astype(jnp.bfloat16)
    hub_back = jnp.einsum("hij,hif->hjf", hub_tiles, own_pick, preferred_element_type=jnp.float32)
    col_hot = (hub_cols[:, None] == tile_range[None, :]).astype(jnp.float32)
    grad_sum = grad_sum + jnp.einsum("hr,hjf->rjf", col_hot, hub_back, precision=highest)
    grad_rows = grad_sum.reshape(rows_dev, width).astype(jnp.bfloat16)
    weight_term = lax.dot_general(
        feats, grad_rows, (((0,), (0,)), ((), ())), preferred_element_type=jnp.float32
    )
    grad_scale = 1.0 / math.sqrt(rows_dev * n_blocks * n_groups)
    grad_weight = lax.psum(weight_term, ("grp", "blk")) * grad_scale
    grad_feats = lax.dot_general(
        grad_rows, weight, (((1,), (1,)), ((), ())), preferred_element_type=jnp.float32
    ).astype(jnp.bfloat16)
    return (layer_out, grad_feats, grad_weight)


def solution(mesh):
    in_specs = (
        P(("grp", "blk"), None),
        P(),
        P(("grp", "blk"), None),
        P(("grp", "blk")),
        P("grp", "blk", None, None, None, None),
        P("grp", "blk", None, None),
        P("grp", "blk", None, None),
        P("grp", "blk", None),
        P("grp", "blk", None, None, None),
        P("grp", "blk", None),
        P(None, "blk", None, None),
        P(None, "blk", None),
    )
    out_specs = (P(("grp", "blk"), None), P(("grp", "blk"), None), P())
    return jax.shard_map(local, mesh=mesh, in_specs=in_specs, out_specs=out_specs, check_vma=False)
```

profile of v0, /device:TPU:1, one launch (start us, length us, event | category | flops | bytes accessed | tf_op | source)
XLA Modules:
  0.0 958.8 jit_solution(11379729683561159299)
XLA Ops:
  51.4 313.8 %while.34 = (s32[]{:T(128)}, bf16[8,128,256]{2,1,0:T(8,128)(2,1)S(1)}, f32[8,128,256]{2,0,1:T(8,128)}, s32[]{:T(128)}, s32[16,32]{1,0:T(8,128)}, /*index=5*/s32[...) while((s32[]{:T(128)}, ...), condition=%wide.region_1.3_spmd.clone, body=%wide.region_0.2_spmd.clone.sunk | while | flops 370411264 | bytes 29365836 | solution.py:83
  73.1 11.3 %collective-permute-done = bf16[8,128,256]{2,1,0:T(8,128)(2,1)S(1)} collective-permute-done((bf16[8,128,256]{2,1,0:T(8,128)(2,1)S(1)}, bf16[8,128,256]{2,1,0:T(8,128)(2,1)S(1)}, u32[]{:S(2)}, u32[]{:S(2)}) %collective-permute-start) | collective-permute-done | bytes 524320 | tf_op jit(solution)/shard_map/while/body/eval_jaxpr/ppermute | solution.py:11
  95.4 14.3 %collective-permute-done = bf16[8,128,256]{2,1,0:T(8,128)(2,1)S(1)} collective-permute-done((bf16[8,128,256]{2,1,0:T(8,128)(2,1)S(1)}, bf16[8,128,256]{2,1,0:T(8,128)(2,1)S(1)}, u32[]{:S(2)}, u32[]{:S(2)}) %collective-permute-start) | collective-permute-done | bytes 524320 | tf_op jit(solution)/shard_map/while/body/eval_jaxpr/ppermute | solution.py:11
  120.7 9.6 collective-permute-done
  141.3 9.6 collective-permute-done
  161.9 9.6 collective-permute-done
  182.5 9.6 collective-permute-done
  203.1 9.6 collective-permute-done
  223.7 9.6 collective-permute-done
  244.3 9.6 collective-permute-done
  264.8 9.6 collective-permute-done
  285.4 9.6 collective-permute-done
  326.6 9.6 collective-permute-done
  347.2 9.6 collective-permute-done
  365.1 15.8 %fusion.65 = f32[8,128,256]{2,0,1:T(8,128)S(1)} fusion(f32[8,128,256]{2,0,1:T(8,128)} %get-tuple-element.494, f32[8,4,128,256]{3,1,2,0:T(4,128)} %all-to-all-done, f32[8,4,8]{2,1,0:T(4,128)S(1)} %fusion.89), kind=kOutput, calls=%fused_computation.79 | convolution fusion | flops 100925440 | bytes 6292480 | tf_op jit(solution)/shard_map/scr,scif->rif/dot_general | solution.py:109
  389.4 21.2 %copy.51 = bf16[1,1,16,32,128,128]{4,5,3,2,1,0:T(8,128)(2,1)} copy(bf16[1,1,16,32,128,128]{5,4,3,2,1,0:T(8,128)(2,1)} %bitcast.174) | data formatting | bytes 33554432 | tf_op args[4]
  425.9 365.8 %while.35 = (s32[]{:T(128)}, f32[8,128,256]{2,0,1:T(8,128)}, s32[]{:T(128)}, s32[16,32]{1,0:T(8,128)}, s32[16]{0:T(128)S(1)}, /*index=5*/bf16[16,32,128,128]{2,3...) while((s32[]{:T(128)}, f32[8,128,256]{2,0,1:T(8,128)}, ...), condition=%wide.region_4.6_spmd.clone, body=%wide.region_3.5_spmd.clone.sunk | while | flops 370411264 | bytes 22025748 | solution.py:123
  452.3 11.6 %collective-permute-done.1 = f32[8,128,256]{2,0,1:T(8,128)} collective-permute-done((f32[8,128,256]{2,0,1:T(8,128)}, f32[8,128,256]{2,0,1:T(8,128)}, u32[]{:S(2)}, u32[]{:S(2)}) %collective-permute-start.1) | collective-permute-done | bytes 1048608 | tf_op jit(solution)/shard_map/while/body/eval_jaxpr/ppermute | solution.py:11
  475.8 12.8 %collective-permute-done.1 = f32[8,128,256]{2,0,1:T(8,128)} collective-permute-done((f32[8,128,256]{2,0,1:T(8,128)}, f32[8,128,256]{2,0,1:T(8,128)}, u32[]{:S(2)}, u32[]{:S(2)}) %collective-permute-start.1) | collective-permute-done | bytes 1048608 | tf_op jit(solution)/shard_map/while/body/eval_jaxpr/ppermute | solution.py:11
  500.5 12.8 %collective-permute-done.1 = f32[8,128,256]{2,0,1:T(8,128)} collective-permute-done((f32[8,128,256]{2,0,1:T(8,128)}, f32[8,128,256]{2,0,1:T(8,128)}, u32[]{:S(2)}, u32[]{:S(2)}) %collective-permute-start.1) | collective-permute-done | bytes 1048608 | tf_op jit(solution)/shard_map/while/body/eval_jaxpr/ppermute | solution.py:11
  525.2 12.8 %collective-permute-done.1 = f32[8,128,256]{2,0,1:T(8,128)} collective-permute-done((f32[8,128,256]{2,0,1:T(8,128)}, f32[8,128,256]{2,0,1:T(8,128)}, u32[]{:S(2)}, u32[]{:S(2)}) %collective-permute-start.1) | collective-permute-done | bytes 1048608 | tf_op jit(solution)/shard_map/while/body/eval_jaxpr/ppermute | solution.py:11
  550.0 12.8 %collective-permute-done.1 = f32[8,128,256]{2,0,1:T(8,128)} collective-permute-done((f32[8,128,256]{2,0,1:T(8,128)}, f32[8,128,256]{2,0,1:T(8,128)}, u32[]{:S(2)}, u32[]{:S(2)}) %collective-permute-start.1) | collective-permute-done | bytes 1048608 | tf_op jit(solution)/shard_map/while/body/eval_jaxpr/ppermute | solution.py:11
  574.7 12.8 %collective-permute-done.1 = f32[8,128,256]{2,0,1:T(8,128)} collective-permute-done((f32[8,128,256]{2,0,1:T(8,128)}, f32[8,128,256]{2,0,1:T(8,128)}, u32[]{:S(2)}, u32[]{:S(2)}) %collective-permute-start.1) | collective-permute-done | bytes 1048608 | tf_op jit(solution)/shard_map/while/body/eval_jaxpr/ppermute | solution.py:11
  599.4 12.8 %collective-permute-done.1 = f32[8,128,256]{2,0,1:T(8,128)} collective-permute-done((f32[8,128,256]{2,0,1:T(8,128)}, f32[8,128,256]{2,0,1:T(8,128)}, u32[]{:S(2)}, u32[]{:S(2)}) %collective-permute-start.1) | collective-permute-done | bytes 1048608 | tf_op jit(solution)/shard_map/while/body/eval_jaxpr/ppermute | solution.py:11
  624.1 12.8 %collective-permute-done.1 = f32[8,128,256]{2,0,1:T(8,128)} collective-permute-done((f32[8,128,256]{2,0,1:T(8,128)}, f32[8,128,256]{2,0,1:T(8,128)}, u32[]{:S(2)}, u32[]{:S(2)}) %collective-permute-start.1) | collective-permute-done | bytes 1048608 | tf_op jit(solution)/shard_map/while/body/eval_jaxpr/ppermute | solution.py:11
  648.8 12.8 %collective-permute-done.1 = f32[8,128,256]{2,0,1:T(8,128)} collective-permute-done((f32[8,128,256]{2,0,1:T(8,128)}, f32[8,128,256]{2,0,1:T(8,128)}, u32[]{:S(2)}, u32[]{:S(2)}) %collective-permute-start.1) | collective-permute-done | bytes 1048608 | tf_op jit(solution)/shard_map/while/body/eval_jaxpr/ppermute | solution.py:11
  673.5 12.8 %collective-permute-done.1 = f32[8,128,256]{2,0,1:T(8,128)} collective-permute-done((f32[8,128,256]{2,0,1:T(8,128)}, f32[8,128,256]{2,0,1:T(8,128)}, u32[]{:S(2)}, u32[]{:S(2)}) %collective-permute-start.1) | collective-permute-done | bytes 1048608 | tf_op jit(solution)/shard_map/while/body/eval_jaxpr/ppermute | solution.py:11
  698.2 12.8 %collective-permute-done.1 = f32[8,128,256]{2,0,1:T(8,128)} collective-permute-done((f32[8,128,256]{2,0,1:T(8,128)}, f32[8,128,256]{2,0,1:T(8,128)}, u32[]{:S(2)}, u32[]{:S(2)}) %collective-permute-start.1) | collective-permute-done | bytes 1048608 | tf_op jit(solution)/shard_map/while/body/eval_jaxpr/ppermute | solution.py:11
  722.9 12.8 %collective-permute-done.1 = f32[8,128,256]{2,0,1:T(8,128)} collective-permute-done((f32[8,128,256]{2,0,1:T(8,128)}, f32[8,128,256]{2,0,1:T(8,128)}, u32[]{:S(2)}, u32[]{:S(2)}) %collective-permute-start.1) | collective-permute-done | bytes 1048608 | tf_op jit(solution)/shard_map/while/body/eval_jaxpr/ppermute | solution.py:11
  747.6 12.8 %collective-permute-done.1 = f32[8,128,256]{2,0,1:T(8,128)} collective-permute-done((f32[8,128,256]{2,0,1:T(8,128)}, f32[8,128,256]{2,0,1:T(8,128)}, u32[]{:S(2)}, u32[]{:S(2)}) %collective-permute-start.1) | collective-permute-done | bytes 1048608 | tf_op jit(solution)/shard_map/while/body/eval_jaxpr/ppermute | solution.py:11
  772.3 12.8 %collective-permute-done.1 = f32[8,128,256]{2,0,1:T(8,128)} collective-permute-done((f32[8,128,256]{2,0,1:T(8,128)}, f32[8,128,256]{2,0,1:T(8,128)}, u32[]{:S(2)}, u32[]{:S(2)}) %collective-permute-start.1) | collective-permute-done | bytes 1048608 | tf_op jit(solution)/shard_map/while/body/eval_jaxpr/ppermute | solution.py:11
  796.8 153.1 %all-reduce.2.cloned.1.call-done = f32[256,256]{0,1:T(8,128)} async-done(((f32[256,256]{0,1:T(8,128)}), f32[256,256]{0,1:T(8,128)}) %all-reduce.2.cloned.1.call-update) | async-done | bytes 262160 | tf_op jit(solution)/shard_map/psum | solution.py:146
  (416 shorter events, 443.7 us)
Async XLA Ops:
  31.5 333.6 %all-to-all-start = ((f32[8,4,128,256]{3,1,2,0:T(4,128)}), f32[8,4,128,256]{3,1,2,0:T(4,128)}, u32[]{:S(2)}, u32[]{:S(2)}) async-start(f32[8,4,128,256]{3,1,2,0:T(4,128)} %copy.55), calls=%async_computation | async-start | bytes 8388608 | tf_op jit(solution)/shard_map/all_to_all | solution.py:102
  68.0 16.4 %collective-permute-start = (bf16[8,128,256]{2,1,0:T(8,128)(2,1)S(1)}, bf16[8,128,256]{2,1,0:T(8,128)(2,1)S(1)}, u32[]{:S(2)}, u32[]{:S(2)}) collective-permute-start(bf16[8,128,256]{2,1,0:T(8,128)(2,1)S(1)} %get-tuple-element.727), channel_id=1, source_target_pairs={{0,1},{1,2},{2,3},{3,4},{4,5},{5,6},{6,7},{7,8},{8,9},{9,10},{10,1... | collective-permute-start | bytes 1572872 | tf_op jit(solution)/shard_map/while/body/eval_jaxpr/ppermute | solution.py:11
  92.8 16.9 %collective-permute-start = (bf16[8,128,256]{2,1,0:T(8,128)(2,1)S(1)}, bf16[8,128,256]{2,1,0:T(8,128)(2,1)S(1)}, u32[]{:S(2)}, u32[]{:S(2)}) collective-permute-start(bf16[8,128,256]{2,1,0:T(8,128)(2,1)S(1)} %get-tuple-element.727), channel_id=1, source_target_pairs={{0,1},{1,2},{2,3},{3,4},{4,5},{5,6},{6,7},{7,8},{8,9},{9,10},{10,1... | collective-permute-start | bytes 1572872 | tf_op jit(solution)/shard_map/while/body/eval_jaxpr/ppermute | solution.py:11
  118.1 12.2 %collective-permute-start = (bf16[8,128,256]{2,1,0:T(8,128)(2,1)S(1)}, bf16[8,128,256]{2,1,0:T(8,128)(2,1)S(1)}, u32[]{:S(2)}, u32[]{:S(2)}) collective-permute-start(bf16[8,128,256]{2,1,0:T(8,128)(2,1)S(1)} %get-tuple-element.727), channel_id=1, source_target_pairs={{0,1},{1,2},{2,3},{3,4},{4,5},{5,6},{6,7},{7,8},{8,9},{9,10},{10,1... | collective-permute-start | bytes 1572872 | tf_op jit(solution)/shard_map/while/body/eval_jaxpr/ppermute | solution.py:11
  138.7 12.2 %collective-permute-start = (bf16[8,128,256]{2,1,0:T(8,128)(2,1)S(1)}, bf16[8,128,256]{2,1,0:T(8,128)(2,1)S(1)}, u32[]{:S(2)}, u32[]{:S(2)}) collective-permute-start(bf16[8,128,256]{2,1,0:T(8,128)(2,1)S(1)} %get-tuple-element.727), channel_id=1, source_target_pairs={{0,1},{1,2},{2,3},{3,4},{4,5},{5,6},{6,7},{7,8},{8,9},{9,10},{10,1... | collective-permute-start | bytes 1572872 | tf_op jit(solution)/shard_map/while/body/eval_jaxpr/ppermute | solution.py:11
  159.3 12.2 %collective-permute-start = (bf16[8,128,256]{2,1,0:T(8,128)(2,1)S(1)}, bf16[8,128,256]{2,1,0:T(8,128)(2,1)S(1)}, u32[]{:S(2)}, u32[]{:S(2)}) collective-permute-start(bf16[8,128,256]{2,1,0:T(8,128)(2,1)S(1)} %get-tuple-element.727), channel_id=1, source_target_pairs={{0,1},{1,2},{2,3},{3,4},{4,5},{5,6},{6,7},{7,8},{8,9},{9,10},{10,1... | collective-permute-start | bytes 1572872 | tf_op jit(solution)/shard_map/while/body/eval_jaxpr/ppermute | solution.py:11
  179.9 12.2 %collective-permute-start = (bf16[8,128,256]{2,1,0:T(8,128)(2,1)S(1)}, bf16[8,128,256]{2,1,0:T(8,128)(2,1)S(1)}, u32[]{:S(2)}, u32[]{:S(2)}) collective-permute-start(bf16[8,128,256]{2,1,0:T(8,128)(2,1)S(1)} %get-tuple-element.727), channel_id=1, source_target_pairs={{0,1},{1,2},{2,3},{3,4},{4,5},{5,6},{6,7},{7,8},{8,9},{9,10},{10,1... | collective-permute-start | bytes 1572872 | tf_op jit(solution)/shard_map/while/body/eval_jaxpr/ppermute | solution.py:11
  200.4 12.2 %collective-permute-start = (bf16[8,128,256]{2,1,0:T(8,128)(2,1)S(1)}, bf16[8,128,256]{2,1,0:T(8,128)(2,1)S(1)}, u32[]{:S(2)}, u32[]{:S(2)}) collective-permute-start(bf16[8,128,256]{2,1,0:T(8,128)(2,1)S(1)} %get-tuple-element.727), channel_id=1, source_target_pairs={{0,1},{1,2},{2,3},{3,4},{4,5},{5,6},{6,7},{7,8},{8,9},{9,10},{10,1... | collective-permute-start | bytes 1572872 | tf_op jit(solution)/shard_map/while/body/eval_jaxpr/ppermute | solution.py:11
  221.0 12.2 %collective-permute-start = (bf16[8,128,256]{2,1,0:T(8,128)(2,1)S(1)}, bf16[8,128,256]{2,1,0:T(8,128)(2,1)S(1)}, u32[]{:S(2)}, u32[]{:S(2)}) collective-permute-start(bf16[8,128,256]{2,1,0:T(8,128)(2,1)S(1)} %get-tuple-element.727), channel_id=1, source_target_pairs={{0,1},{1,2},{2,3},{3,4},{4,5},{5,6},{6,7},{7,8},{8,9},{9,10},{10,1... | collective-permute-start | bytes 1572872 | tf_op jit(solution)/shard_map/while/body/eval_jaxpr/ppermute | solution.py:11
  241.6 12.2 %collective-permute-start = (bf16[8,128,256]{2,1,0:T(8,128)(2,1)S(1)}, bf16[8,128,256]{2,1,0:T(8,128)(2,1)S(1)}, u32[]{:S(2)}, u32[]{:S(2)}) collective-permute-start(bf16[8,128,256]{2,1,0:T(8,128)(2,1)S(1)} %get-tuple-element.727), channel_id=1, source_target_pairs={{0,1},{1,2},{2,3},{3,4},{4,5},{5,6},{6,7},{7,8},{8,9},{9,10},{10,1... | collective-permute-start | bytes 1572872 | tf_op jit(solution)/shard_map/while/body/eval_jaxpr/ppermute | solution.py:11
  262.2 12.2 %collective-permute-start = (bf16[8,128,256]{2,1,0:T(8,128)(2,1)S(1)}, bf16[8,128,256]{2,1,0:T(8,128)(2,1)S(1)}, u32[]{:S(2)}, u32[]{:S(2)}) collective-permute-start(bf16[8,128,256]{2,1,0:T(8,128)(2,1)S(1)} %get-tuple-element.727), channel_id=1, source_target_pairs={{0,1},{1,2},{2,3},{3,4},{4,5},{5,6},{6,7},{7,8},{8,9},{9,10},{10,1... | collective-permute-start | bytes 1572872 | tf_op jit(solution)/shard_map/while/body/eval_jaxpr/ppermute | solution.py:11
  282.8 12.2 %collective-permute-start = (bf16[8,128,256]{2,1,0:T(8,128)(2,1)S(1)}, bf16[8,128,256]{2,1,0:T(8,128)(2,1)S(1)}, u32[]{:S(2)}, u32[]{:S(2)}) collective-permute-start(bf16[8,128,256]{2,1,0:T(8,128)(2,1)S(1)} %get-tuple-element.727), channel_id=1, source_target_pairs={{0,1},{1,2},{2,3},{3,4},{4,5},{5,6},{6,7},{7,8},{8,9},{9,10},{10,1... | collective-permute-start | bytes 1572872 | tf_op jit(solution)/shard_map/while/body/eval_jaxpr/ppermute | solution.py:11
  303.4 12.2 %collective-permute-start = (bf16[8,128,256]{2,1,0:T(8,128)(2,1)S(1)}, bf16[8,128,256]{2,1,0:T(8,128)(2,1)S(1)}, u32[]{:S(2)}, u32[]{:S(2)}) collective-permute-start(bf16[8,128,256]{2,1,0:T(8,128)(2,1)S(1)} %get-tuple-element.727), channel_id=1, source_target_pairs={{0,1},{1,2},{2,3},{3,4},{4,5},{5,6},{6,7},{7,8},{8,9},{9,10},{10,1... | collective-permute-start | bytes 1572872 | tf_op jit(solution)/shard_map/while/body/eval_jaxpr/ppermute | solution.py:11
  324.0 12.2 %collective-permute-start = (bf16[8,128,256]{2,1,0:T(8,128)(2,1)S(1)}, bf16[8,128,256]{2,1,0:T(8,128)(2,1)S(1)}, u32[]{:S(2)}, u32[]{:S(2)}) collective-permute-start(bf16[8,128,256]{2,1,0:T(8,128)(2,1)S(1)} %get-tuple-element.727), channel_id=1, source_target_pairs={{0,1},{1,2},{2,3},{3,4},{4,5},{5,6},{6,7},{7,8},{8,9},{9,10},{10,1... | collective-permute-start | bytes 1572872 | tf_op jit(solution)/shard_map/while/body/eval_jaxpr/ppermute | solution.py:11
  344.6 12.2 %collective-permute-start = (bf16[8,128,256]{2,1,0:T(8,128)(2,1)S(1)}, bf16[8,128,256]{2,1,0:T(8,128)(2,1)S(1)}, u32[]{:S(2)}, u32[]{:S(2)}) collective-permute-start(bf16[8,128,256]{2,1,0:T(8,128)(2,1)S(1)} %get-tuple-element.727), channel_id=1, source_target_pairs={{0,1},{1,2},{2,3},{3,4},{4,5},{5,6},{6,7},{7,8},{8,9},{9,10},{10,1... | collective-permute-start | bytes 1572872 | tf_op jit(solution)/shard_map/while/body/eval_jaxpr/ppermute | solution.py:11
  385.7 36.3 %all-to-all-start.1 = ((bf16[8,4,128,256]{3,2,1,0:T(8,128)(2,1)}), bf16[8,4,128,256]{3,2,1,0:T(8,128)(2,1)S(1)}, u32[]{:S(2)}, u32[]{:S(2)}) async-start(bf16[8,4,128,256]{3,2,1,0:T(8,128)(2,1)} %copy.62), calls=%async_computation.1 | async-start | bytes 4194304 | tf_op jit(solution)/shard_map/all_to_all | solution.py:130
  389.3 560.6 %all-reduce.2.cloned.1.call-start = ((), (), s32[]{:S(2)}) async-start(), calls=%async_computation.2 | async-start | bytes 524288 | tf_op jit(solution)/shard_map/psum | solution.py:146
  425.9 13.3 %collective-permute-start.1 = (f32[8,128,256]{2,0,1:T(8,128)}, f32[8,128,256]{2,0,1:T(8,128)}, u32[]{:S(2)}, u32[]{:S(2)}) collective-permute-start(f32[8,128,256]{2,0,1:T(8,128)} %get-tuple-element.763), channel_id=1, source_target_pairs={{0,1},{1,2},{2,3},{3,4},{4,5},{5,6},{6,7},{7,8},{8,9},{9,10},{10,1... | collective-permute-start | bytes 3145736 | tf_op jit(solution)/shard_map/while/body/eval_jaxpr/ppermute | solution.py:11
  445.8 18.2 %collective-permute-start.1 = (f32[8,128,256]{2,0,1:T(8,128)}, f32[8,128,256]{2,0,1:T(8,128)}, u32[]{:S(2)}, u32[]{:S(2)}) collective-permute-start(f32[8,128,256]{2,0,1:T(8,128)} %get-tuple-element.763), channel_id=1, source_target_pairs={{0,1},{1,2},{2,3},{3,4},{4,5},{5,6},{6,7},{7,8},{8,9},{9,10},{10,1... | collective-permute-start | bytes 3145736 | tf_op jit(solution)/shard_map/while/body/eval_jaxpr/ppermute | solution.py:11
  470.5 18.2 %collective-permute-start.1 = (f32[8,128,256]{2,0,1:T(8,128)}, f32[8,128,256]{2,0,1:T(8,128)}, u32[]{:S(2)}, u32[]{:S(2)}) collective-permute-start(f32[8,128,256]{2,0,1:T(8,128)} %get-tuple-element.763), channel_id=1, source_target_pairs={{0,1},{1,2},{2,3},{3,4},{4,5},{5,6},{6,7},{7,8},{8,9},{9,10},{10,1... | collective-permute-start | bytes 3145736 | tf_op jit(solution)/shard_map/while/body/eval_jaxpr/ppermute | solution.py:11
  495.2 18.2 %collective-permute-start.1 = (f32[8,128,256]{2,0,1:T(8,128)}, f32[8,128,256]{2,0,1:T(8,128)}, u32[]{:S(2)}, u32[]{:S(2)}) collective-permute-start(f32[8,128,256]{2,0,1:T(8,128)} %get-tuple-element.763), channel_id=1, source_target_pairs={{0,1},{1,2},{2,3},{3,4},{4,5},{5,6},{6,7},{7,8},{8,9},{9,10},{10,1... | collective-permute-start | bytes 3145736 | tf_op jit(solution)/shard_map/while/body/eval_jaxpr/ppermute | solution.py:11
  519.9 18.2 %collective-permute-start.1 = (f32[8,128,256]{2,0,1:T(8,128)}, f32[8,128,256]{2,0,1:T(8,128)}, u32[]{:S(2)}, u32[]{:S(2)}) collective-permute-start(f32[8,128,256]{2,0,1:T(8,128)} %get-tuple-element.763), channel_id=1, source_target_pairs={{0,1},{1,2},{2,3},{3,4},{4,5},{5,6},{6,7},{7,8},{8,9},{9,10},{10,1... | collective-permute-start | bytes 3145736 | tf_op jit(solution)/shard_map/while/body/eval_jaxpr/ppermute | solution.py:11
  544.6 18.2 %collective-permute-start.1 = (f32[8,128,256]{2,0,1:T(8,128)}, f32[8,128,256]{2,0,1:T(8,128)}, u32[]{:S(2)}, u32[]{:S(2)}) collective-permute-start(f32[8,128,256]{2,0,1:T(8,128)} %get-tuple-element.763), channel_id=1, source_target_pairs={{0,1},{1,2},{2,3},{3,4},{4,5},{5,6},{6,7},{7,8},{8,9},{9,10},{10,1... | collective-permute-start | bytes 3145736 | tf_op jit(solution)/shard_map/while/body/eval_jaxpr/ppermute | solution.py:11
  569.3 18.2 %collective-permute-start.1 = (f32[8,128,256]{2,0,1:T(8,128)}, f32[8,128,256]{2,0,1:T(8,128)}, u32[]{:S(2)}, u32[]{:S(2)}) collective-permute-start(f32[8,128,256]{2,0,1:T(8,128)} %get-tuple-element.763), channel_id=1, source_target_pairs={{0,1},{1,2},{2,3},{3,4},{4,5},{5,6},{6,7},{7,8},{8,9},{9,10},{10,1... | collective-permute-start | bytes 3145736 | tf_op jit(solution)/shard_map/while/body/eval_jaxpr/ppermute | solution.py:11
  594.0 18.2 %collective-permute-start.1 = (f32[8,128,256]{2,0,1:T(8,128)}, f32[8,128,256]{2,0,1:T(8,128)}, u32[]{:S(2)}, u32[]{:S(2)}) collective-permute-start(f32[8,128,256]{2,0,1:T(8,128)} %get-tuple-element.763), channel_id=1, source_target_pairs={{0,1},{1,2},{2,3},{3,4},{4,5},{5,6},{6,7},{7,8},{8,9},{9,10},{10,1... | collective-permute-start | bytes 3145736 | tf_op jit(solution)/shard_map/while/body/eval_jaxpr/ppermute | solution.py:11
  618.7 18.2 %collective-permute-start.1 = (f32[8,128,256]{2,0,1:T(8,128)}, f32[8,128,256]{2,0,1:T(8,128)}, u32[]{:S(2)}, u32[]{:S(2)}) collective-permute-start(f32[8,128,256]{2,0,1:T(8,128)} %get-tuple-element.763), channel_id=1, source_target_pairs={{0,1},{1,2},{2,3},{3,4},{4,5},{5,6},{6,7},{7,8},{8,9},{9,10},{10,1... | collective-permute-start | bytes 3145736 | tf_op jit(solution)/shard_map/while/body/eval_jaxpr/ppermute | solution.py:11
  643.5 18.2 %collective-permute-start.1 = (f32[8,128,256]{2,0,1:T(8,128)}, f32[8,128,256]{2,0,1:T(8,128)}, u32[]{:S(2)}, u32[]{:S(2)}) collective-permute-start(f32[8,128,256]{2,0,1:T(8,128)} %get-tuple-element.763), channel_id=1, source_target_pairs={{0,1},{1,2},{2,3},{3,4},{4,5},{5,6},{6,7},{7,8},{8,9},{9,10},{10,1... | collective-permute-start | bytes 3145736 | tf_op jit(solution)/shard_map/while/body/eval_jaxpr/ppermute | solution.py:11
  668.2 18.2 %collective-permute-start.1 = (f32[8,128,256]{2,0,1:T(8,128)}, f32[8,128,256]{2,0,1:T(8,128)}, u32[]{:S(2)}, u32[]{:S(2)}) collective-permute-start(f32[8,128,256]{2,0,1:T(8,128)} %get-tuple-element.763), channel_id=1, source_target_pairs={{0,1},{1,2},{2,3},{3,4},{4,5},{5,6},{6,7},{7,8},{8,9},{9,10},{10,1... | collective-permute-start | bytes 3145736 | tf_op jit(solution)/shard_map/while/body/eval_jaxpr/ppermute | solution.py:11
  692.9 18.2 %collective-permute-start.1 = (f32[8,128,256]{2,0,1:T(8,128)}, f32[8,128,256]{2,0,1:T(8,128)}, u32[]{:S(2)}, u32[]{:S(2)}) collective-permute-start(f32[8,128,256]{2,0,1:T(8,128)} %get-tuple-element.763), channel_id=1, source_target_pairs={{0,1},{1,2},{2,3},{3,4},{4,5},{5,6},{6,7},{7,8},{8,9},{9,10},{10,1... | collective-permute-start | bytes 3145736 | tf_op jit(solution)/shard_map/while/body/eval_jaxpr/ppermute | solution.py:11
  717.6 18.2 %collective-permute-start.1 = (f32[8,128,256]{2,0,1:T(8,128)}, f32[8,128,256]{2,0,1:T(8,128)}, u32[]{:S(2)}, u32[]{:S(2)}) collective-permute-start(f32[8,128,256]{2,0,1:T(8,128)} %get-tuple-element.763), channel_id=1, source_target_pairs={{0,1},{1,2},{2,3},{3,4},{4,5},{5,6},{6,7},{7,8},{8,9},{9,10},{10,1... | collective-permute-start | bytes 3145736 | tf_op jit(solution)/shard_map/while/body/eval_jaxpr/ppermute | solution.py:11
  742.3 18.2 %collective-permute-start.1 = (f32[8,128,256]{2,0,1:T(8,128)}, f32[8,128,256]{2,0,1:T(8,128)}, u32[]{:S(2)}, u32[]{:S(2)}) collective-permute-start(f32[8,128,256]{2,0,1:T(8,128)} %get-tuple-element.763), channel_id=1, source_target_pairs={{0,1},{1,2},{2,3},{3,4},{4,5},{5,6},{6,7},{7,8},{8,9},{9,10},{10,1... | collective-permute-start | bytes 3145736 | tf_op jit(solution)/shard_map/while/body/eval_jaxpr/ppermute | solution.py:11
  767.0 18.2 %collective-permute-start.1 = (f32[8,128,256]{2,0,1:T(8,128)}, f32[8,128,256]{2,0,1:T(8,128)}, u32[]{:S(2)}, u32[]{:S(2)}) collective-permute-start(f32[8,128,256]{2,0,1:T(8,128)} %get-tuple-element.763), channel_id=1, source_target_pairs={{0,1},{1,2},{2,3},{3,4},{4,5},{5,6},{6,7},{7,8},{8,9},{9,10},{10,1... | collective-permute-start | bytes 3145736 | tf_op jit(solution)/shard_map/while/body/eval_jaxpr/ppermute | solution.py:11
  (40 other events, 442.4 us)
Sparse Core Ops, SparseCore 0:
  795.8 154.0 all-reduce.1
where the time goes:
time: 967 us; the launch traced here: 959 us
  waiting for transfers between devices  483 us (50%)
  matrix products  275 us (28%)
  local copies, waits for them, and re-layouts  122 us (13%)
  other arithmetic  46.4 us (5%)
  starting transfers between devices  16.2 us (2%)
  between operations  14.5 us (1%)
    ppermute x30, waiting for transfers between devices, shifted(): lax.ppermute(value, axis, [(i, (i + by) % size) for i in range(size)])  330 us
    psum x1, waiting for transfers between devices, local(): grad_weight = lax.psum(weight_term, ('grp', 'blk')) * grad_scale  153 us
    dot_general x16, matrix products, backward_block(): return jnp.einsum('tr,tjf->rjf', placing, product, precision=highest)  104 us
    dot_general x16, matrix products, forward_block(): return jnp.einsum('tr,tif->rif', placing, product, precision=highest)  72.6 us
    dot_general x16, matrix products, forward_block(): jnp.einsum('tij,tjf->tif', blk_vals, picked, preferred_element_type=jnp.f...  34.1 us
    dot_general x16, matrix products, backward_block(): jnp.einsum('tij,tif->tjf', blk_vals, picked, preferred_element_type=jnp.f...  32.7 us
    unnamed x20, local copies, waits for them, and re-layouts  22.8 us
    convert_element_type x32, other arithmetic, block_parts(): live_mask = (slot_range < blk_count).astype(jnp.float32)  20.7 us
  transfers between devices with their start and end apart: 33, of which 31 were waited for; matrix products, arithmetic and copies ran while one was open for 29% of the time, Pallas kernels for 0%

commit v1 on v0

--- a/solution.py
+++ b/solution.py
@@ -1,14 +1,91 @@
+import functools
 import math
 
 import jax
 import jax.numpy as jnp
 from jax import lax
+from jax.experimental import pallas as pl
+from jax.experimental.pallas import tpu as pltpu
 from jax.sharding import PartitionSpec as P
 
 
-def shifted(value, axis, by):
-    size = lax.axis_size(axis)
-    return lax.ppermute(value, axis, [(i, (i + by) % size) for i in range(size)])
+def forward_kernel(rows_ref, cols_ref, count_ref, vals_ref, panel_ref, out_ref):
+    c = pl.program_id(0)
+    slots = vals_ref.shape[1]
+
+    @pl.when(c == 0)
+    def _():
+        out_ref[...] = jnp.zeros_like(out_ref)
+
+    def body(t, carry):
+        r = rows_ref[c * slots + t]
+        k = cols_ref[c * slots + t]
+        out_ref[r] += jnp.dot(vals_ref[0, t], panel_ref[0, k], preferred_element_type=jnp.float32)
+        return carry
+
+    lax.fori_loop(0, count_ref[c], body, 0)
+
+
+def backward_kernel(rows_ref, cols_ref, count_ref, vals_ref, grad_ref, out_ref):
+    c = pl.program_id(0)
+    slots = vals_ref.shape[1]
+    out_ref[...] = jnp.zeros_like(out_ref)
+
+    def body(t, carry):
+        r = rows_ref[c * slots + t]
+        k = cols_ref[c * slots + t]
+        out_ref[0, k] += lax.dot_general(
+            vals_ref[0, t], grad_ref[r], (((0,), (0,)), ((), ())), preferred_element_type=jnp.float32
+        )
+        return carry
+
+    lax.fori_loop(0, count_ref[c], body, 0)
+
+
+def tile_forward(rows, cols, count, vals, panels):
+    n_src, slots, tile, _ = vals.shape
+    row_tiles, width = panels.shape[1], panels.shape[3]
+    grid_spec = pltpu.PrefetchScalarGridSpec(
+        num_scalar_prefetch=3,
+        grid=(n_src,),
+        in_specs=[
+            pl.BlockSpec((1, slots, tile, tile), lambda c, *_: (c, 0, 0, 0)),
+            pl.BlockSpec((1, row_tiles, tile, width), lambda c, *_: (c, 0, 0, 0)),
+        ],
+        out_specs=pl.BlockSpec((row_tiles, tile, width), lambda c, *_: (0, 0, 0)),
+    )
+    flops = 2 * n_src * slots * tile * tile * width
+    return pl.pallas_call(
+        forward_kernel,
+        out_shape=jax.ShapeDtypeStruct((row_tiles, tile, width), jnp.float32),
+        grid_spec=grid_spec,
+        cost_estimate=pl.CostEstimate(
+            flops=flops, transcendentals=0, bytes_accessed=vals.size * 2 + panels.size * 2
+        ),
+    )(rows, cols, count, vals, panels)
+
+
+def tile_backward(rows, cols, count, vals, grad_tiles):
+    n_src, slots, tile, _ = vals.shape
+    row_tiles, width = grad_tiles.shape[0], grad_tiles.shape[2]
+    grid_spec = pltpu.PrefetchScalarGridSpec(
+        num_scalar_prefetch=3,
+        grid=(n_src,),
+        in_specs=[
+            pl.BlockSpec((1, slots, tile, tile), lambda c, *_: (c, 0, 0, 0)),
+            pl.BlockSpec((row_tiles, tile, width), lambda c, *_: (0, 0, 0)),
+        ],
+        out_specs=pl.BlockSpec((1, row_tiles, tile, width), lambda c, *_: (c, 0, 0, 0)),
+    )
+    flops = 2 * n_src * slots * tile * tile * width
+    return pl.pallas_call(
+        backward_kernel,
+        out_shape=jax.ShapeDtypeStruct((n_src, row_tiles, tile, width), jnp.float32),
+        grid_spec=grid_spec,
+        cost_estimate=pl.CostEstimate(
+            flops=flops, transcendentals=0, bytes_accessed=vals.size * 2 + n_src * row_tiles * tile * width * 4
+        ),
+    )(rows, cols, count, vals, grad_tiles)
 
 
 def local(
@@ -27,60 +104,26 @@
 ):
     n_blocks = lax.axis_size("blk")
     n_groups = lax.axis_size("grp")
-    my_block = lax.axis_index("blk")
     my_group = lax.axis_index("grp")
     rows_dev = feats.shape[0]
     width = feats.shape[1]
     tile_size = tile_vals.shape[-1]
     row_tiles = rows_dev // tile_size
-    slot_count = tile_vals.shape[3]
     hub_count = hub_vals.shape[2]
     capacity = max(2, hub_count // 4)
     highest = lax.Precision.HIGHEST
     dev_vals = tile_vals[0, 0]
-    dev_rows = tile_row[0, 0]
-    dev_cols = tile_col[0, 0]
+    dev_rows = tile_row[0, 0].reshape(-1)
+    dev_cols = tile_col[0, 0].reshape(-1)
     dev_count = tile_count[0, 0]
     tile_range = jnp.arange(row_tiles, dtype=jnp.int32)
-    slot_range = jnp.arange(slot_count, dtype=jnp.int32)
     proj = jnp.dot(feats, weight, preferred_element_type=jnp.float32).astype(jnp.bfloat16)
     own_panel = proj.reshape(row_tiles, tile_size, width)
 
-    def block_parts(source):
-        blk_vals = lax.dynamic_index_in_dim(dev_vals, source, 0, keepdims=False)
-        blk_rows = lax.dynamic_index_in_dim(dev_rows, source, 0, keepdims=False)
-        blk_cols = lax.dynamic_index_in_dim(dev_cols, source, 0, keepdims=False)
-        blk_count = lax.dynamic_index_in_dim(dev_count, source, 0, keepdims=False)
-        live_mask = (slot_range < blk_count).astype(jnp.float32)
-        return (blk_vals, blk_rows, blk_cols, live_mask)
-
-    def forward_block(source, panel_now):
-        blk_vals, blk_rows, blk_cols, live_mask = block_parts(source)
-        picked = jnp.take(panel_now, blk_cols, axis=0)
-        product = jnp.einsum("tij,tjf->tif", blk_vals, picked, preferred_element_type=jnp.float32)
-        placing = (blk_rows[:, None] == tile_range[None, :]).astype(jnp.float32) * live_mask[
-            :, None
-        ]
-        return jnp.einsum("tr,tif->rif", placing, product, precision=highest)
-
-    def backward_block(target, grad_tiles):
-        blk_vals, blk_rows, blk_cols, live_mask = block_parts(target)
-        picked = jnp.take(grad_tiles, blk_rows, axis=0)
-        product = jnp.einsum("tij,tif->tjf", blk_vals, picked, preferred_element_type=jnp.float32)
-        placing = (blk_cols[:, None] == tile_range[None, :]).astype(jnp.float32) * live_mask[
-            :, None
-        ]
-        return jnp.einsum("tr,tjf->rjf", placing, product, precision=highest)
-
-    agg_sum = forward_block(my_block, own_panel)
-
-    def forward_turn(k, carry):
-        panel_now, running = carry
-        panel_now = shifted(panel_now, "blk", 1)
-        source = (my_block - k) % n_blocks
-        return (panel_now, running + forward_block(source, panel_now))
-
-    _, agg_sum = lax.fori_loop(1, n_blocks, forward_turn, (own_panel, agg_sum))
+    panels = lax.all_gather(proj, "blk", axis=0, tiled=True)
+    panels = panels.reshape(n_blocks, row_tiles, tile_size, width)
+    agg_sum = tile_forward(dev_rows, dev_cols, dev_count, dev_vals, panels)
+
     dest_all = hub_dest[:, 0, :, 0]
     hub_rows_all = hub_row[:, 0, :]
     hub_range = jnp.arange(hub_count, dtype=jnp.int32)
@@ -114,13 +157,10 @@
     keep = (labels >= 0).astype(jnp.float32)[:, None]
     grad_agg = (cotangent.astype(jnp.float32) * keep * slope).astype(jnp.bfloat16)
     grad_tiles = grad_agg.reshape(row_tiles, tile_size, width)
-    grad_sum = backward_block((my_block + n_blocks - 1) % n_blocks, grad_tiles)
-
-    def backward_turn(k, running):
-        running = shifted(running, "blk", 1)
-        return running + backward_block((my_block + n_blocks - 1 - k) % n_blocks, grad_tiles)
-
-    grad_sum = lax.fori_loop(1, n_blocks, backward_turn, grad_sum)
+
+    partials = tile_backward(dev_rows, dev_cols, dev_count, dev_vals, grad_tiles)
+    grad_sum = lax.psum_scatter(partials, "blk", scatter_dimension=0, tiled=True)[0]
+
     back_send = jnp.einsum(
         "scr,rif->scif",
         routing.astype(jnp.bfloat16),

time: 967 us -> 571 us (0.59)
  matrix products: 275 us -> 22.2 us
  waiting for transfers between devices: 483 us -> 342 us
  Pallas kernels: 0 us -> 116 us
  local copies, waits for them, and re-layouts: 122 us -> 19.9 us
  blocking collectives: 0 us -> 42.8 us
  other arithmetic: 46.4 us -> 6.61 us
  starting transfers between devices: 16.2 us -> 6.38 us
    ppermute x30 -> x0, waiting for transfers between devices: 330 us -> none  [shifted(): lax.ppermute(value, axis, [(i, (i + by) % size) for i in range(size)])]
    dot_general x64 -> x0, matrix products: 243 us -> none  [the longest x16 104 us: backward_block(): return jnp.einsum('tr,tjf->rjf', placing, product, precision=highest)]
    reduce_scatter x0 -> x1, waiting for transfers between devices: none -> 122 us  [local(): lax.psum_scatter(partials, 'blk', scatter_dimension=0, tiled=True)[0]]
    pallas_call x0 -> x2, Pallas kernels: none -> 116 us  [the longest x1 65.9 us: tile_backward(): pl.pallas_call(backward_kernel, out_shape=jax.ShapeDtypeStruct((n_src, ro...]
    all_to_all x1, waiting for transfers between devices: 0.01 us -> 48.1 us  [local(): lax.all_to_all(send_buf, 'grp', split_axis=0, concat_axis=0, tiled=True)]
    all_to_all x0 -> x1, blocking collectives: none -> 42.8 us  [local(): lax.all_to_all(back_send, 'grp', split_axis=0, concat_axis=0, tiled=True)]
    all_gather x0 -> x1, waiting for transfers between devices: none -> 28.9 us  [local(): panels = lax.all_gather(proj, 'blk', axis=0, tiled=True)]
    gather x32 -> x0, local copies, waits for them, and re-layouts: 24.5 us -> none  [the longest x16 12.3 us: forward_block(): picked = jnp.take(panel_now, blk_cols, axis=0)]
  transfers between devices with their start and end apart: 33 -> 4, of which waited for: 31 -> 4; matrix products, arithmetic and copies ran while one was open for 29% -> 7% of each run, Pallas kernels for 0% -> 0%
where the time goes in v1:
time: 571 us; the launch traced here: 570 us
  waiting for transfers between devices  342 us (60%)
  Pallas kernels  116 us (20%)
  blocking collectives  42.8 us (7%)
  matrix products  22.2 us (4%)
  local copies, waits for them, and re-layouts  19.9 us (3%)
  between operations  14 us (2%)
  other arithmetic  6.61 us (1%)
  starting transfers between devices  6.38 us (1%)
    psum x1, waiting for transfers between devices, local(): grad_weight = lax.psum(weight_term, ('grp', 'blk')) * grad_scale  142 us
    reduce_scatter x1, waiting for transfers between devices, local(): lax.psum_scatter(partials, 'blk', scatter_dimension=0, tiled=True)[0]  122 us
    pallas_call x1, Pallas kernels, tile_backward(): pl.pallas_call(backward_kernel, out_shape=jax.ShapeDtypeStruct((n_src, ro...  65.9 us
    pallas_call x1, Pallas kernels, tile_forward(): pl.pallas_call(forward_kernel, out_shape=jax.ShapeDtypeStruct((row_tiles,...  50.5 us
    all_to_all x1, waiting for transfers between devices, local(): lax.all_to_all(send_buf, 'grp', split_axis=0, concat_axis=0, tiled=True)  48.1 us
    all_to_all x1, blocking collectives, local(): lax.all_to_all(back_send, 'grp', split_axis=0, concat_axis=0, tiled=True)  42.8 us
    all_gather x1, waiting for transfers between devices, local(): panels = lax.all_gather(proj, 'blk', axis=0, tiled=True)  28.9 us
  transfers between devices with their start and end apart: 4, of which 4 were waited for; matrix products, arithmetic and copies ran while one was open for 7% of the time, Pallas kernels for 0%

profile of v1, /device:TPU:1, one launch (start us, length us, event | category | flops | bytes accessed | tf_op | source)
XLA Modules:
  0.0 569.7 jit_solution(8747163919453422820)
XLA Ops:
  7.2 2.2 convolution_convert_fusion.2
  9.5 0.7 fusion.41
  10.1 1.7 gather_fusion
  11.8 1.9 convolution_bitcast_fusion.1
  13.8 2.2 copy.56
  16.4 3.6 fusion.31
  19.9 5.2 reshape.100
  25.1 5.1 copy.57
  30.2 6.3 %all-to-all-start = ((f32[8,4,128,256]{3,1,2,0:T(4,128)}), f32[8,4,128,256]{3,1,2,0:T(4,128)}, u32[]{:S(2)}, u32[]{:S(2)}) async-start(f32[8,4,128,256]{3,1,2,0:T(4,128)} %copy.57), calls=%async_computation | async-start | bytes 8388608 | tf_op jit(solution)/shard_map/all_to_all | solution.py:145
  36.5 0.7 reshape_squeeze.6.rows_ref
  37.2 0.7 reshape_squeeze.7.cols_ref
  38.0 48.1 %all-to-all-done = f32[8,4,128,256]{3,1,2,0:T(4,128)} async-done(((f32[8,4,128,256]{3,1,2,0:T(4,128)}), f32[8,4,128,256]{3,1,2,0:T(4,128)}, u32[]{:S(2)}, u32[]{:S(2)}) %all-to-all-start) | async-done | bytes 4194336 | tf_op jit(solution)/shard_map/all_to_all | solution.py:145
  86.1 6.8 %convolution_bitcast_fusion.2 = f32[8,128,256]{2,0,1:T(8,128)S(1)} fusion(f32[8,4,128,256]{3,1,2,0:T(4,128)} %all-to-all-done, f32[8,4,8]{2,1,0:T(4,128)S(1)} %fusion.22), kind=kOutput, calls=%fused_computation.7 | convolution fusion | flops 100663296 | bytes 5243904 | tf_op jit(solution)/shard_map/scr,scif->rif/dot_general | solution.py:152
  92.9 28.9 %all-gather.2.cloned.1.call-done = bf16[16384,256]{1,0:T(8,128)(2,1)} async-done(((bf16[1024,256]{1,0:T(8,128)(2,1)}), bf16[16384,256]{1,0:T(8,128)(2,1)}) %all-gather.2.cloned.1.call-update) | async-done | bytes 8388624 | tf_op jit(solution)/shard_map/all_gather | solution.py:123
  121.8 50.5 %shard_map.139 = f32[8,128,256]{2,1,0:T(8,128)} custom-call(s32[512]{0:T(512)} %reshape_squeeze.6.rows_ref, s32[512]{0:T(512)} %reshape_squeeze.7.cols_ref, s32[16]{0:T(128)} %bitcast.108, bf16[16,32,128,128]{3,2,1,0:T(8,128)(2,1)} %bitcast.97, bf16[16,8,128,256]{3,2,1,0:T(8,128)(2,1)} %bitcast.100), custom_call_target="tpu_custom_call" | custom-call | flops 4294967296 | bytes 25165824 | tf_op jit(solution)/shard_map/pallas_call | solution.py:58
  172.3 1.7 copy_add_fusion
  174.0 1.4 fusion.13
  175.4 65.9 %shard_map.140 = f32[16,8,128,256]{3,2,1,0:T(8,128)} custom-call(s32[512]{0:T(512)} %reshape_squeeze.6.rows_ref, s32[512]{0:T(512)} %reshape_squeeze.7.cols_ref, s32[16]{0:T(128)} %bitcast.109, bf16[16,32,128,128]{3,2,1,0:T(8,128)(2,1)} %bitcast.98, bf16[8,128,256]{2,1,0:T(8,128)(2,1)} %bitcast.102), custom_call_target="tpu_custom_call" | custom-call | flops 4294967296 | bytes 33554432 | tf_op jit(solution)/shard_map/pallas_call | solution.py:81
  241.5 1.0 copy-done.1
  242.4 0.7 convolution_convert_fusion
  243.6 42.8 %all_to_all.10 = bf16[8,4,128,256]{3,2,1,0:T(8,128)(2,1)S(1)} all-to-all(bf16[8,4,128,256]{3,2,1,0:T(8,128)(2,1)S(1)} %copy.62), channel_id=1, replica_groups=mesh['grp'=8,'blk'=16] {'grp'}, dimensions={0} | all-to-all | bytes 4194304 | tf_op jit(solution)/shard_map/all_to_all | solution.py:170
  286.4 1.3 fusion.2
  287.6 0.6 convolution_bitcast_fusion
  288.2 2.1 copy.65
  290.2 2.8 fusion.38
  293.1 122.5 %reduce-scatter.2.cloned.1.call-done = f32[1,8,128,256]{3,2,1,0:T(8,128)} async-done(((f32[16,8,128,256]{3,2,1,0:T(8,128)}), f32[1,8,128,256]{3,2,1,0:T(8,128)}) %reduce-scatter.2.cloned.1.call-update) | async-done | bytes 1048592 | tf_op jit(solution)/shard_map/reduce_scatter | solution.py:162
  415.6 1.6 fusion.5
  417.1 1.0 convolution_bitcast_fusion.3
  418.2 1.1 convolution_convert_fusion.1
  419.3 142.0 %all-reduce.2.cloned.1.call-done = f32[256,256]{0,1:T(8,128)} async-done(((f32[256,256]{0,1:T(8,128)}), f32[256,256]{0,1:T(8,128)}) %all-reduce.2.cloned.1.call-update) | async-done | bytes 262160 | tf_op jit(solution)/shard_map/psum | solution.py:186
  561.4 1.0 broadcast_multiply_fusion
  562.3 0.8 copy.67
  (37 shorter events, 1.2 us)
Async XLA Ops:
  7.2 4.7 copy-start
  7.2 4.6 copy-start.9
  7.2 114.6 %all-gather.2.cloned.1.call-start = ((), (), s32[]{:S(2)}) async-start(), calls=%async_computation.3 | async-start | bytes 8912896 | tf_op jit(solution)/shard_map/all_gather | solution.py:123
  13.8 2.3 copy-start.5
  30.2 6.3 %copy-start.6 = (s32[1,1,16,32]{3,2,1,0:T(8,128)S(1)}, s32[1,1,16,32]{3,2,1,0:T(8,128)}, u32[]{:S(2)}) copy-start(s32[1,1,16,32]{3,2,1,0:T(8,128)} %param.17) | copy-start | bytes 6148
  30.2 7.0 %copy-start.7 = (s32[1,1,16,32]{3,2,1,0:T(8,128)S(1)}, s32[1,1,16,32]{3,2,1,0:T(8,128)}, u32[]{:S(2)}) copy-start(s32[1,1,16,32]{3,2,1,0:T(8,128)} %param.18) | copy-start | bytes 6148
  30.2 7.6 %copy-start.8 = (s32[1024]{0:T(1024)S(1)}, s32[1024]{0:T(1024)}, u32[]{:S(2)}) copy-start(s32[1024]{0:T(1024)} %param.15) | copy-start | bytes 12292
  30.2 7.6 %copy-start.10 = (s32[8,1,16]{2,1,0:T(1,128)S(1)}, s32[8,1,16]{2,1,0:T(1,128)}, u32[]{:S(2)}) copy-start(s32[8,1,16]{2,1,0:T(1,128)} %param.23) | copy-start | bytes 1540
  30.2 55.9 %all-to-all-start = ((f32[8,4,128,256]{3,1,2,0:T(4,128)}), f32[8,4,128,256]{3,1,2,0:T(4,128)}, u32[]{:S(2)}, u32[]{:S(2)}) async-start(f32[8,4,128,256]{3,1,2,0:T(4,128)} %copy.57), calls=%async_computation | async-start | bytes 8388608 | tf_op jit(solution)/shard_map/all_to_all | solution.py:145
  36.5 379.1 %reduce-scatter.2.cloned.1.call-start = ((), (), s32[]{:S(2)}) async-start(), calls=%async_computation.4 | async-start | bytes 17825792 | tf_op jit(solution)/shard_map/reduce_scatter | solution.py:162
  172.3 1.7 copy-start.3
  241.4 1.0 copy-start.1
  241.4 320.0 %all-reduce.2.cloned.1.call-start = ((), (), s32[]{:S(2)}) async-start(), calls=%async_computation.5 | async-start | bytes 524288 | tf_op jit(solution)/shard_map/psum | solution.py:186
  293.1 124.1 %copy-start.2 = (bf16[1024,256]{1,0:T(8,128)(2,1)S(1)}, bf16[1024,256]{1,0:T(8,128)(2,1)}, u32[]{:S(2)}) copy-start(bf16[1024,256]{1,0:T(8,128)(2,1)} %param.12) | copy-start | bytes 1572868
  293.1 125.1 %copy-start.4 = (bf16[256,256]{1,0:T(8,128)(2,1)S(1)}, bf16[256,256]{1,0:T(8,128)(2,1)}, u32[]{:S(2)}) copy-start(bf16[256,256]{1,0:T(8,128)(2,1)} %param.13) | copy-start | bytes 393220
Sparse Core Ops, SparseCore 0:
  11.0 110.7 all-gather.1
  241.5 173.9 reduce-scatter.1
  421.6 139.7 all-reduce.1

commit v2 on v1

--- a/solution.py
+++ b/solution.py
@@ -9,37 +9,66 @@
 from jax.sharding import PartitionSpec as P
 
 
+UNROLL = 4
+
+
+def grouped_slots(count, slots, visit):
+    def body(g, carry):
+        terms = []
+        for j in range(UNROLL):
+            t = g * UNROLL + j
+            terms.append((t, t < count))
+        visit(terms)
+        return carry
+
+    lax.fori_loop(0, (count + UNROLL - 1) // UNROLL, body, 0)
+
+
+def clamp_tile(index, limit):
+    return jnp.minimum(jnp.maximum(index, 0), limit - 1)
+
+
 def forward_kernel(rows_ref, cols_ref, count_ref, vals_ref, panel_ref, out_ref):
     c = pl.program_id(0)
     slots = vals_ref.shape[1]
+    row_tiles = out_ref.shape[0]
 
     @pl.when(c == 0)
     def _():
         out_ref[...] = jnp.zeros_like(out_ref)
 
-    def body(t, carry):
-        r = rows_ref[c * slots + t]
-        k = cols_ref[c * slots + t]
-        out_ref[r] += jnp.dot(vals_ref[0, t], panel_ref[0, k], preferred_element_type=jnp.float32)
-        return carry
-
-    lax.fori_loop(0, count_ref[c], body, 0)
+    def visit(terms):
+        parts = []
+        for t, valid in terms:
+            r = clamp_tile(rows_ref[c * slots + t], row_tiles)
+            k = clamp_tile(cols_ref[c * slots + t], row_tiles)
+            prod = jnp.dot(vals_ref[0, t], panel_ref[0, k], preferred_element_type=jnp.float32)
+            parts.append((r, jnp.where(valid, prod, 0.0)))
+        for r, prod in parts:
+            out_ref[r] += prod
+
+    grouped_slots(count_ref[c], slots, visit)
 
 
 def backward_kernel(rows_ref, cols_ref, count_ref, vals_ref, grad_ref, out_ref):
     c = pl.program_id(0)
     slots = vals_ref.shape[1]
+    row_tiles = grad_ref.shape[0]
     out_ref[...] = jnp.zeros_like(out_ref)
 
-    def body(t, carry):
-        r = rows_ref[c * slots + t]
-        k = cols_ref[c * slots + t]
-        out_ref[0, k] += lax.dot_general(
-            vals_ref[0, t], grad_ref[r], (((0,), (0,)), ((), ())), preferred_element_type=jnp.float32
-        )
-        return carry
-
-    lax.fori_loop(0, count_ref[c], body, 0)
+    def visit(terms):
+        parts = []
+        for t, valid in terms:
+            r = clamp_tile(rows_ref[c * slots + t], row_tiles)
+            k = clamp_tile(cols_ref[c * slots + t], row_tiles)
+            prod = lax.dot_general(
+                vals_ref[0, t], grad_ref[r], (((0,), (0,)), ((), ())), preferred_element_type=jnp.float32
+            )
+            parts.append((k, jnp.where(valid, prod, 0.0)))
+        for k, prod in parts:
+            out_ref[0, k] += prod
+
+    grouped_slots(count_ref[c], slots, visit)
 
 
 def tile_forward(rows, cols, count, vals, panels):
@@ -183,7 +212,7 @@
         feats, grad_rows, (((0,), (0,)), ((), ())), preferred_element_type=jnp.float32
     )
     grad_scale = 1.0 / math.sqrt(rows_dev * n_blocks * n_groups)
-    grad_weight = lax.psum(weight_term, ("grp", "blk")) * grad_scale
+    grad_weight = lax.psum(lax.psum(weight_term, "blk"), "grp") * grad_scale
     grad_feats = lax.dot_general(
         grad_rows, weight, (((1,), (1,)), ((), ())), preferred_element_type=jnp.float32
     ).astype(jnp.bfloat16)

time: 571 us -> 554 us (0.970)
  Pallas kernels: 116 us -> 59.4 us
  waiting for transfers between devices: 342 us -> 390 us
  blocking collectives: 42.8 us -> 30.5 us
    psum x1 -> x2, waiting for transfers between devices: 142 us -> 207 us  [local(): grad_weight = lax.psum(lax.psum(weight_term, 'blk'), 'grp') * grad_scale]
    pallas_call x1, Pallas kernels: 65.9 us -> 31.8 us  [tile_backward(): pl.pallas_call(backward_kernel, out_shape=jax.ShapeDtypeStruct((n_src, ro...]
    pallas_call x1, Pallas kernels: 50.5 us -> 27.5 us  [tile_forward(): pl.pallas_call(forward_kernel, out_shape=jax.ShapeDtypeStruct((row_tiles,...]
    reduce_scatter x1, waiting for transfers between devices: 122 us -> 105 us  [local(): lax.psum_scatter(partials, 'blk', scatter_dimension=0, tiled=True)[0]]
    all_to_all x1, blocking collectives: 42.8 us -> 30.5 us  [local(): lax.all_to_all(back_send, 'grp', split_axis=0, concat_axis=0, tiled=True)]
  transfers between devices with their start and end apart: 4 -> 5, of which waited for: 4 -> 5; matrix products, arithmetic and copies ran while one was open for 7% -> 7% of each run, Pallas kernels for 0% -> 0%
where the time goes in v2:
time: 554 us; the launch traced here: 548 us
  waiting for transfers between devices  390 us (70%)
  Pallas kernels  59.4 us (11%)
  blocking collectives  30.5 us (6%)
  matrix products  21.7 us (4%)
  local copies, waits for them, and re-layouts  19.9 us (4%)
  between operations  14 us (3%)
  other arithmetic  6.61 us (1%)
  starting transfers between devices  6.42 us (1%)
    psum x2, waiting for transfers between devices, local(): grad_weight = lax.psum(lax.psum(weight_term, 'blk'), 'grp') * grad_scale  207 us
    reduce_scatter x1, waiting for transfers between devices, local(): lax.psum_scatter(partials, 'blk', scatter_dimension=0, tiled=True)[0]  105 us
    all_to_all x1, waiting for transfers between devices, local(): lax.all_to_all(send_buf, 'grp', split_axis=0, concat_axis=0, tiled=True)  48.1 us
    pallas_call x1, Pallas kernels, tile_backward(): pl.pallas_call(backward_kernel, out_shape=jax.ShapeDtypeStruct((n_src, ro...  31.8 us
    all_to_all x1, blocking collectives, local(): lax.all_to_all(back_send, 'grp', split_axis=0, concat_axis=0, tiled=True)  30.5 us
    all_gather x1, waiting for transfers between devices, local(): panels = lax.all_gather(proj, 'blk', axis=0, tiled=True)  28.9 us
    pallas_call x1, Pallas kernels, tile_forward(): pl.pallas_call(forward_kernel, out_shape=jax.ShapeDtypeStruct((row_tiles,...  27.5 us
  transfers between devices with their start and end apart: 5, of which 5 were waited for; matrix products, arithmetic and copies ran while one was open for 7% of the time, Pallas kernels for 0%

profile of v2, /device:TPU:1, one launch (start us, length us, event | category | flops | bytes accessed | tf_op | source)
XLA Modules:
  0.0 548.2 jit_solution(10463152768806692617)
XLA Ops:
  7.2 2.2 convolution_convert_fusion.2
  9.5 0.7 fusion.41
  10.1 1.7 gather_fusion
  11.8 1.9 convolution_bitcast_fusion.1
  13.8 2.2 copy.56
  16.4 3.6 fusion.31
  19.9 5.2 reshape.100
  25.1 5.1 copy.57
  30.2 6.3 %all-to-all-start = ((f32[8,4,128,256]{3,1,2,0:T(4,128)}), f32[8,4,128,256]{3,1,2,0:T(4,128)}, u32[]{:S(2)}, u32[]{:S(2)}) async-start(f32[8,4,128,256]{3,1,2,0:T(4,128)} %copy.57), calls=%async_computation | async-start | bytes 8388608 | tf_op jit(solution)/shard_map/all_to_all | solution.py:174
  36.5 0.7 reshape_squeeze.6.rows_ref
  37.2 0.7 reshape_squeeze.7.cols_ref
  38.0 48.1 %all-to-all-done = f32[8,4,128,256]{3,1,2,0:T(4,128)} async-done(((f32[8,4,128,256]{3,1,2,0:T(4,128)}), f32[8,4,128,256]{3,1,2,0:T(4,128)}, u32[]{:S(2)}, u32[]{:S(2)}) %all-to-all-start) | async-done | bytes 4194336 | tf_op jit(solution)/shard_map/all_to_all | solution.py:174
  86.1 6.8 %convolution_bitcast_fusion.2 = f32[8,128,256]{2,0,1:T(8,128)S(1)} fusion(f32[8,4,128,256]{3,1,2,0:T(4,128)} %all-to-all-done, f32[8,4,8]{2,1,0:T(4,128)S(1)} %fusion.22), kind=kOutput, calls=%fused_computation.7 | convolution fusion | flops 100663296 | bytes 5243904 | tf_op jit(solution)/shard_map/scr,scif->rif/dot_general | solution.py:181
  92.9 28.9 %all-gather.2.cloned.1.call-done = bf16[16384,256]{1,0:T(8,128)(2,1)} async-done(((bf16[1024,256]{1,0:T(8,128)(2,1)}), bf16[16384,256]{1,0:T(8,128)(2,1)}) %all-gather.2.cloned.1.call-update) | async-done | bytes 8388624 | tf_op jit(solution)/shard_map/all_gather | solution.py:152
  121.8 27.5 %shard_map.139 = f32[8,128,256]{2,1,0:T(8,128)} custom-call(s32[512]{0:T(512)} %reshape_squeeze.6.rows_ref, s32[512]{0:T(512)} %reshape_squeeze.7.cols_ref, s32[16]{0:T(128)} %bitcast.108, bf16[16,32,128,128]{3,2,1,0:T(8,128)(2,1)} %bitcast.97, bf16[16,8,128,256]{3,2,1,0:T(8,128)(2,1)} %bitcast.100), custom_call_target="tpu_custom_call" | custom-call | flops 4294967296 | bytes 25165824 | tf_op jit(solution)/shard_map/pallas_call | solution.py:87
  149.4 1.7 copy_add_fusion
  151.0 1.4 fusion.13
  152.5 31.8 %shard_map.140 = f32[16,8,128,256]{3,2,1,0:T(8,128)} custom-call(s32[512]{0:T(512)} %reshape_squeeze.6.rows_ref, s32[512]{0:T(512)} %reshape_squeeze.7.cols_ref, s32[16]{0:T(128)} %bitcast.109, bf16[16,32,128,128]{3,2,1,0:T(8,128)(2,1)} %bitcast.98, bf16[8,128,256]{2,1,0:T(8,128)(2,1)} %bitcast.102), custom_call_target="tpu_custom_call" | custom-call | flops 4294967296 | bytes 33554432 | tf_op jit(solution)/shard_map/pallas_call | solution.py:110
  184.4 1.0 copy-done.1
  185.3 0.7 convolution_convert_fusion
  186.5 30.5 %all_to_all.10 = bf16[8,4,128,256]{3,2,1,0:T(8,128)(2,1)S(1)} all-to-all(bf16[8,4,128,256]{3,2,1,0:T(8,128)(2,1)S(1)} %copy.62), channel_id=1, replica_groups=mesh['grp'=8,'blk'=16] {'grp'}, dimensions={0} | all-to-all | bytes 4194304 | tf_op jit(solution)/shard_map/all_to_all | solution.py:199
  217.0 1.3 fusion.2
  218.8 2.1 copy.65
  220.8 2.4 fusion.38
  223.3 105.3 %reduce-scatter.2.cloned.1.call-done = f32[1,8,128,256]{3,2,1,0:T(8,128)} async-done(((f32[16,8,128,256]{3,2,1,0:T(8,128)}), f32[1,8,128,256]{3,2,1,0:T(8,128)}) %reduce-scatter.2.cloned.1.call-update) | async-done | bytes 1048592 | tf_op jit(solution)/shard_map/reduce_scatter | solution.py:191
  328.5 1.6 fusion.5
  330.1 1.0 convolution_bitcast_fusion.3
  331.2 136.2 %all-reduce.3.cloned.1.call-done = f32[256,256]{0,1:T(8,128)} async-done(((f32[256,256]{0,1:T(8,128)}), f32[256,256]{0,1:T(8,128)}) %all-reduce.3.cloned.1.call-update) | async-done | bytes 262160 | tf_op jit(solution)/shard_map/psum | solution.py:215
  467.5 1.1 convolution_convert_fusion.1
  468.6 71.2 %all-reduce.5.cloned.1.call-done = f32[256,256]{0,1:T(8,128)} async-done(((f32[256,256]{0,1:T(8,128)}), f32[256,256]{0,1:T(8,128)}) %all-reduce.5.cloned.1.call-update) | async-done | bytes 262160 | tf_op jit(solution)/shard_map/psum | solution.py:215
  539.8 1.0 broadcast_multiply_fusion
  540.8 0.8 copy.67
  (40 shorter events, 1.8 us)
Async XLA Ops:
  7.2 4.7 copy-start
  7.2 4.6 copy-start.9
  7.2 114.6 %all-gather.2.cloned.1.call-start = ((), (), s32[]{:S(2)}) async-start(), calls=%async_computation.3 | async-start | bytes 8912896 | tf_op jit(solution)/shard_map/all_gather | solution.py:152
  13.8 2.3 copy-start.5
  30.2 6.3 %copy-start.6 = (s32[1,1,16,32]{3,2,1,0:T(8,128)S(1)}, s32[1,1,16,32]{3,2,1,0:T(8,128)}, u32[]{:S(2)}) copy-start(s32[1,1,16,32]{3,2,1,0:T(8,128)} %param.17) | copy-start | bytes 6148
  30.2 7.0 %copy-start.7 = (s32[1,1,16,32]{3,2,1,0:T(8,128)S(1)}, s32[1,1,16,32]{3,2,1,0:T(8,128)}, u32[]{:S(2)}) copy-start(s32[1,1,16,32]{3,2,1,0:T(8,128)} %param.18) | copy-start | bytes 6148
  30.2 7.6 %copy-start.8 = (s32[1024]{0:T(1024)S(1)}, s32[1024]{0:T(1024)}, u32[]{:S(2)}) copy-start(s32[1024]{0:T(1024)} %param.15) | copy-start | bytes 12292
  30.2 7.6 %copy-start.10 = (s32[8,1,16]{2,1,0:T(1,128)S(1)}, s32[8,1,16]{2,1,0:T(1,128)}, u32[]{:S(2)}) copy-start(s32[8,1,16]{2,1,0:T(1,128)} %param.23) | copy-start | bytes 1540
  30.2 55.9 %all-to-all-start = ((f32[8,4,128,256]{3,1,2,0:T(4,128)}), f32[8,4,128,256]{3,1,2,0:T(4,128)}, u32[]{:S(2)}, u32[]{:S(2)}) async-start(f32[8,4,128,256]{3,1,2,0:T(4,128)} %copy.57), calls=%async_computation | async-start | bytes 8388608 | tf_op jit(solution)/shard_map/all_to_all | solution.py:174
  36.5 292.1 %reduce-scatter.2.cloned.1.call-start = ((), (), s32[]{:S(2)}) async-start(), calls=%async_computation.4 | async-start | bytes 17825792 | tf_op jit(solution)/shard_map/reduce_scatter | solution.py:191
  149.4 1.7 copy-start.3
  184.3 1.0 copy-start.1
  184.3 283.1 %all-reduce.3.cloned.1.call-start = ((), (), s32[]{:S(2)}) async-start(), calls=%async_computation.5 | async-start | bytes 524288 | tf_op jit(solution)/shard_map/psum | solution.py:215
  223.2 106.9 %copy-start.2 = (bf16[1024,256]{1,0:T(8,128)(2,1)S(1)}, bf16[1024,256]{1,0:T(8,128)(2,1)}, u32[]{:S(2)}) copy-start(bf16[1024,256]{1,0:T(8,128)(2,1)} %param.12) | copy-start | bytes 1572868
  223.2 244.2 %copy-start.4 = (bf16[256,256]{1,0:T(8,128)(2,1)S(1)}, bf16[256,256]{1,0:T(8,128)(2,1)}, u32[]{:S(2)}) copy-start(bf16[256,256]{1,0:T(8,128)(2,1)} %param.13) | copy-start | bytes 393220
  331.2 208.6 %all-reduce.5.cloned.1.call-start = ((), (), s32[]{:S(2)}) async-start(), calls=%async_computation.6 | async-start | bytes 524288 | tf_op jit(solution)/shard_map/psum | solution.py:215
Sparse Core Ops, SparseCore 0:
  11.0 110.7 all-gather.1
  184.4 144.0 reduce-scatter.1
  331.7 135.6 all-reduce.2
  469.8 69.9 all-reduce.4

commit v3 on v2

--- a/solution.py
+++ b/solution.py
@@ -115,6 +115,101 @@
             flops=flops, transcendentals=0, bytes_accessed=vals.size * 2 + n_src * row_tiles * tile * width * 4
         ),
     )(rows, cols, count, vals, grad_tiles)
+
+MESH_ID = pl.DeviceIdType.MESH
+
+
+def weight_sum_kernel(n_grp, n_blk, x_ref, out_ref, part, grp_part, whole, sems):
+    g = lax.axis_index("grp")
+    b = lax.axis_index("blk")
+    send1, recv1, send2, recv2, send3, recv3 = sems
+    barrier = pltpu.get_barrier_semaphore()
+    for i in range(1, n_blk):
+        pl.semaphore_signal(barrier, 1, device_id=(g, (b + i) % n_blk), device_id_type=MESH_ID)
+    for i in range(1, n_grp):
+        pl.semaphore_signal(barrier, 1, device_id=((g + i) % n_grp, b), device_id_type=MESH_ID)
+    pl.semaphore_wait(barrier, n_blk - 1 + n_grp - 1)
+
+    def blk_copy(src, dst, send, recv, to, slot):
+        return pltpu.make_async_remote_copy(
+            src_ref=src, dst_ref=dst, send_sem=send.at[to], recv_sem=recv.at[slot],
+            device_id=(g, to), device_id_type=MESH_ID,
+        )
+
+    def grp_copy(src, dst, send, recv, to, slot):
+        return pltpu.make_async_remote_copy(
+            src_ref=src, dst_ref=dst, send_sem=send.at[to], recv_sem=recv.at[slot],
+            device_id=(to, b), device_id_type=MESH_ID,
+        )
+
+    out1 = []
+    for i in range(1, n_blk):
+        to = (b + i) % n_blk
+        cp = blk_copy(x_ref.at[to], part.at[b], send1, recv1, to, b)
+        cp.start()
+        out1.append(cp)
+    part[b] = x_ref[b]
+    for i in range(1, n_blk):
+        src = (b + n_blk - i) % n_blk
+        blk_copy(x_ref.at[b], part.at[src], send1, recv1, src, src).wait_recv()
+    for cp in out1:
+        cp.wait_send()
+    acc = part[0]
+    for j in range(1, n_blk):
+        acc = acc + part[j]
+    grp_part[g] = acc
+
+    out2 = []
+    for i in range(1, n_grp):
+        to = (g + i) % n_grp
+        cp = grp_copy(grp_part.at[g], grp_part.at[g], send2, recv2, to, g)
+        cp.start()
+        out2.append(cp)
+    for i in range(1, n_grp):
+        src = (g + n_grp - i) % n_grp
+        grp_copy(grp_part.at[src], grp_part.at[src], send2, recv2, src, src).wait_recv()
+    for cp in out2:
+        cp.wait_send()
+    acc = grp_part[0]
+    for j in range(1, n_grp):
+        acc = acc + grp_part[j]
+    whole[b] = acc
+
+    out3 = []
+    for i in range(1, n_blk):
+        to = (b + i) % n_blk
+        cp = blk_copy(whole.at[b], whole.at[b], send3, recv3, to, b)
+        cp.start()
+        out3.append(cp)
+    for i in range(1, n_blk):
+        src = (b + n_blk - i) % n_blk
+        blk_copy(whole.at[src], whole.at[src], send3, recv3, src, src).wait_recv()
+    for cp in out3:
+        cp.wait_send()
+    out_ref[...] = whole[...]
+
+
+def weight_sum(term, n_grp, n_blk):
+    rows, cols = term.shape
+    chunk = rows * cols // (n_blk * 128)
+    x = term.reshape(n_blk, chunk, 128)
+    vmem = pl.BlockSpec(memory_space=pltpu.VMEM)
+    out = pl.pallas_call(
+        functools.partial(weight_sum_kernel, n_grp, n_blk),
+        out_shape=jax.ShapeDtypeStruct(x.shape, jnp.float32),
+        in_specs=[vmem],
+        out_specs=vmem,
+        scratch_shapes=[
+            pltpu.VMEM(x.shape, jnp.float32),
+            pltpu.VMEM((n_grp, chunk, 128), jnp.float32),
+            pltpu.VMEM(x.shape, jnp.float32),
+            [pltpu.SemaphoreType.DMA((n_blk,)), pltpu.SemaphoreType.DMA((n_blk,)),
+             pltpu.SemaphoreType.DMA((n_grp,)), pltpu.SemaphoreType.DMA((n_grp,)),
+             pltpu.SemaphoreType.DMA((n_blk,)), pltpu.SemaphoreType.DMA((n_blk,))],
+        ],
+        compiler_params=pltpu.CompilerParams(collective_id=0, has_side_effects=True),
+    )(x)
+    return out.reshape(rows, cols)
 
 
 def local(
@@ -212,7 +307,7 @@
         feats, grad_rows, (((0,), (0,)), ((), ())), preferred_element_type=jnp.float32
     )
     grad_scale = 1.0 / math.sqrt(rows_dev * n_blocks * n_groups)
-    grad_weight = lax.psum(lax.psum(weight_term, "blk"), "grp") * grad_scale
+    grad_weight = weight_sum(weight_term, n_groups, n_blocks) * grad_scale
     grad_feats = lax.dot_general(
         grad_rows, weight, (((1,), (1,)), ((), ())), preferred_element_type=jnp.float32
     ).astype(jnp.bfloat16)

time: 554 us -> 367 us (0.66)
  waiting for transfers between devices: 390 us -> 186 us
  Pallas kernels: 59.4 us -> 78 us
    psum x2 -> x0, waiting for transfers between devices: 207 us -> none  [local(): grad_weight = lax.psum(lax.psum(weight_term, 'blk'), 'grp') * grad_scale]
    pallas_call x0 -> x1, Pallas kernels: none -> 22.9 us  [weight_sum(): pl.pallas_call(functools.partial(weight_sum_kernel, n_grp, n_blk), out_sh...]
  transfers between devices with their start and end apart: 5 -> 3, of which waited for: 5 -> 3; matrix products, arithmetic and copies ran while one was open for 7% -> 10% of each run, Pallas kernels for 0% -> 0%
where the time goes in v3:
time: 367 us; the launch traced here: 365 us
  waiting for transfers between devices  186 us (51%)
  Pallas kernels  78 us (21%)
  blocking collectives  32.7 us (9%)
  matrix products  21 us (6%)
  local copies, waits for them, and re-layouts  20.7 us (6%)
  between operations  14.3 us (4%)
  other arithmetic  6.62 us (2%)
  starting transfers between devices  6.33 us (2%)
    reduce_scatter x1, waiting for transfers between devices, local(): lax.psum_scatter(partials, 'blk', scatter_dimension=0, tiled=True)[0]  109 us
    all_to_all x1, waiting for transfers between devices, local(): lax.all_to_all(send_buf, 'grp', split_axis=0, concat_axis=0, tiled=True)  48.1 us
    all_to_all x1, blocking collectives, local(): lax.all_to_all(back_send, 'grp', split_axis=0, concat_axis=0, tiled=True)  32.7 us
    pallas_call x1, Pallas kernels, tile_backward(): pl.pallas_call(backward_kernel, out_shape=jax.ShapeDtypeStruct((n_src, ro...  29.6 us
    all_gather x1, waiting for transfers between devices, local(): panels = lax.all_gather(proj, 'blk', axis=0, tiled=True)  28.9 us
    pallas_call x1, Pallas kernels, tile_forward(): pl.pallas_call(forward_kernel, out_shape=jax.ShapeDtypeStruct((row_tiles,...  25.6 us
    pallas_call x1, Pallas kernels, weight_sum(): pl.pallas_call(functools.partial(weight_sum_kernel, n_grp, n_blk), out_sh...  22.9 us
    reshape x2, local copies, waits for them, and re-layouts, local(): send_buf = send_buf.reshape(n_groups, capacity, tile_size, width)  10.3 us
  transfers between devices with their start and end apart: 3, of which 3 were waited for; matrix products, arithmetic and copies ran while one was open for 10% of the time, Pallas kernels for 0%

profile of v3, /device:TPU:1, one launch (start us, length us, event | category | flops | bytes accessed | tf_op | source)
XLA Modules:
  0.0 365.3 jit_solution(3011504003118858723)
XLA Ops:
  7.2 2.2 convolution_convert_fusion.2
  9.5 0.7 fusion.41
  10.1 1.7 gather_fusion
  11.8 1.9 convolution_bitcast_fusion.1
  13.8 2.2 copy.56
  16.4 3.6 fusion.31
  19.9 5.2 %reshape.106 = f32[8,4,128,256]{3,1,0,2:T(4,128)} reshape(f32[32,128,256]{2,0,1:T(8,128)} %fusion.31) | data formatting | bytes 8388608 | tf_op jit(solution)/shard_map/reshape | solution.py:268
  25.1 5.1 %copy.57 = f32[8,4,128,256]{3,1,2,0:T(4,128)} copy(f32[8,4,128,256]{3,1,0,2:T(4,128)} %reshape.106) | data formatting | bytes 8388608 | tf_op jit(solution)/shard_map/reshape | solution.py:268
  30.2 6.3 %all-to-all-start = ((f32[8,4,128,256]{3,1,2,0:T(4,128)}), f32[8,4,128,256]{3,1,2,0:T(4,128)}, u32[]{:S(2)}, u32[]{:S(2)}) async-start(f32[8,4,128,256]{3,1,2,0:T(4,128)} %copy.57), calls=%async_computation | async-start | bytes 8388608 | tf_op jit(solution)/shard_map/all_to_all | solution.py:269
  36.5 0.7 reshape_squeeze.6.rows_ref
  37.2 0.7 reshape_squeeze.7.cols_ref
  38.0 48.1 %all-to-all-done = f32[8,4,128,256]{3,1,2,0:T(4,128)} async-done(((f32[8,4,128,256]{3,1,2,0:T(4,128)}), f32[8,4,128,256]{3,1,2,0:T(4,128)}, u32[]{:S(2)}, u32[]{:S(2)}) %all-to-all-start) | async-done | bytes 4194336 | tf_op jit(solution)/shard_map/all_to_all | solution.py:269
  86.1 6.8 %convolution_bitcast_fusion.2 = f32[8,128,256]{2,0,1:T(8,128)S(1)} fusion(f32[8,4,128,256]{3,1,2,0:T(4,128)} %all-to-all-done, f32[8,4,8]{2,1,0:T(4,128)S(1)} %fusion.22), kind=kOutput, calls=%fused_computation.7 | convolution fusion | flops 100663296 | bytes 5243904 | tf_op jit(solution)/shard_map/scr,scif->rif/dot_general | solution.py:276
  92.9 28.9 %all-gather.2.cloned.1.call-done = bf16[16384,256]{1,0:T(8,128)(2,1)} async-done(((bf16[1024,256]{1,0:T(8,128)(2,1)}), bf16[16384,256]{1,0:T(8,128)(2,1)}) %all-gather.2.cloned.1.call-update) | async-done | bytes 8388624 | tf_op jit(solution)/shard_map/all_gather | solution.py:247
  121.8 25.6 %shard_map.139 = f32[8,128,256]{2,1,0:T(8,128)} custom-call(s32[512]{0:T(512)} %reshape_squeeze.6.rows_ref, s32[512]{0:T(512)} %reshape_squeeze.7.cols_ref, s32[16]{0:T(128)} %bitcast.108, bf16[16,32,128,128]{3,2,1,0:T(8,128)(2,1)} %bitcast.97, bf16[16,8,128,256]{3,2,1,0:T(8,128)(2,1)} %bitcast.100), custom_call_target="tpu_custom_call" | custom-call | flops 4294967296 | bytes 25165824 | tf_op jit(solution)/shard_map/pallas_call | solution.py:87
  147.4 1.7 copy_add_fusion
  149.1 1.4 fusion.13
  150.5 29.6 %shard_map.140 = f32[16,8,128,256]{3,2,1,0:T(8,128)} custom-call(s32[512]{0:T(512)} %reshape_squeeze.6.rows_ref, s32[512]{0:T(512)} %reshape_squeeze.7.cols_ref, s32[16]{0:T(128)} %bitcast.109, bf16[16,32,128,128]{3,2,1,0:T(8,128)(2,1)} %bitcast.98, bf16[8,128,256]{2,1,0:T(8,128)(2,1)} %bitcast.102), custom_call_target="tpu_custom_call" | custom-call | flops 4294967296 | bytes 33554432 | tf_op jit(solution)/shard_map/pallas_call | solution.py:110
  180.1 1.0 copy-done.1
  181.1 0.7 convolution_convert_fusion
  182.3 32.7 %all_to_all.10 = bf16[8,4,128,256]{3,2,1,0:T(8,128)(2,1)S(1)} all-to-all(bf16[8,4,128,256]{3,2,1,0:T(8,128)(2,1)S(1)} %copy.62), channel_id=1, replica_groups=mesh['grp'=8,'blk'=16] {'grp'}, dimensions={0} | all-to-all | bytes 4194304 | tf_op jit(solution)/shard_map/all_to_all | solution.py:294
  215.0 1.3 fusion.2
  216.2 0.6 convolution_bitcast_fusion
  216.8 2.1 copy.65
  218.8 2.4 fusion.38
  221.3 108.7 %reduce-scatter.2.cloned.1.call-done = f32[1,8,128,256]{3,2,1,0:T(8,128)} async-done(((f32[16,8,128,256]{3,2,1,0:T(8,128)}), f32[1,8,128,256]{3,2,1,0:T(8,128)}) %reduce-scatter.2.cloned.1.call-update) | async-done | bytes 1048592 | tf_op jit(solution)/shard_map/reduce_scatter | solution.py:286
  330.0 1.6 fusion.5
  331.5 1.1 convolution_convert_fusion.1
  333.1 0.7 reshape.110.x_ref
  333.9 22.9 %shard_map.141 = f32[16,32,128]{2,1,0:T(8,128)} custom-call(f32[16,32,128]{2,1,0:T(8,128)} %reshape.110.x_ref), custom_call_target="tpu_custom_call" | custom-call | tf_op jit(solution)/shard_map/pallas_call | solution.py:197
  356.7 1.0 broadcast_multiply_fusion
  357.7 0.8 mul.60
  (37 shorter events, 1.6 us)
Async XLA Ops:
  7.2 4.7 %copy-start = (bf16[1,1,16,128,128]{4,3,2,1,0:T(8,128)(2,1)S(1)}, bf16[1,1,16,128,128]{4,3,2,1,0:T(8,128)(2,1)}, u32[]{:S(2)}) copy-start(bf16[1,1,16,128,128]{4,3,2,1,0:T(8,128)(2,1)} %param.20) | copy-start | bytes 1572868
  7.2 4.6 %copy-start.9 = (s32[1,1,16]{2,1,0:T(1,128)S(1)}, s32[1,1,16]{2,1,0:T(1,128)}, u32[]{:S(2)}) copy-start(s32[1,1,16]{2,1,0:T(1,128)} %param.21) | copy-start | bytes 196
  7.2 114.6 %all-gather.2.cloned.1.call-start = ((), (), s32[]{:S(2)}) async-start(), calls=%async_computation.3 | async-start | bytes 8912896 | tf_op jit(solution)/shard_map/all_gather | solution.py:247
  13.8 2.3 copy-start.5
  30.2 6.3 %copy-start.6 = (s32[1,1,16,32]{3,2,1,0:T(8,128)S(1)}, s32[1,1,16,32]{3,2,1,0:T(8,128)}, u32[]{:S(2)}) copy-start(s32[1,1,16,32]{3,2,1,0:T(8,128)} %param.17) | copy-start | bytes 6148
  30.2 7.0 %copy-start.7 = (s32[1,1,16,32]{3,2,1,0:T(8,128)S(1)}, s32[1,1,16,32]{3,2,1,0:T(8,128)}, u32[]{:S(2)}) copy-start(s32[1,1,16,32]{3,2,1,0:T(8,128)} %param.18) | copy-start | bytes 6148
  30.2 7.6 %copy-start.8 = (s32[1024]{0:T(1024)S(1)}, s32[1024]{0:T(1024)}, u32[]{:S(2)}) copy-start(s32[1024]{0:T(1024)} %param.15) | copy-start | bytes 12292
  30.2 7.6 %copy-start.10 = (s32[8,1,16]{2,1,0:T(1,128)S(1)}, s32[8,1,16]{2,1,0:T(1,128)}, u32[]{:S(2)}) copy-start(s32[8,1,16]{2,1,0:T(1,128)} %param.23) | copy-start | bytes 1540
  30.2 55.9 %all-to-all-start = ((f32[8,4,128,256]{3,1,2,0:T(4,128)}), f32[8,4,128,256]{3,1,2,0:T(4,128)}, u32[]{:S(2)}, u32[]{:S(2)}) async-start(f32[8,4,128,256]{3,1,2,0:T(4,128)} %copy.57), calls=%async_computation | async-start | bytes 8388608 | tf_op jit(solution)/shard_map/all_to_all | solution.py:269
  36.5 293.5 %reduce-scatter.2.cloned.1.call-start = ((), (), s32[]{:S(2)}) async-start(), calls=%async_computation.4 | async-start | bytes 17825792 | tf_op jit(solution)/shard_map/reduce_scatter | solution.py:286
  147.4 1.7 copy-start.3
  180.1 1.0 copy-start.1
  221.2 110.3 %copy-start.4 = (bf16[256,256]{1,0:T(8,128)(2,1)S(1)}, bf16[256,256]{1,0:T(8,128)(2,1)}, u32[]{:S(2)}) copy-start(bf16[256,256]{1,0:T(8,128)(2,1)} %param.13) | copy-start | bytes 393220
  221.2 111.4 %copy-start.2 = (bf16[1024,256]{1,0:T(8,128)(2,1)S(1)}, bf16[1024,256]{1,0:T(8,128)(2,1)}, u32[]{:S(2)}) copy-start(bf16[1024,256]{1,0:T(8,128)(2,1)} %param.12) | copy-start | bytes 1572868
Sparse Core Ops, SparseCore 0:
  11.0 110.7 all-gather.1
  180.2 149.7 reduce-scatter.1

commit v4 on v3

--- a/solution.py
+++ b/solution.py
@@ -50,11 +50,11 @@
     grouped_slots(count_ref[c], slots, visit)
 
 
-def backward_kernel(rows_ref, cols_ref, count_ref, vals_ref, grad_ref, out_ref):
+def backward_kernel(rows_ref, cols_ref, count_ref, vals_ref, grad_ref, out_ref, acc_ref):
     c = pl.program_id(0)
     slots = vals_ref.shape[1]
     row_tiles = grad_ref.shape[0]
-    out_ref[...] = jnp.zeros_like(out_ref)
+    acc_ref[...] = jnp.zeros_like(acc_ref)
 
     def visit(terms):
         parts = []
@@ -66,9 +66,10 @@
             )
             parts.append((k, jnp.where(valid, prod, 0.0)))
         for k, prod in parts:
-            out_ref[0, k] += prod
+            acc_ref[k] += prod
 
     grouped_slots(count_ref[c], slots, visit)
+    out_ref[0] = acc_ref[...].astype(out_ref.dtype)
 
 
 def tile_forward(rows, cols, count, vals, panels):
@@ -105,16 +106,18 @@
             pl.BlockSpec((row_tiles, tile, width), lambda c, *_: (0, 0, 0)),
         ],
         out_specs=pl.BlockSpec((1, row_tiles, tile, width), lambda c, *_: (c, 0, 0, 0)),
+        scratch_shapes=[pltpu.VMEM((row_tiles, tile, width), jnp.float32)],
     )
     flops = 2 * n_src * slots * tile * tile * width
     return pl.pallas_call(
         backward_kernel,
-        out_shape=jax.ShapeDtypeStruct((n_src, row_tiles, tile, width), jnp.float32),
+        out_shape=jax.ShapeDtypeStruct((n_src, row_tiles, tile, width), jnp.bfloat16),
         grid_spec=grid_spec,
         cost_estimate=pl.CostEstimate(
-            flops=flops, transcendentals=0, bytes_accessed=vals.size * 2 + n_src * row_tiles * tile * width * 4
+            flops=flops, transcendentals=0, bytes_accessed=vals.size * 2 + n_src * row_tiles * tile * width * 2
         ),
     )(rows, cols, count, vals, grad_tiles)
+
 
 MESH_ID = pl.DeviceIdType.MESH
 
@@ -210,6 +213,55 @@
         compiler_params=pltpu.CompilerParams(collective_id=0, has_side_effects=True),
     )(x)
     return out.reshape(rows, cols)
+
+
+def exchange_kernel(n_blk, by_dest, src_ref, out_ref, send, recv, own):
+    g = lax.axis_index("grp")
+    b = lax.axis_index("blk")
+    barrier = pltpu.get_barrier_semaphore()
+    for i in range(1, n_blk):
+        pl.semaphore_signal(barrier, 1, device_id=(g, (b + i) % n_blk), device_id_type=MESH_ID)
+    pl.semaphore_wait(barrier, n_blk - 1)
+
+    def piece(to):
+        return src_ref.at[to] if by_dest else src_ref
+
+    def remote(to, slot):
+        return pltpu.make_async_remote_copy(
+            src_ref=piece(to), dst_ref=out_ref.at[slot], send_sem=send.at[to], recv_sem=recv.at[slot],
+            device_id=(g, to), device_id_type=MESH_ID,
+        )
+
+    local = pltpu.make_async_copy(piece(b), out_ref.at[b], own)
+    local.start()
+    sent = []
+    for i in range(1, n_blk):
+        cp = remote((b + i) % n_blk, b)
+        cp.start()
+        sent.append(cp)
+    for i in range(1, n_blk):
+        src = (b + n_blk - i) % n_blk
+        remote(src, src).wait_recv()
+    for cp in sent:
+        cp.wait_send()
+    local.wait()
+
+
+def exchange(src, n_blk, by_dest, collective):
+    shape = src.shape[1:] if by_dest else src.shape
+    any_space = pl.BlockSpec(memory_space=pl.ANY)
+    return pl.pallas_call(
+        functools.partial(exchange_kernel, n_blk, by_dest),
+        out_shape=jax.ShapeDtypeStruct((n_blk,) + shape, src.dtype),
+        in_specs=[any_space],
+        out_specs=any_space,
+        scratch_shapes=[
+            pltpu.SemaphoreType.DMA((n_blk,)),
+            pltpu.SemaphoreType.DMA((n_blk,)),
+            pltpu.SemaphoreType.DMA,
+        ],
+        compiler_params=pltpu.CompilerParams(collective_id=collective, has_side_effects=True),
+    )(src)
 
 
 def local(
@@ -244,8 +296,7 @@
     proj = jnp.dot(feats, weight, preferred_element_type=jnp.float32).astype(jnp.bfloat16)
     own_panel = proj.reshape(row_tiles, tile_size, width)
 
-    panels = lax.all_gather(proj, "blk", axis=0, tiled=True)
-    panels = panels.reshape(n_blocks, row_tiles, tile_size, width)
+    panels = exchange(own_panel, n_blocks, False, 1)
     agg_sum = tile_forward(dev_rows, dev_cols, dev_count, dev_vals, panels)
 
     dest_all = hub_dest[:, 0, :, 0]
@@ -283,7 +334,8 @@
     grad_tiles = grad_agg.reshape(row_tiles, tile_size, width)
 
     partials = tile_backward(dev_rows, dev_cols, dev_count, dev_vals, grad_tiles)
-    grad_sum = lax.psum_scatter(partials, "blk", scatter_dimension=0, tiled=True)[0]
+    received_parts = exchange(partials, n_blocks, True, 2)
+    grad_sum = jnp.sum(received_parts.astype(jnp.float32), axis=0)
 
     back_send = jnp.einsum(
         "scr,rif->scif",

time: 367 us -> 442 us (1.20)
  Pallas kernels: 78 us -> 375 us
  waiting for transfers between devices: 186 us -> 0.01 us
  blocking collectives: 32.7 us -> 0 us
  between operations: 14.3 us -> 0.89 us
  starting transfers between devices: 6.33 us -> 12.2 us
    pallas_call x0 -> x2, Pallas kernels: none -> 298 us  [exchange(): pl.pallas_call(functools.partial(exchange_kernel, n_blk, by_dest), out_sh...]
    reduce_scatter x1 -> x0, waiting for transfers between devices: 109 us -> none  [local(): lax.psum_scatter(partials, 'blk', scatter_dimension=0, tiled=True)[0]]
    all_to_all x1, waiting for transfers between devices: 48.1 us -> 0.01 us  [local(): lax.all_to_all(send_buf, 'grp', split_axis=0, concat_axis=0, tiled=True)]
    all_to_all x1 -> x0, blocking collectives: 32.7 us -> none  [local(): lax.all_to_all(back_send, 'grp', split_axis=0, concat_axis=0, tiled=True)]
    all_gather x1 -> x0, waiting for transfers between devices: 28.9 us -> none  [local(): panels = lax.all_gather(proj, 'blk', axis=0, tiled=True)]
    reduce_sum x0 -> x1, other arithmetic: none -> 5.99 us  [local(): grad_sum = jnp.sum(received_parts.astype(jnp.float32), axis=0)]
    all_to_all x0 -> x1, starting transfers between devices: none -> 5.98 us  [local(): lax.all_to_all(back_send, 'grp', split_axis=0, concat_axis=0, tiled=True)]
  transfers between devices with their start and end apart: 3 -> 2, of which waited for: 3 -> 0; matrix products, arithmetic and copies ran while one was open for 10% -> 2% of each run, Pallas kernels for 0% -> 80%
where the time goes in v4:
time: 442 us; the launch traced here: 441 us
  Pallas kernels  375 us (85%)
  matrix products  21.1 us (5%)
  local copies, waits for them, and re-layouts  21 us (5%)
  starting transfers between devices  12.2 us (3%)
  other arithmetic  10.3 us (2%)
    pallas_call x2, Pallas kernels, exchange(): pl.pallas_call(functools.partial(exchange_kernel, n_blk, by_dest), out_sh...  298 us
    pallas_call x1, Pallas kernels, tile_backward(): pl.pallas_call(backward_kernel, out_shape=jax.ShapeDtypeStruct((n_src, ro...  29.1 us
    pallas_call x1, Pallas kernels, tile_forward(): pl.pallas_call(forward_kernel, out_shape=jax.ShapeDtypeStruct((row_tiles,...  25.7 us
    pallas_call x1, Pallas kernels, weight_sum(): pl.pallas_call(functools.partial(weight_sum_kernel, n_grp, n_blk), out_sh...  22.4 us
    reshape x2, local copies, waits for them, and re-layouts, local(): send_buf = send_buf.reshape(n_groups, capacity, tile_size, width)  10.1 us
  transfers between devices with their start and end apart: 2, of which 0 were waited for; matrix products, arithmetic and copies ran while one was open for 2% of the time, Pallas kernels for 80%

profile of v4, /device:TPU:1, one launch (start us, length us, event | category | flops | bytes accessed | tf_op | source)
XLA Modules:
  0.0 440.6 jit_solution(5667455736761120445)
XLA Ops:
  0.6 0.7 compare_and_fusion
  1.4 0.7 fusion.40
  2.0 1.4 convolution_convert_fusion.2
  3.4 0.6 gather_fusion
  4.1 1.9 convolution_bitcast_fusion.1
  6.0 2.2 copy.44
  8.5 3.6 fusion.31
  12.1 5.2 %reshape.102 = f32[8,4,128,256]{3,1,0,2:T(4,128)} reshape(f32[32,128,256]{2,0,1:T(8,128)} %fusion.31) | data formatting | bytes 8388608 | tf_op jit(solution)/shard_map/reshape | solution.py:319
  17.3 4.9 %copy.45 = f32[8,4,128,256]{3,1,2,0:T(4,128)} copy(f32[8,4,128,256]{3,1,0,2:T(4,128)} %reshape.102) | data formatting | bytes 8388608 | tf_op jit(solution)/shard_map/reshape | solution.py:319
  22.2 6.2 %all-to-all-start = ((f32[8,4,128,256]{3,1,2,0:T(4,128)}), f32[8,4,128,256]{3,1,2,0:T(4,128)}, u32[]{:S(2)}, u32[]{:S(2)}) async-start(f32[8,4,128,256]{3,1,2,0:T(4,128)} %copy.45), calls=%async_computation | async-start | bytes 8388608 | tf_op jit(solution)/shard_map/all_to_all | solution.py:320
  28.5 155.5 %shard_map.139.panel_ref = bf16[16,8,128,256]{3,2,1,0:T(8,128)(2,1)} custom-call(bf16[8,128,256]{2,1,0:T(8,128)(2,1)} %bitcast.95), custom_call_target="tpu_custom_call" | custom-call | tf_op jit(solution)/shard_map/pallas_call | solution.py:253
  184.0 0.7 reshape_squeeze.6.rows_ref
  184.6 0.7 reshape_squeeze.7.cols_ref
  185.5 25.7 %shard_map.140 = f32[8,128,256]{2,1,0:T(8,128)} custom-call(s32[512]{0:T(512)} %reshape_squeeze.6.rows_ref, s32[512]{0:T(512)} %reshape_squeeze.7.cols_ref, s32[16]{0:T(128)} %bitcast.103, bf16[16,32,128,128]{3,2,1,0:T(8,128)(2,1)} %bitcast.92, bf16[16,8,128,256]{3,2,1,0:T(8,128)(2,1)} %shard_map.139.panel_ref), custom_call_target="tpu_custom_call" | custom-call | flops 4294967296 | bytes 25165824 | tf_op jit(solution)/shard_map/pallas_call | solution.py:88
  211.2 6.9 %convolution_bitcast_fusion.2 = f32[8,128,256]{2,0,1:T(8,128)S(1)} fusion(f32[8,4,128,256]{3,1,2,0:T(4,128)} %all-to-all-done, f32[8,4,8]{2,1,0:T(4,128)S(1)} %fusion.22), kind=kOutput, calls=%fused_computation.8 | convolution fusion | flops 100663296 | bytes 5243904 | tf_op jit(solution)/shard_map/scr,scif->rif/dot_general | solution.py:327
  218.5 0.6 copy-done.5
  219.2 1.3 fusion.13
  220.5 0.7 convolution_convert_fusion
  221.1 1.8 copy.50
  222.9 6.0 %all-to-all-start.1 = ((bf16[8,4,128,256]{3,2,1,0:T(8,128)(2,1)}), bf16[8,4,128,256]{3,2,1,0:T(8,128)(2,1)S(1)}, u32[]{:S(2)}, u32[]{:S(2)}) async-start(bf16[8,4,128,256]{3,2,1,0:T(8,128)(2,1)} %copy.50), calls=%async_computation.1 | async-start | bytes 4194304 | tf_op jit(solution)/shard_map/all_to_all | solution.py:346
  228.9 29.1 %shard_map.141.src_ref = bf16[16,8,128,256]{3,2,1,0:T(8,128)(2,1)} custom-call(s32[512]{0:T(512)} %reshape_squeeze.6.rows_ref, s32[512]{0:T(512)} %reshape_squeeze.7.cols_ref, s32[16]{0:T(128)} %bitcast.104, bf16[16,32,128,128]{3,2,1,0:T(8,128)(2,1)} %bitcast.93, bf16[8,128,256]{2,1,0:T(8,128)(2,1)} %bitcast.98), custom_call_target="tpu_custom_call" | custom-call | flops 4294967296 | bytes 25165824 | tf_op jit(solution)/shard_map/pallas_call | solution.py:112
  258.0 142.5 %shard_map.142 = bf16[16,8,128,256]{3,2,1,0:T(8,128)(2,1)} custom-call(bf16[16,8,128,256]{3,2,1,0:T(8,128)(2,1)} %shard_map.141.src_ref), custom_call_target="tpu_custom_call" | custom-call | tf_op jit(solution)/shard_map/pallas_call | solution.py:253
  400.5 6.0 %convert_reduce_fusion = f32[8,128,256]{2,1,0:T(8,128)} fusion(bf16[16,8,128,256]{3,2,1,0:T(8,128)(2,1)} %shard_map.142), kind=kLoop, calls=%fused_computation.1 | loop fusion | flops 8126464 | bytes 9437184 | tf_op jit(solution)/shard_map/reduce_sum | solution.py:338
  406.5 1.3 fusion.2
  407.7 0.6 convolution_bitcast_fusion
  408.3 2.1 copy.53
  410.4 3.2 fusion.5
  414.5 1.1 convolution_convert_fusion.1
  415.8 0.7 reshape.106.x_ref
  416.5 22.4 %shard_map.143 = f32[16,32,128]{2,1,0:T(8,128)} custom-call(f32[16,32,128]{2,1,0:T(8,128)} %reshape.106.x_ref), custom_call_target="tpu_custom_call" | custom-call | tf_op jit(solution)/shard_map/pallas_call | solution.py:200
  438.9 1.0 broadcast_multiply_fusion
  439.9 0.8 mul.60
  (39 shorter events, 1.9 us)
Async XLA Ops:
  0.6 3.4 copy-start
  3.4 2.5 copy-start.1
  6.0 2.3 copy-start.7
  22.2 189.0 %all-to-all-start = ((f32[8,4,128,256]{3,1,2,0:T(4,128)}), f32[8,4,128,256]{3,1,2,0:T(4,128)}, u32[]{:S(2)}, u32[]{:S(2)}) async-start(f32[8,4,128,256]{3,1,2,0:T(4,128)} %copy.45), calls=%async_computation | async-start | bytes 8388608 | tf_op jit(solution)/shard_map/all_to_all | solution.py:320
  28.4 155.5 %copy-start.8 = (s32[1,1,16,32]{3,2,1,0:T(8,128)S(1)}, s32[1,1,16,32]{3,2,1,0:T(8,128)}, u32[]{:S(2)}) copy-start(s32[1,1,16,32]{3,2,1,0:T(8,128)} %param.17) | copy-start | bytes 6148
  28.4 156.2 %copy-start.9 = (s32[1,1,16,32]{3,2,1,0:T(8,128)S(1)}, s32[1,1,16,32]{3,2,1,0:T(8,128)}, u32[]{:S(2)}) copy-start(s32[1,1,16,32]{3,2,1,0:T(8,128)} %param.18) | copy-start | bytes 6148
  28.5 156.9 %copy-start.10 = (s32[1024]{0:T(1024)S(1)}, s32[1024]{0:T(1024)}, u32[]{:S(2)}) copy-start(s32[1024]{0:T(1024)} %param.15) | copy-start | bytes 12292
  28.5 156.9 %copy-start.12 = (s32[8,1,16]{2,1,0:T(1,128)S(1)}, s32[8,1,16]{2,1,0:T(1,128)}, u32[]{:S(2)}) copy-start(s32[8,1,16]{2,1,0:T(1,128)} %param.23) | copy-start | bytes 1540
  211.2 6.9 %copy-start.3 = (f32[8,128,256]{2,1,0:T(8,128)S(1)}, f32[8,128,256]{2,1,0:T(8,128)}, u32[]{:S(2)}) copy-start(f32[8,128,256]{2,1,0:T(8,128)} %shard_map.140) | copy-start | bytes 3145732
  218.1 1.0 copy-start.5
  220.5 2.5 copy-start.2
  222.9 183.5 %all-to-all-start.1 = ((bf16[8,4,128,256]{3,2,1,0:T(8,128)(2,1)}), bf16[8,4,128,256]{3,2,1,0:T(8,128)(2,1)S(1)}, u32[]{:S(2)}, u32[]{:S(2)}) async-start(bf16[8,4,128,256]{3,2,1,0:T(8,128)(2,1)} %copy.50), calls=%async_computation.1 | async-start | bytes 4194304 | tf_op jit(solution)/shard_map/all_to_all | solution.py:346
  408.3 2.1 copy-start.11
  410.4 3.4 copy-start.4
  413.6 0.9 copy-start.6

commit v5 on v4

--- a/solution.py
+++ b/solution.py
@@ -296,7 +296,8 @@
     proj = jnp.dot(feats, weight, preferred_element_type=jnp.float32).astype(jnp.bfloat16)
     own_panel = proj.reshape(row_tiles, tile_size, width)
 
-    panels = exchange(own_panel, n_blocks, False, 1)
+    panels = lax.all_gather(proj, "blk", axis=0, tiled=True)
+    panels = panels.reshape(n_blocks, row_tiles, tile_size, width)
     agg_sum = tile_forward(dev_rows, dev_cols, dev_count, dev_vals, panels)
 
     dest_all = hub_dest[:, 0, :, 0]
@@ -334,7 +335,7 @@
     grad_tiles = grad_agg.reshape(row_tiles, tile_size, width)
 
     partials = tile_backward(dev_rows, dev_cols, dev_count, dev_vals, grad_tiles)
-    received_parts = exchange(partials, n_blocks, True, 2)
+    received_parts = lax.all_to_all(partials, "blk", split_axis=0, concat_axis=0, tiled=True)
     grad_sum = jnp.sum(received_parts.astype(jnp.float32), axis=0)
 
     back_send = jnp.einsum(

time: 442 us -> 355 us (0.80)
  Pallas kernels: 375 us -> 88.1 us
  waiting for transfers between devices: 0.01 us -> 185 us
  between operations: 0.89 us -> 14.3 us
    pallas_call x2 -> x0, Pallas kernels: 298 us -> none  [exchange(): pl.pallas_call(functools.partial(exchange_kernel, n_blk, by_dest), out_sh...]
    all_to_all x0 -> x1, waiting for transfers between devices: none -> 108 us  [local(): lax.all_to_all(partials, 'blk', split_axis=0, concat_axis=0, tiled=True)]
    all_to_all x1, waiting for transfers between devices: 0.01 us -> 48.1 us  [local(): lax.all_to_all(send_buf, 'grp', split_axis=0, concat_axis=0, tiled=True)]
    all_gather x0 -> x1, waiting for transfers between devices: none -> 28.9 us  [local(): panels = lax.all_gather(proj, 'blk', axis=0, tiled=True)]
    all_to_all x0 -> x1, starting transfers between devices: none -> 4.99 us  [local(): lax.all_to_all(partials, 'blk', split_axis=0, concat_axis=0, tiled=True)]
    pallas_call x1, Pallas kernels: 22.4 us -> 27.2 us  [weight_sum(): pl.pallas_call(functools.partial(weight_sum_kernel, n_grp, n_blk), out_sh...]
  transfers between devices with their start and end apart: 2 -> 4, of which waited for: 0 -> 3; matrix products, arithmetic and copies ran while one was open for 2% -> 9% of each run, Pallas kernels for 80% -> 9%
where the time goes in v5:
time: 355 us; the launch traced here: 354 us
  waiting for transfers between devices  185 us (52%)
  Pallas kernels  88.1 us (25%)
  local copies, waits for them, and re-layouts  21.6 us (6%)
  matrix products  20 us (6%)
  starting transfers between devices  14.9 us (4%)
  between operations  14.3 us (4%)
  other arithmetic  9.94 us (3%)
    all_to_all x1, waiting for transfers between devices, local(): lax.all_to_all(partials, 'blk', split_axis=0, concat_axis=0, tiled=True)  108 us
    all_to_all x1, waiting for transfers between devices, local(): lax.all_to_all(send_buf, 'grp', split_axis=0, concat_axis=0, tiled=True)  48.1 us
    pallas_call x1, Pallas kernels, tile_backward(): pl.pallas_call(backward_kernel, out_shape=jax.ShapeDtypeStruct((n_src, ro...  32.5 us
    all_gather x1, waiting for transfers between devices, local(): panels = lax.all_gather(proj, 'blk', axis=0, tiled=True)  28.9 us
    pallas_call x1, Pallas kernels, tile_forward(): pl.pallas_call(forward_kernel, out_shape=jax.ShapeDtypeStruct((row_tiles,...  28.5 us
    pallas_call x1, Pallas kernels, weight_sum(): pl.pallas_call(functools.partial(weight_sum_kernel, n_grp, n_blk), out_sh...  27.2 us
    reshape x2, local copies, waits for them, and re-layouts, local(): send_buf = send_buf.reshape(n_groups, capacity, tile_size, width)  10.3 us
  transfers between devices with their start and end apart: 4, of which 3 were waited for; matrix products, arithmetic and copies ran while one was open for 9% of the time, Pallas kernels for 9%

profile of v5, /device:TPU:1, one launch (start us, length us, event | category | flops | bytes accessed | tf_op | source)
XLA Modules:
  0.0 354.1 jit_solution(162381058032172688)
XLA Ops:
  7.2 2.2 convolution_convert_fusion.2
  9.5 0.7 fusion.40
  10.1 1.7 gather_fusion
  11.8 1.9 convolution_bitcast_fusion.1
  13.8 2.2 copy.57
  16.3 3.6 %fusion.31 = f32[32,128,256]{2,0,1:T(8,128)} fusion(f32[16,128,256]{2,0,1:T(8,128)S(1)} %copy.57, s32[16]{0:T(128)S(1)} %bitcast_add_fusion), kind=kOutput, calls=%fused_computation.51 | convolution fusion | flops 201327104 | bytes 6291520 | tf_op jit(solution)/shard_map/hs,hif->sif/dot_general | solution.py:319
  19.9 5.2 %reshape.106 = f32[8,4,128,256]{3,1,0,2:T(4,128)} reshape(f32[32,128,256]{2,0,1:T(8,128)} %fusion.31) | data formatting | bytes 8388608 | tf_op jit(solution)/shard_map/reshape | solution.py:320
  25.1 5.1 %copy.58 = f32[8,4,128,256]{3,1,2,0:T(4,128)} copy(f32[8,4,128,256]{3,1,0,2:T(4,128)} %reshape.106) | data formatting | bytes 8388608 | tf_op jit(solution)/shard_map/reshape | solution.py:320
  30.2 6.3 %all-to-all-start = ((f32[8,4,128,256]{3,1,2,0:T(4,128)}), f32[8,4,128,256]{3,1,2,0:T(4,128)}, u32[]{:S(2)}, u32[]{:S(2)}) async-start(f32[8,4,128,256]{3,1,2,0:T(4,128)} %copy.58), calls=%async_computation | async-start | bytes 8388608 | tf_op jit(solution)/shard_map/all_to_all | solution.py:321
  36.5 0.7 reshape_squeeze.6.rows_ref
  37.1 0.7 reshape_squeeze.7.cols_ref
  38.0 48.1 %all-to-all-done = f32[8,4,128,256]{3,1,2,0:T(4,128)} async-done(((f32[8,4,128,256]{3,1,2,0:T(4,128)}), f32[8,4,128,256]{3,1,2,0:T(4,128)}, u32[]{:S(2)}, u32[]{:S(2)}) %all-to-all-start) | async-done | bytes 4194336 | tf_op jit(solution)/shard_map/all_to_all | solution.py:321
  86.1 6.8 %convolution_bitcast_fusion.2 = f32[8,128,256]{2,0,1:T(8,128)S(1)} fusion(f32[8,4,128,256]{3,1,2,0:T(4,128)} %all-to-all-done, f32[8,4,8]{2,1,0:T(4,128)S(1)} %fusion.22), kind=kOutput, calls=%fused_computation.8 | convolution fusion | flops 100663296 | bytes 5243904 | tf_op jit(solution)/shard_map/scr,scif->rif/dot_general | solution.py:328
  92.9 28.9 %all-gather.2.cloned.1.call-done = bf16[16384,256]{1,0:T(8,128)(2,1)} async-done(((bf16[1024,256]{1,0:T(8,128)(2,1)}), bf16[16384,256]{1,0:T(8,128)(2,1)}) %all-gather.2.cloned.1.call-update) | async-done | bytes 8388624 | tf_op jit(solution)/shard_map/all_gather | solution.py:299
  121.8 28.5 %shard_map.139 = f32[8,128,256]{2,1,0:T(8,128)} custom-call(s32[512]{0:T(512)} %reshape_squeeze.6.rows_ref, s32[512]{0:T(512)} %reshape_squeeze.7.cols_ref, s32[16]{0:T(128)} %bitcast.104, bf16[16,32,128,128]{3,2,1,0:T(8,128)(2,1)} %bitcast.93, bf16[16,8,128,256]{3,2,1,0:T(8,128)(2,1)} %bitcast.96), custom_call_target="tpu_custom_call" | custom-call | flops 4294967296 | bytes 25165824 | tf_op jit(solution)/shard_map/pallas_call | solution.py:88
  150.3 1.7 copy_add_fusion
  152.0 1.3 fusion.13
  153.3 0.7 convolution_convert_fusion
  154.0 1.8 copy.63
  155.8 3.6 %all-to-all-start.2 = ((bf16[8,4,128,256]{3,2,1,0:T(8,128)(2,1)}), bf16[8,4,128,256]{3,2,1,0:T(8,128)(2,1)S(1)}, u32[]{:S(2)}, u32[]{:S(2)}) async-start(bf16[8,4,128,256]{3,2,1,0:T(8,128)(2,1)} %copy.63), calls=%async_computation.2 | async-start | bytes 4194304 | tf_op jit(solution)/shard_map/all_to_all | solution.py:347
  159.4 32.5 %shard_map.140 = bf16[16,8,128,256]{3,2,1,0:T(8,128)(2,1)} custom-call(s32[512]{0:T(512)} %reshape_squeeze.6.rows_ref, s32[512]{0:T(512)} %reshape_squeeze.7.cols_ref, s32[16]{0:T(128)} %bitcast.105, bf16[16,32,128,128]{3,2,1,0:T(8,128)(2,1)} %bitcast.94, bf16[8,128,256]{2,1,0:T(8,128)(2,1)} %bitcast.99), custom_call_target="tpu_custom_call" | custom-call | flops 4294967296 | bytes 25165824 | tf_op jit(solution)/shard_map/pallas_call | solution.py:112
  191.9 5.0 %all-to-all-start.1 = ((bf16[16,8,128,256]{3,2,1,0:T(8,128)(2,1)}), bf16[16,8,128,256]{3,2,1,0:T(8,128)(2,1)}, u32[]{:S(2)}, u32[]{:S(2)}) async-start(bf16[16,8,128,256]{3,2,1,0:T(8,128)(2,1)} %shard_map.140), calls=%async_computation.1 | async-start | bytes 16777216 | tf_op jit(solution)/shard_map/all_to_all | solution.py:338
  196.9 1.3 fusion.2
  198.7 2.1 copy.66
  200.8 108.3 %all-to-all-done.1 = bf16[16,8,128,256]{3,2,1,0:T(8,128)(2,1)} async-done(((bf16[16,8,128,256]{3,2,1,0:T(8,128)(2,1)}), bf16[16,8,128,256]{3,2,1,0:T(8,128)(2,1)}, u32[]{:S(2)}, u32[]{:S(2)}) %all-to-all-start.1) | async-done | bytes 8388640 | tf_op jit(solution)/shard_map/all_to_all | solution.py:338
  309.0 5.0 %convert_reduce_fusion = f32[8,128,256]{2,1,0:T(8,128)S(1)} fusion(bf16[16,8,128,256]{3,2,1,0:T(8,128)(2,1)} %all-to-all-done.1), kind=kLoop, calls=%fused_computation.1 | loop fusion | flops 8126464 | bytes 9437184 | tf_op jit(solution)/shard_map/reduce_sum | solution.py:339
  314.1 1.4 fusion.5
  316.4 1.1 convolution_convert_fusion.1
  317.6 0.7 reshape.110.x_ref
  318.4 27.2 %shard_map.141 = f32[16,32,128]{2,1,0:T(8,128)} custom-call(f32[16,32,128]{2,1,0:T(8,128)} %reshape.110.x_ref), custom_call_target="tpu_custom_call" | custom-call | tf_op jit(solution)/shard_map/pallas_call | solution.py:200
  345.5 1.0 broadcast_multiply_fusion
  346.5 0.8 mul.60
  (40 shorter events, 2.1 us)
Async XLA Ops:
  7.2 4.7 %copy-start = (bf16[1,1,16,128,128]{4,3,2,1,0:T(8,128)(2,1)S(1)}, bf16[1,1,16,128,128]{4,3,2,1,0:T(8,128)(2,1)}, u32[]{:S(2)}) copy-start(bf16[1,1,16,128,128]{4,3,2,1,0:T(8,128)(2,1)} %param.20) | copy-start | bytes 1572868
  7.2 4.6 %copy-start.10 = (s32[1,1,16]{2,1,0:T(1,128)S(1)}, s32[1,1,16]{2,1,0:T(1,128)}, u32[]{:S(2)}) copy-start(s32[1,1,16]{2,1,0:T(1,128)} %param.21) | copy-start | bytes 196
  7.2 114.6 %all-gather.2.cloned.1.call-start = ((), (), s32[]{:S(2)}) async-start(), calls=%async_computation.3 | async-start | bytes 8912896 | tf_op jit(solution)/shard_map/all_gather | solution.py:299
  13.8 2.3 copy-start.6
  30.2 6.3 %copy-start.7 = (s32[1,1,16,32]{3,2,1,0:T(8,128)S(1)}, s32[1,1,16,32]{3,2,1,0:T(8,128)}, u32[]{:S(2)}) copy-start(s32[1,1,16,32]{3,2,1,0:T(8,128)} %param.17) | copy-start | bytes 6148
  30.2 6.9 %copy-start.8 = (s32[1,1,16,32]{3,2,1,0:T(8,128)S(1)}, s32[1,1,16,32]{3,2,1,0:T(8,128)}, u32[]{:S(2)}) copy-start(s32[1,1,16,32]{3,2,1,0:T(8,128)} %param.18) | copy-start | bytes 6148
  30.2 7.6 %copy-start.9 = (s32[1024]{0:T(1024)S(1)}, s32[1024]{0:T(1024)}, u32[]{:S(2)}) copy-start(s32[1024]{0:T(1024)} %param.15) | copy-start | bytes 12292
  30.2 7.6 %copy-start.11 = (s32[8,1,16]{2,1,0:T(1,128)S(1)}, s32[8,1,16]{2,1,0:T(1,128)}, u32[]{:S(2)}) copy-start(s32[8,1,16]{2,1,0:T(1,128)} %param.23) | copy-start | bytes 1540
  30.2 55.9 %all-to-all-start = ((f32[8,4,128,256]{3,1,2,0:T(4,128)}), f32[8,4,128,256]{3,1,2,0:T(4,128)}, u32[]{:S(2)}, u32[]{:S(2)}) async-start(f32[8,4,128,256]{3,1,2,0:T(4,128)} %copy.58), calls=%async_computation | async-start | bytes 8388608 | tf_op jit(solution)/shard_map/all_to_all | solution.py:321
  150.3 1.7 copy-start.4
  153.3 2.5 copy-start.2
  155.8 36.1 %all-to-all-start.2 = ((bf16[8,4,128,256]{3,2,1,0:T(8,128)(2,1)}), bf16[8,4,128,256]{3,2,1,0:T(8,128)(2,1)S(1)}, u32[]{:S(2)}, u32[]{:S(2)}) async-start(bf16[8,4,128,256]{3,2,1,0:T(8,128)(2,1)} %copy.63), calls=%async_computation.2 | async-start | bytes 4194304 | tf_op jit(solution)/shard_map/all_to_all | solution.py:347
  191.9 117.2 %all-to-all-start.1 = ((bf16[16,8,128,256]{3,2,1,0:T(8,128)(2,1)}), bf16[16,8,128,256]{3,2,1,0:T(8,128)(2,1)}, u32[]{:S(2)}, u32[]{:S(2)}) async-start(bf16[16,8,128,256]{3,2,1,0:T(8,128)(2,1)} %shard_map.140), calls=%async_computation.1 | async-start | bytes 16777216 | tf_op jit(solution)/shard_map/all_to_all | solution.py:338
  200.8 113.3 %copy-start.1 = (f32[16,128,256]{2,0,1:T(8,128)S(1)}, f32[16,128,256]{2,0,1:T(8,128)}, u32[]{:S(2)}) copy-start(f32[16,128,256]{2,0,1:T(8,128)} %copy.66) | copy-start | bytes 6291460
  314.1 1.5 copy-start.3
  315.5 0.9 copy-start.5
Sparse Core Ops, SparseCore 0:
  11.0 110.7 all-gather.1

commit v6 on v4

--- a/solution.py
+++ b/solution.py
@@ -50,7 +50,7 @@
     grouped_slots(count_ref[c], slots, visit)
 
 
-def backward_kernel(rows_ref, cols_ref, count_ref, vals_ref, grad_ref, out_ref, acc_ref):
+def backward_kernel(rows_ref, cols_ref, count_ref, core_ref, vals_ref, grad_ref, out_ref, acc_ref):
     c = pl.program_id(0)
     slots = vals_ref.shape[1]
     row_tiles = grad_ref.shape[0]
@@ -69,7 +69,7 @@
             acc_ref[k] += prod
 
     grouped_slots(count_ref[c], slots, visit)
-    out_ref[0] = acc_ref[...].astype(out_ref.dtype)
+    out_ref[0, 0] = acc_ref[...].astype(out_ref.dtype)
 
 
 def tile_forward(rows, cols, count, vals, panels):
@@ -95,28 +95,30 @@
     )(rows, cols, count, vals, panels)
 
 
-def tile_backward(rows, cols, count, vals, grad_tiles):
+def tile_backward(rows, cols, count, vals, grad_tiles, core):
     n_src, slots, tile, _ = vals.shape
     row_tiles, width = grad_tiles.shape[0], grad_tiles.shape[2]
     grid_spec = pltpu.PrefetchScalarGridSpec(
-        num_scalar_prefetch=3,
+        num_scalar_prefetch=4,
         grid=(n_src,),
         in_specs=[
             pl.BlockSpec((1, slots, tile, tile), lambda c, *_: (c, 0, 0, 0)),
             pl.BlockSpec((row_tiles, tile, width), lambda c, *_: (0, 0, 0)),
         ],
-        out_specs=pl.BlockSpec((1, row_tiles, tile, width), lambda c, *_: (c, 0, 0, 0)),
+        out_specs=pl.BlockSpec(
+            (1, 1, row_tiles, tile, width), lambda c, r, k, n, core_ref: ((c + core_ref[0]) % 2, c // 2, 0, 0, 0)
+        ),
         scratch_shapes=[pltpu.VMEM((row_tiles, tile, width), jnp.float32)],
     )
     flops = 2 * n_src * slots * tile * tile * width
     return pl.pallas_call(
         backward_kernel,
-        out_shape=jax.ShapeDtypeStruct((n_src, row_tiles, tile, width), jnp.bfloat16),
+        out_shape=jax.ShapeDtypeStruct((2, n_src // 2, row_tiles, tile, width), jnp.float32),
         grid_spec=grid_spec,
         cost_estimate=pl.CostEstimate(
-            flops=flops, transcendentals=0, bytes_accessed=vals.size * 2 + n_src * row_tiles * tile * width * 2
+            flops=flops, transcendentals=0, bytes_accessed=vals.size * 2 + n_src * row_tiles * tile * width * 4
         ),
-    )(rows, cols, count, vals, grad_tiles)
+    )(rows, cols, count, core, vals, grad_tiles)
 
 
 MESH_ID = pl.DeviceIdType.MESH
@@ -296,7 +298,13 @@
     proj = jnp.dot(feats, weight, preferred_element_type=jnp.float32).astype(jnp.bfloat16)
     own_panel = proj.reshape(row_tiles, tile_size, width)
 
-    panels = exchange(own_panel, n_blocks, False, 1)
+    core = lax.axis_index("blk") % 2
+    core_groups = [[i for i in range(n_blocks) if i % 2 == k] for k in range(2)]
+    sibling = [(i, i ^ 1) for i in range(n_blocks)]
+    half = lax.all_gather(own_panel, "blk", axis=0, tiled=False, axis_index_groups=core_groups)
+    other = lax.ppermute(half, "blk", sibling)
+    pair = jnp.where(core == 0, jnp.stack([half, other], 1), jnp.stack([other, half], 1))
+    panels = pair.reshape(n_blocks, row_tiles, tile_size, width)
     agg_sum = tile_forward(dev_rows, dev_cols, dev_count, dev_vals, panels)
 
     dest_all = hub_dest[:, 0, :, 0]
@@ -333,8 +341,12 @@
     grad_agg = (cotangent.astype(jnp.float32) * keep * slope).astype(jnp.bfloat16)
     grad_tiles = grad_agg.reshape(row_tiles, tile_size, width)
 
-    partials = tile_backward(dev_rows, dev_cols, dev_count, dev_vals, grad_tiles)
-    received_parts = exchange(partials, n_blocks, True, 2)
+    partials = tile_backward(dev_rows, dev_cols, dev_count, dev_vals, grad_tiles, core.reshape(1))
+    from_sibling = lax.ppermute(partials[1], "blk", sibling)
+    pair_sum = (partials[0] + from_sibling).astype(jnp.bfloat16)
+    received_parts = lax.all_to_all(
+        pair_sum, "blk", split_axis=0, concat_axis=0, tiled=True, axis_index_groups=core_groups
+    )
     grad_sum = jnp.sum(received_parts.astype(jnp.float32), axis=0)
 
     back_send = jnp.einsum(

time: 442 us -> 412 us (0.932)
  Pallas kernels: 375 us -> 96.9 us
  waiting for transfers between devices: 0.01 us -> 182 us
  starting transfers between devices: 12.2 us -> 34.6 us
  other arithmetic: 10.3 us -> 26 us
  local copies, waits for them, and re-layouts: 21 us -> 36.4 us
  between operations: 0.89 us -> 14.3 us
    pallas_call x3 -> x1, Pallas kernels: 327 us -> 31.3 us  [tile_backward(): pl.pallas_call(backward_kernel, out_shape=jax.ShapeDtypeStruct((2, n_src...]
    all_gather x0 -> x1, waiting for transfers between devices: none -> 68.4 us  [local(): lax.all_gather(own_panel, 'blk', axis=0, tiled=False, axis_index_groups=c...]
    all_to_all x1, waiting for transfers between devices: 0.01 us -> 48.1 us  [local(): lax.all_to_all(send_buf, 'grp', split_axis=0, concat_axis=0, tiled=True)]
    all_to_all x0 -> x1, waiting for transfers between devices: none -> 47.1 us  [local(): lax.all_to_all(pair_sum, 'blk', split_axis=0, concat_axis=0, tiled=True,...]
    all_to_all x1, waiting for transfers between devices: 0.01 us -> 17.9 us  [local(): lax.all_to_all(back_send, 'grp', split_axis=0, concat_axis=0, tiled=True)]
    pallas_call x1, Pallas kernels: 22.4 us -> 39.3 us  [weight_sum(): pl.pallas_call(functools.partial(weight_sum_kernel, n_grp, n_blk), out_sh...]
    all_to_all x1, starting transfers between devices: 5.98 us -> 22.4 us  [local(): lax.all_to_all(back_send, 'grp', split_axis=0, concat_axis=0, tiled=True)]
    convert_element_type x0 -> x1, other arithmetic: none -> 9.21 us  [local(): pair_sum = (partials[0] + from_sibling).astype(jnp.bfloat16)]
  transfers between devices with their start and end apart: 2 -> 6, of which waited for: 0 -> 4; matrix products, arithmetic and copies ran while one was open for 2% -> 11% of each run, Pallas kernels for 80% -> 0%
where the time goes in v6:
time: 412 us; the launch traced here: 410 us
  waiting for transfers between devices  182 us (44%)
  Pallas kernels  96.9 us (24%)
  local copies, waits for them, and re-layouts  36.4 us (9%)
  starting transfers between devices  34.6 us (8%)
  other arithmetic  26 us (6%)
  matrix products  20.1 us (5%)
  between operations  14.3 us (3%)
    all_gather x1, waiting for transfers between devices, local(): lax.all_gather(own_panel, 'blk', axis=0, tiled=False, axis_index_groups=c...  68.4 us
    all_to_all x1, waiting for transfers between devices, local(): lax.all_to_all(send_buf, 'grp', split_axis=0, concat_axis=0, tiled=True)  48.1 us
    all_to_all x1, waiting for transfers between devices, local(): lax.all_to_all(pair_sum, 'blk', split_axis=0, concat_axis=0, tiled=True,...  47.1 us
    pallas_call x1, Pallas kernels, weight_sum(): pl.pallas_call(functools.partial(weight_sum_kernel, n_grp, n_blk), out_sh...  39.3 us
    pallas_call x1, Pallas kernels, tile_backward(): pl.pallas_call(backward_kernel, out_shape=jax.ShapeDtypeStruct((2, n_src...  31.3 us
    pallas_call x1, Pallas kernels, tile_forward(): pl.pallas_call(forward_kernel, out_shape=jax.ShapeDtypeStruct((row_tiles,...  26.3 us
    all_to_all x1, starting transfers between devices, local(): lax.all_to_all(back_send, 'grp', split_axis=0, concat_axis=0, tiled=True)  22.4 us
    all_to_all x1, waiting for transfers between devices, local(): lax.all_to_all(back_send, 'grp', split_axis=0, concat_axis=0, tiled=True)  17.9 us
  transfers between devices with their start and end apart: 6, of which 4 were waited for; matrix products, arithmetic and copies ran while one was open for 11% of the time, Pallas kernels for 0%

profile of v6, /device:TPU:1, one launch (start us, length us, event | category | flops | bytes accessed | tf_op | source)
XLA Modules:
  0.0 410.0 jit_solution(16780497967974313740)
XLA Ops:
  7.2 2.2 convolution_convert_fusion.2
  10.1 1.7 gather_fusion
  12.5 1.9 convolution_bitcast_fusion.1
  14.4 2.2 copy.60
  17.0 68.4 %all-gather.2.cloned.1.call-done = bf16[8,8,128,256]{3,2,1,0:T(8,128)(2,1)} async-done(((bf16[1,8,128,256]{3,2,1,0:T(8,128)(2,1)}), bf16[8,8,128,256]{3,2,1,0:T(8,128)(2,1)}) %all-gather.2.cloned.1.call-update) | async-done | bytes 4194320 | tf_op jit(solution)/shard_map/all_gather | solution.py:304
  85.4 1.1 collective-permute-start
  86.5 3.6 fusion.33
  90.1 5.2 %reshape.110 = f32[8,4,128,256]{3,1,0,2:T(4,128)} reshape(f32[32,128,256]{2,0,1:T(8,128)} %fusion.33) | data formatting | bytes 8388608 | tf_op jit(solution)/shard_map/reshape | solution.py:327
  95.3 4.9 %copy.61 = f32[8,4,128,256]{3,1,2,0:T(4,128)} copy(f32[8,4,128,256]{3,1,0,2:T(4,128)} %reshape.110) | data formatting | bytes 8388608 | tf_op jit(solution)/shard_map/reshape | solution.py:327
  100.2 4.7 %all-to-all-start = ((f32[8,4,128,256]{3,1,2,0:T(4,128)}), f32[8,4,128,256]{3,1,2,0:T(4,128)}, u32[]{:S(2)}, u32[]{:S(2)}) async-start(f32[8,4,128,256]{3,1,2,0:T(4,128)} %copy.61), calls=%async_computation | async-start | bytes 8388608 | tf_op jit(solution)/shard_map/all_to_all | solution.py:328
  106.5 48.1 %all-to-all-done = f32[8,4,128,256]{3,1,2,0:T(4,128)} async-done(((f32[8,4,128,256]{3,1,2,0:T(4,128)}), f32[8,4,128,256]{3,1,2,0:T(4,128)}, u32[]{:S(2)}, u32[]{:S(2)}) %all-to-all-start) | async-done | bytes 4194336 | tf_op jit(solution)/shard_map/all_to_all | solution.py:328
  154.6 7.0 %convolution_bitcast_fusion.2 = f32[8,128,256]{2,0,1:T(8,128)S(1)} fusion(f32[8,4,128,256]{3,1,2,0:T(4,128)} %all-to-all-done, f32[8,4,8]{2,1,0:T(4,128)S(1)} %fusion.24), kind=kOutput, calls=%fused_computation.13 | convolution fusion | flops 100663296 | bytes 5243904 | tf_op jit(solution)/shard_map/scr,scif->rif/dot_general | solution.py:335
  161.6 8.1 %maximum_select_fusion = bf16[8,2,8,128,256]{4,3,2,0,1:T(8,128)(2,1)} fusion(bf16[8,1,8,128,256]{4,3,2,0,1:T(8,128)(2,1)} %bitcast.4, bf16[8,1,8,128,256]{4,3,2,0,1:T(8,128)(2,1)S(1)} %bitcast.117, pred[]{:T(512)S(6)} %eq.84), kind=kLoop, calls=%fused_computation.5 | loop fusion | flops 12582912 | bytes 16777216 | tf_op jit(solution)/shard_map/jit(_where)/select_n | solution.py:306
  169.7 7.7 %copy.58 = bf16[8,2,8,128,256]{4,3,2,1,0:T(8,128)(2,1)} copy(bf16[8,2,8,128,256]{4,3,2,0,1:T(8,128)(2,1)} %maximum_select_fusion) | data formatting | bytes 16777216 | tf_op jit(solution)/shard_map/jit(_where)/select_n | solution.py:306
  177.5 26.3 %shard_map.139 = f32[8,128,256]{2,1,0:T(8,128)} custom-call(s32[512]{0:T(512)} %reshape_squeeze.6.rows_ref, s32[512]{0:T(512)} %reshape_squeeze.7.cols_ref, s32[16]{0:T(128)} %bitcast.120, bf16[16,32,128,128]{3,2,1,0:T(8,128)(2,1)} %bitcast.107, bf16[16,8,128,256]{3,2,1,0:T(8,128)(2,1)} %bitcast.109), custom_call_target="tpu_custom_call" | custom-call | flops 4294967296 | bytes 25165824 | tf_op jit(solution)/shard_map/pallas_call | solution.py:88
  203.7 1.6 copy_add_fusion.1
  205.4 1.4 fusion.14
  206.8 31.3 %shard_map.140 = f32[2,8,8,128,256]{4,3,2,1,0:T(8,128)} custom-call(s32[512]{0:T(512)} %reshape_squeeze.6.rows_ref, s32[512]{0:T(512)} %reshape_squeeze.7.cols_ref, s32[16]{0:T(128)} %bitcast.121, s32[1]{0:T(128)} %bitcast.21.core_ref, bf16[16,32,128,128]{3,2,1,0:T(8,128)(2,1)} %bitcast.108, bf16[8,128,256]{2,1,0:T(8,128)(2,1)} %bitcast.113), custom_call_target="tpu_custom_call" | custom-call | flops 4294967296 | bytes 33554432 | tf_op jit(solution)/shard_map/pallas_call | solution.py:114
  238.1 7.7 %slice_bitcast_fusion = f32[8,8,128,256]{3,2,1,0:T(8,128)} fusion(f32[2,8,8,128,256]{4,3,2,1,0:T(8,128)} %shard_map.140), kind=kLoop, calls=%fused_computation.1 | loop fusion | bytes 16777216 | tf_op jit(solution)/shard_map/squeeze | solution.py:345
  245.8 1.8 collective-permute-start.1
  248.3 1.8 copy.66
  250.1 22.4 %all-to-all-start.2 = ((bf16[8,4,128,256]{3,2,1,0:T(8,128)(2,1)}), bf16[8,4,128,256]{3,2,1,0:T(8,128)(2,1)S(1)}, u32[]{:S(2)}, u32[]{:S(2)}) async-start(bf16[8,4,128,256]{3,2,1,0:T(8,128)(2,1)} %copy.66), calls=%async_computation.2 | async-start | bytes 4194304 | tf_op jit(solution)/shard_map/all_to_all | solution.py:358
  272.5 9.2 %fusion.1 = bf16[8,8,128,256]{3,2,1,0:T(8,128)(2,1)} fusion(f32[8,8,128,256]{3,2,1,0:T(8,128)} %collective-permute-done.1, f32[2,8,8,128,256]{4,3,2,1,0:T(8,128)} %shard_map.140), kind=kLoop, calls=%fused_computation.4 | loop fusion | flops 4194304 | bytes 20971520 | tf_op jit(solution)/shard_map/convert_element_type | solution.py:346
  281.7 17.9 %all-to-all-done.2 = bf16[8,4,128,256]{3,2,1,0:T(8,128)(2,1)S(1)} async-done(((bf16[8,4,128,256]{3,2,1,0:T(8,128)(2,1)}), bf16[8,4,128,256]{3,2,1,0:T(8,128)(2,1)S(1)}, u32[]{:S(2)}, u32[]{:S(2)}) %all-to-all-start.2) | async-done | bytes 2097184 | tf_op jit(solution)/shard_map/all_to_all | solution.py:358
  299.6 4.6 %all-to-all-start.1 = ((bf16[8,8,128,256]{3,2,1,0:T(8,128)(2,1)}), bf16[8,8,128,256]{3,2,1,0:T(8,128)(2,1)}, u32[]{:S(2)}, u32[]{:S(2)}) async-start(bf16[8,8,128,256]{3,2,1,0:T(8,128)(2,1)} %fusion.1), calls=%async_computation.1 | async-start | bytes 8388608 | tf_op jit(solution)/shard_map/all_to_all | solution.py:347
  304.2 1.3 fusion.4
  306.0 2.1 copy.69
  308.1 47.1 %all-to-all-done.1 = bf16[8,8,128,256]{3,2,1,0:T(8,128)(2,1)} async-done(((bf16[8,8,128,256]{3,2,1,0:T(8,128)(2,1)}), bf16[8,8,128,256]{3,2,1,0:T(8,128)(2,1)}, u32[]{:S(2)}, u32[]{:S(2)}) %all-to-all-start.1) | async-done | bytes 4194336 | tf_op jit(solution)/shard_map/all_to_all | solution.py:347
  355.2 3.0 convert_reduce_fusion
  358.3 1.3 fusion.15
  359.7 1.1 convolution_convert_fusion.1
  362.1 39.3 %shard_map.141 = f32[16,32,128]{2,1,0:T(8,128)} custom-call(f32[16,32,128]{2,1,0:T(8,128)} %reshape.115.x_ref), custom_call_target="tpu_custom_call" | custom-call | tf_op jit(solution)/shard_map/pallas_call | solution.py:202
  (50 shorter events, 7.5 us)
Async XLA Ops:
  7.2 5.3 %copy-start = (bf16[1,1,16,128,128]{4,3,2,1,0:T(8,128)(2,1)S(1)}, bf16[1,1,16,128,128]{4,3,2,1,0:T(8,128)(2,1)}, u32[]{:S(2)}) copy-start(bf16[1,1,16,128,128]{4,3,2,1,0:T(8,128)(2,1)} %param.20) | copy-start | bytes 1572868
  7.2 78.2 %all-gather.2.cloned.1.call-start = ((), (), s32[]{:S(2)}) async-start(), calls=%async_computation.3 | async-start | bytes 4718592 | tf_op jit(solution)/shard_map/all_gather | solution.py:304
  11.8 4.9 %copy-start.7 = (s32[8,1,16,1]{2,3,1,0:T(1,128)S(1)}, s32[8,1,16,1]{2,3,1,0:T(1,128)}, u32[]{:S(2)}) copy-start(s32[8,1,16,1]{2,3,1,0:T(1,128)} %param.22) | copy-start | bytes 1540
  85.4 76.2 %collective-permute-start = (bf16[8,8,128,256]{3,2,1,0:T(8,128)(2,1)}, bf16[8,8,128,256]{3,2,1,0:T(8,128)(2,1)}, u32[]{:S(2)}, u32[]{:S(2)}) collective-permute-start(bf16[8,8,128,256]{3,2,1,0:T(8,128)(2,1)} %all-gather.2.cloned.1.call-done), channel_id=1, source_target_pairs={{0,1},{1,0},{2,3},{3,2},{4,5},{5,4},{6,7},{7,6},{8,9},{9,8},{10,11... | collective-permute-start | bytes 12582920 | tf_op jit(solution)/shard_map/ppermute | solution.py:305
  100.2 4.8 %copy-start.8 = (s32[1,1,16,32]{3,2,1,0:T(8,128)S(1)}, s32[1,1,16,32]{3,2,1,0:T(8,128)}, u32[]{:S(2)}) copy-start(s32[1,1,16,32]{3,2,1,0:T(8,128)} %param.17) | copy-start | bytes 6148
  100.2 5.4 %copy-start.9 = (s32[1,1,16,32]{3,2,1,0:T(8,128)S(1)}, s32[1,1,16,32]{3,2,1,0:T(8,128)}, u32[]{:S(2)}) copy-start(s32[1,1,16,32]{3,2,1,0:T(8,128)} %param.18) | copy-start | bytes 6148
  100.2 6.1 %copy-start.10 = (s32[1024]{0:T(1024)S(1)}, s32[1024]{0:T(1024)}, u32[]{:S(2)}) copy-start(s32[1024]{0:T(1024)} %param.15) | copy-start | bytes 12292
  100.2 6.1 %copy-start.12 = (s32[8,1,16]{2,1,0:T(1,128)S(1)}, s32[8,1,16]{2,1,0:T(1,128)}, u32[]{:S(2)}) copy-start(s32[8,1,16]{2,1,0:T(1,128)} %param.23) | copy-start | bytes 1540
  100.2 54.4 %all-to-all-start = ((f32[8,4,128,256]{3,1,2,0:T(4,128)}), f32[8,4,128,256]{3,1,2,0:T(4,128)}, u32[]{:S(2)}, u32[]{:S(2)}) async-start(f32[8,4,128,256]{3,1,2,0:T(4,128)} %copy.61), calls=%async_computation | async-start | bytes 8388608 | tf_op jit(solution)/shard_map/all_to_all | solution.py:328
  154.6 7.0 %copy-start.3 = (bf16[8,8,128,256]{3,2,1,0:T(8,128)(2,1)S(1)}, bf16[8,8,128,256]{3,2,1,0:T(8,128)(2,1)}, u32[]{:S(2)}) copy-start(bf16[8,8,128,256]{3,2,1,0:T(8,128)(2,1)} %all-gather.2.cloned.1.call-done) | copy-start | bytes 12582916
  177.5 27.9 %copy-start.5 = (bf16[1024,256]{1,0:T(8,128)(2,1)S(1)}, bf16[1024,256]{1,0:T(8,128)(2,1)}, u32[]{:S(2)}) copy-start(bf16[1024,256]{1,0:T(8,128)(2,1)} %param.14) | copy-start | bytes 1572868
  238.1 9.5 %copy-start.2 = (bf16[1024,256]{1,0:T(8,128)(2,1)S(1)}, bf16[1024,256]{1,0:T(8,128)(2,1)}, u32[]{:S(2)}) copy-start(bf16[1024,256]{1,0:T(8,128)(2,1)} %get-tuple-element.3) | copy-start | bytes 1572868
  245.8 26.7 %collective-permute-start.1 = (f32[8,8,128,256]{3,2,1,0:T(8,128)}, f32[8,8,128,256]{3,2,1,0:T(8,128)}, u32[]{:S(2)}, u32[]{:S(2)}) collective-permute-start(f32[8,8,128,256]{3,2,1,0:T(8,128)} %slice_bitcast_fusion), channel_id=1, source_target_pairs={{0,1},{1,0},{2,3},{3,2},{4,5},{5,4},{6,7},{7,6},{8,9},{9,8},{10,11... | collective-permute-start | bytes 25165832 | tf_op jit(solution)/shard_map/ppermute | solution.py:345
  250.1 49.5 %all-to-all-start.2 = ((bf16[8,4,128,256]{3,2,1,0:T(8,128)(2,1)}), bf16[8,4,128,256]{3,2,1,0:T(8,128)(2,1)S(1)}, u32[]{:S(2)}, u32[]{:S(2)}) async-start(bf16[8,4,128,256]{3,2,1,0:T(8,128)(2,1)} %copy.66), calls=%async_computation.2 | async-start | bytes 4194304 | tf_op jit(solution)/shard_map/all_to_all | solution.py:358
  299.6 55.6 %all-to-all-start.1 = ((bf16[8,8,128,256]{3,2,1,0:T(8,128)(2,1)}), bf16[8,8,128,256]{3,2,1,0:T(8,128)(2,1)}, u32[]{:S(2)}, u32[]{:S(2)}) async-start(bf16[8,8,128,256]{3,2,1,0:T(8,128)(2,1)} %fusion.1), calls=%async_computation.1 | async-start | bytes 8388608 | tf_op jit(solution)/shard_map/all_to_all | solution.py:347
  306.0 52.3 %copy-start.11 = (s32[1,1,16]{2,1,0:T(1,128)S(1)}, s32[1,1,16]{2,1,0:T(1,128)}, u32[]{:S(2)}) copy-start(s32[1,1,16]{2,1,0:T(1,128)} %param.21) | copy-start | bytes 196
  308.1 50.2 %copy-start.1 = (f32[16,128,256]{2,0,1:T(8,128)S(1)}, f32[16,128,256]{2,0,1:T(8,128)}, u32[]{:S(2)}) copy-start(f32[16,128,256]{2,0,1:T(8,128)} %copy.69) | copy-start | bytes 6291460
  308.1 51.6 %copy-start.6 = (bf16[256,256]{1,0:T(8,128)(2,1)S(1)}, bf16[256,256]{1,0:T(8,128)(2,1)}, u32[]{:S(2)}) copy-start(bf16[256,256]{1,0:T(8,128)(2,1)} %param.13) | copy-start | bytes 393220
  358.3 2.6 copy-start.4
Sparse Core Ops, SparseCore 0:
  10.9 74.4 all-gather.1

commit v7 on v6

--- a/solution.py
+++ b/solution.py
@@ -50,8 +50,11 @@
     grouped_slots(count_ref[c], slots, visit)
 
 
-def backward_kernel(rows_ref, cols_ref, count_ref, core_ref, vals_ref, grad_ref, out_ref, acc_ref):
-    c = pl.program_id(0)
+def backward_kernel(rows_ref, cols_ref, count_ref, core_ref, vals_ref, grad_ref, keep_ref, send_ref, acc_ref):
+    i = pl.program_id(0)
+    half = pl.num_programs(0) // 2
+    p = i // half
+    c = 2 * (i % half) + (p + core_ref[0]) % 2
     slots = vals_ref.shape[1]
     row_tiles = grad_ref.shape[0]
     acc_ref[...] = jnp.zeros_like(acc_ref)
@@ -69,7 +72,14 @@
             acc_ref[k] += prod
 
     grouped_slots(count_ref[c], slots, visit)
-    out_ref[0, 0] = acc_ref[...].astype(out_ref.dtype)
+
+    @pl.when(p == 0)
+    def _():
+        keep_ref[0] = acc_ref[...]
+
+    @pl.when(p == 1)
+    def _():
+        send_ref[0] = acc_ref[...]
 
 
 def tile_forward(rows, cols, count, vals, panels):
@@ -98,22 +108,29 @@
 def tile_backward(rows, cols, count, vals, grad_tiles, core):
     n_src, slots, tile, _ = vals.shape
     row_tiles, width = grad_tiles.shape[0], grad_tiles.shape[2]
+    half = n_src // 2
+
+    def source(i, core_ref):
+        return 2 * (i % half) + (i // half + core_ref[0]) % 2
+
     grid_spec = pltpu.PrefetchScalarGridSpec(
         num_scalar_prefetch=4,
         grid=(n_src,),
         in_specs=[
-            pl.BlockSpec((1, slots, tile, tile), lambda c, *_: (c, 0, 0, 0)),
-            pl.BlockSpec((row_tiles, tile, width), lambda c, *_: (0, 0, 0)),
+            pl.BlockSpec((1, slots, tile, tile), lambda i, r, k, n, core_ref: (source(i, core_ref), 0, 0, 0)),
+            pl.BlockSpec((row_tiles, tile, width), lambda i, *_: (0, 0, 0)),
         ],
-        out_specs=pl.BlockSpec(
-            (1, 1, row_tiles, tile, width), lambda c, r, k, n, core_ref: ((c + core_ref[0]) % 2, c // 2, 0, 0, 0)
-        ),
+        out_specs=[
+            pl.BlockSpec((1, row_tiles, tile, width), lambda i, *_: (jnp.minimum(i, half - 1), 0, 0, 0)),
+            pl.BlockSpec((1, row_tiles, tile, width), lambda i, *_: (jnp.maximum(i - half, 0), 0, 0, 0)),
+        ],
         scratch_shapes=[pltpu.VMEM((row_tiles, tile, width), jnp.float32)],
     )
     flops = 2 * n_src * slots * tile * tile * width
+    part = jax.ShapeDtypeStruct((half, row_tiles, tile, width), jnp.float32)
     return pl.pallas_call(
         backward_kernel,
-        out_shape=jax.ShapeDtypeStruct((2, n_src // 2, row_tiles, tile, width), jnp.float32),
+        out_shape=(part, part),
         grid_spec=grid_spec,
         cost_estimate=pl.CostEstimate(
             flops=flops, transcendentals=0, bytes_accessed=vals.size * 2 + n_src * row_tiles * tile * width * 4
@@ -301,10 +318,8 @@
     core = lax.axis_index("blk") % 2
     core_groups = [[i for i in range(n_blocks) if i % 2 == k] for k in range(2)]
     sibling = [(i, i ^ 1) for i in range(n_blocks)]
-    half = lax.all_gather(own_panel, "blk", axis=0, tiled=False, axis_index_groups=core_groups)
-    other = lax.ppermute(half, "blk", sibling)
-    pair = jnp.where(core == 0, jnp.stack([half, other], 1), jnp.stack([other, half], 1))
-    panels = pair.reshape(n_blocks, row_tiles, tile_size, width)
+    panels = lax.all_gather(proj, "blk", axis=0, tiled=True)
+    panels = panels.reshape(n_blocks, row_tiles, tile_size, width)
     agg_sum = tile_forward(dev_rows, dev_cols, dev_count, dev_vals, panels)
 
     dest_all = hub_dest[:, 0, :, 0]
@@ -341,9 +356,9 @@
     grad_agg = (cotangent.astype(jnp.float32) * keep * slope).astype(jnp.bfloat16)
     grad_tiles = grad_agg.reshape(row_tiles, tile_size, width)
 
-    partials = tile_backward(dev_rows, dev_cols, dev_count, dev_vals, grad_tiles, core.reshape(1))
-    from_sibling = lax.ppermute(partials[1], "blk", sibling)
-    pair_sum = (partials[0] + from_sibling).astype(jnp.bfloat16)
+    keep, send = tile_backward(dev_rows, dev_cols, dev_count, dev_vals, grad_tiles, core.reshape(1))
+    from_sibling = lax.ppermute(send, "blk", sibling)
+    pair_sum = (keep + from_sibling).astype(jnp.bfloat16)
     received_parts = lax.all_to_all(
         pair_sum, "blk", split_axis=0, concat_axis=0, tiled=True, axis_index_groups=core_groups
     )

time: 412 us -> 333 us (0.81)
  waiting for transfers between devices: 182 us -> 142 us
  starting transfers between devices: 34.6 us -> 17.9 us
  local copies, waits for them, and re-layouts: 36.4 us -> 21.1 us
  other arithmetic: 26 us -> 17.9 us
    all_gather x1, waiting for transfers between devices: 68.4 us -> 29 us  [local(): panels = lax.all_gather(proj, 'blk', axis=0, tiled=True)]
    all_to_all x1, starting transfers between devices: 22.4 us -> 6.73 us  [local(): lax.all_to_all(back_send, 'grp', split_axis=0, concat_axis=0, tiled=True)]
    select_n x1 -> x0, other arithmetic: 8.1 us -> none  [local(): jnp.where(core == 0, jnp.stack([half, other], 1), jnp.stack([other, half]...]
    select_n x1 -> x0, local copies, waits for them, and re-layouts: 7.73 us -> none  [local(): jnp.where(core == 0, jnp.stack([half, other], 1), jnp.stack([other, half]...]
    squeeze x1 -> x0, local copies, waits for them, and re-layouts: 7.67 us -> none  [local(): from_sibling = lax.ppermute(partials[1], 'blk', sibling)]
    ppermute x2 -> x1, waiting for transfers between devices: 0.01 us -> 4.2 us  [local(): from_sibling = lax.ppermute(send, 'blk', sibling)]
    all_to_all x1, waiting for transfers between devices: 17.9 us -> 13.7 us  [local(): lax.all_to_all(back_send, 'grp', split_axis=0, concat_axis=0, tiled=True)]
  transfers between devices with their start and end apart: 6 -> 5, of which waited for: 4 -> 5; matrix products, arithmetic and copies ran while one was open for 11% -> 14% of each run, Pallas kernels for 0% -> 0%
where the time goes in v7:
time: 333 us; the launch traced here: 332 us
  waiting for transfers between devices  142 us (43%)
  Pallas kernels  98.6 us (30%)
  local copies, waits for them, and re-layouts  21.1 us (6%)
  matrix products  20 us (6%)
  starting transfers between devices  17.9 us (5%)
  other arithmetic  17.9 us (5%)
  between operations  14.3 us (4%)
    all_to_all x1, waiting for transfers between devices, local(): lax.all_to_all(send_buf, 'grp', split_axis=0, concat_axis=0, tiled=True)  48.1 us
    all_to_all x1, waiting for transfers between devices, local(): lax.all_to_all(pair_sum, 'blk', split_axis=0, concat_axis=0, tiled=True,...  47 us
    pallas_call x1, Pallas kernels, weight_sum(): pl.pallas_call(functools.partial(weight_sum_kernel, n_grp, n_blk), out_sh...  39.4 us
    pallas_call x1, Pallas kernels, tile_backward(): pl.pallas_call(backward_kernel, out_shape=(part, part), grid_spec=grid_sp...  32.4 us
    all_gather x1, waiting for transfers between devices, local(): panels = lax.all_gather(proj, 'blk', axis=0, tiled=True)  29 us
    pallas_call x1, Pallas kernels, tile_forward(): pl.pallas_call(forward_kernel, out_shape=jax.ShapeDtypeStruct((row_tiles,...  26.9 us
    all_to_all x1, waiting for transfers between devices, local(): lax.all_to_all(back_send, 'grp', split_axis=0, concat_axis=0, tiled=True)  13.7 us
    reshape x2, local copies, waits for them, and re-layouts, local(): send_buf = send_buf.reshape(n_groups, capacity, tile_size, width)  10.2 us
  transfers between devices with their start and end apart: 5, of which 5 were waited for; matrix products, arithmetic and copies ran while one was open for 14% of the time, Pallas kernels for 0%

profile of v7, /device:TPU:1, one launch (start us, length us, event | category | flops | bytes accessed | tf_op | source)
XLA Modules:
  0.0 331.8 jit_solution(2051030762998694658)
XLA Ops:
  7.2 2.2 convolution_convert_fusion.2
  10.1 1.7 gather_fusion
  12.5 1.9 convolution_bitcast_fusion.1
  14.4 2.2 copy.57
  17.0 3.6 %fusion.31 = f32[32,128,256]{2,0,1:T(8,128)} fusion(f32[16,128,256]{2,0,1:T(8,128)S(1)} %copy.57, s32[16]{0:T(128)S(1)} %bitcast_add_fusion), kind=kOutput, calls=%fused_computation.52 | convolution fusion | flops 201327104 | bytes 6291520 | tf_op jit(solution)/shard_map/hs,hif->sif/dot_general | solution.py:341
  20.6 5.3 %reshape.109 = f32[8,4,128,256]{3,1,0,2:T(4,128)} reshape(f32[32,128,256]{2,0,1:T(8,128)} %fusion.31) | data formatting | bytes 8388608 | tf_op jit(solution)/shard_map/reshape | solution.py:342
  25.8 4.9 %copy.58 = f32[8,4,128,256]{3,1,2,0:T(4,128)} copy(f32[8,4,128,256]{3,1,0,2:T(4,128)} %reshape.109) | data formatting | bytes 8388608 | tf_op jit(solution)/shard_map/reshape | solution.py:342
  30.7 6.4 %all-to-all-start = ((f32[8,4,128,256]{3,1,2,0:T(4,128)}), f32[8,4,128,256]{3,1,2,0:T(4,128)}, u32[]{:S(2)}, u32[]{:S(2)}) async-start(f32[8,4,128,256]{3,1,2,0:T(4,128)} %copy.58), calls=%async_computation | async-start | bytes 8388608 | tf_op jit(solution)/shard_map/all_to_all | solution.py:343
  38.6 48.1 %all-to-all-done = f32[8,4,128,256]{3,1,2,0:T(4,128)} async-done(((f32[8,4,128,256]{3,1,2,0:T(4,128)}), f32[8,4,128,256]{3,1,2,0:T(4,128)}, u32[]{:S(2)}, u32[]{:S(2)}) %all-to-all-start) | async-done | bytes 4194336 | tf_op jit(solution)/shard_map/all_to_all | solution.py:343
  86.7 6.8 %convolution_bitcast_fusion.2 = f32[8,128,256]{2,0,1:T(8,128)S(1)} fusion(f32[8,4,128,256]{3,1,2,0:T(4,128)} %all-to-all-done, f32[8,4,8]{2,1,0:T(4,128)S(1)} %fusion.22), kind=kOutput, calls=%fused_computation.9 | convolution fusion | flops 100663296 | bytes 5243904 | tf_op jit(solution)/shard_map/scr,scif->rif/dot_general | solution.py:350
  93.6 29.0 %all-gather.2.cloned.1.call-done = bf16[16384,256]{1,0:T(8,128)(2,1)} async-done(((bf16[1024,256]{1,0:T(8,128)(2,1)}), bf16[16384,256]{1,0:T(8,128)(2,1)}) %all-gather.2.cloned.1.call-update) | async-done | bytes 8388624 | tf_op jit(solution)/shard_map/all_gather | solution.py:321
  122.6 26.9 %shard_map.139 = f32[8,128,256]{2,1,0:T(8,128)} custom-call(s32[512]{0:T(512)} %reshape_squeeze.6.rows_ref, s32[512]{0:T(512)} %reshape_squeeze.7.cols_ref, s32[16]{0:T(128)} %bitcast.107, bf16[16,32,128,128]{3,2,1,0:T(8,128)(2,1)} %bitcast.96, bf16[16,8,128,256]{3,2,1,0:T(8,128)(2,1)} %bitcast.99), custom_call_target="tpu_custom_call" | custom-call | flops 4294967296 | bytes 25165824 | tf_op jit(solution)/shard_map/pallas_call | solution.py:98
  149.5 1.6 copy_add_fusion.1
  151.1 1.4 fusion.12
  152.5 32.4 %shard_map.140 = (f32[8,8,128,256]{3,2,1,0:T(8,128)}, f32[8,8,128,256]{3,2,1,0:T(8,128)}) custom-call(s32[512]{0:T(512)} %reshape_squeeze.6.rows_ref, s32[512]{0:T(512)} %reshape_squeeze.7.cols_ref, s32[16]{0:T(128)} %bitcast.108, s32[1]{0:T(128)} %bitcast.18.core_ref, bf16[16,32,128,128]{3,2,1,0:T(8,128)(2,1)} %bitcast.97, bf16[8,128,256]{2,1,0:T(8,128)(2,1)} %bitcast.101), custom_call_target="tpu_custom_call" | custom-call | flops 4294967296 | bytes 33554432 | tf_op jit(solution)/shard_map/pallas_call | solution.py:131
  184.9 0.7 convolution_convert_fusion
  185.6 1.9 copy.63
  187.5 6.7 %all-to-all-start.2 = ((bf16[8,4,128,256]{3,2,1,0:T(8,128)(2,1)}), bf16[8,4,128,256]{3,2,1,0:T(8,128)(2,1)S(1)}, u32[]{:S(2)}, u32[]{:S(2)}) async-start(bf16[8,4,128,256]{3,2,1,0:T(8,128)(2,1)} %copy.63), calls=%async_computation.2 | async-start | bytes 4194304 | tf_op jit(solution)/shard_map/all_to_all | solution.py:373
  194.2 4.2 %collective-permute-done = f32[8,8,128,256]{3,2,1,0:T(8,128)} collective-permute-done((f32[8,8,128,256]{3,2,1,0:T(8,128)}, f32[8,8,128,256]{3,2,1,0:T(8,128)}, u32[]{:S(2)}, u32[]{:S(2)}) %collective-permute-start) | collective-permute-done | bytes 8388640 | tf_op jit(solution)/shard_map/ppermute | solution.py:360
  198.4 9.2 %add_convert_fusion = bf16[8,8,128,256]{3,2,1,0:T(8,128)(2,1)} fusion(f32[8,8,128,256]{3,2,1,0:T(8,128)} %get-tuple-element.5, f32[8,8,128,256]{3,2,1,0:T(8,128)} %collective-permute-done), kind=kLoop, calls=%fused_computation.2 | loop fusion | flops 4194304 | bytes 20971520 | tf_op jit(solution)/shard_map/convert_element_type | solution.py:361
  207.6 13.7 %all-to-all-done.2 = bf16[8,4,128,256]{3,2,1,0:T(8,128)(2,1)S(1)} async-done(((bf16[8,4,128,256]{3,2,1,0:T(8,128)(2,1)}), bf16[8,4,128,256]{3,2,1,0:T(8,128)(2,1)S(1)}, u32[]{:S(2)}, u32[]{:S(2)}) %all-to-all-start.2) | async-done | bytes 2097184 | tf_op jit(solution)/shard_map/all_to_all | solution.py:373
  221.3 4.7 %all-to-all-start.1 = ((bf16[8,8,128,256]{3,2,1,0:T(8,128)(2,1)}), bf16[8,8,128,256]{3,2,1,0:T(8,128)(2,1)}, u32[]{:S(2)}, u32[]{:S(2)}) async-start(bf16[8,8,128,256]{3,2,1,0:T(8,128)(2,1)} %add_convert_fusion), calls=%async_computation.1 | async-start | bytes 8388608 | tf_op jit(solution)/shard_map/all_to_all | solution.py:362
  226.1 1.3 fusion.2
  227.9 2.1 copy.66
  230.0 47.0 %all-to-all-done.1 = bf16[8,8,128,256]{3,2,1,0:T(8,128)(2,1)} async-done(((bf16[8,8,128,256]{3,2,1,0:T(8,128)(2,1)}), bf16[8,8,128,256]{3,2,1,0:T(8,128)(2,1)}, u32[]{:S(2)}, u32[]{:S(2)}) %all-to-all-start.1) | async-done | bytes 4194336 | tf_op jit(solution)/shard_map/all_to_all | solution.py:362
  277.0 3.0 convert_reduce_fusion
  280.0 1.3 fusion.13
  281.5 1.1 convolution_convert_fusion.1
  283.1 0.7 reshape.114.x_ref
  283.8 39.4 %shard_map.141 = f32[16,32,128]{2,1,0:T(8,128)} custom-call(f32[16,32,128]{2,1,0:T(8,128)} %reshape.114.x_ref), custom_call_target="tpu_custom_call" | custom-call | tf_op jit(solution)/shard_map/pallas_call | solution.py:219
  323.2 1.0 broadcast_multiply_fusion
  324.2 0.8 mul.60
  (43 shorter events, 4.4 us)
Async XLA Ops:
  7.2 5.3 %copy-start = (bf16[1,1,16,128,128]{4,3,2,1,0:T(8,128)(2,1)S(1)}, bf16[1,1,16,128,128]{4,3,2,1,0:T(8,128)(2,1)}, u32[]{:S(2)}) copy-start(bf16[1,1,16,128,128]{4,3,2,1,0:T(8,128)(2,1)} %param.20) | copy-start | bytes 1572868
  7.2 115.4 %all-gather.2.cloned.1.call-start = ((), (), s32[]{:S(2)}) async-start(), calls=%async_computation.3 | async-start | bytes 8912896 | tf_op jit(solution)/shard_map/all_gather | solution.py:321
  11.8 4.9 %copy-start.6 = (s32[8,1,16,1]{2,3,1,0:T(1,128)S(1)}, s32[8,1,16,1]{2,3,1,0:T(1,128)}, u32[]{:S(2)}) copy-start(s32[8,1,16,1]{2,3,1,0:T(1,128)} %param.22) | copy-start | bytes 1540
  30.7 6.4 %copy-start.7 = (s32[1,1,16,32]{3,2,1,0:T(8,128)S(1)}, s32[1,1,16,32]{3,2,1,0:T(8,128)}, u32[]{:S(2)}) copy-start(s32[1,1,16,32]{3,2,1,0:T(8,128)} %param.17) | copy-start | bytes 6148
  30.7 7.0 %copy-start.8 = (s32[1,1,16,32]{3,2,1,0:T(8,128)S(1)}, s32[1,1,16,32]{3,2,1,0:T(8,128)}, u32[]{:S(2)}) copy-start(s32[1,1,16,32]{3,2,1,0:T(8,128)} %param.18) | copy-start | bytes 6148
  30.7 7.7 %copy-start.9 = (s32[1024]{0:T(1024)S(1)}, s32[1024]{0:T(1024)}, u32[]{:S(2)}) copy-start(s32[1024]{0:T(1024)} %param.15) | copy-start | bytes 12292
  30.7 7.7 %copy-start.11 = (s32[8,1,16]{2,1,0:T(1,128)S(1)}, s32[8,1,16]{2,1,0:T(1,128)}, u32[]{:S(2)}) copy-start(s32[8,1,16]{2,1,0:T(1,128)} %param.23) | copy-start | bytes 1540
  30.7 56.0 %all-to-all-start = ((f32[8,4,128,256]{3,1,2,0:T(4,128)}), f32[8,4,128,256]{3,1,2,0:T(4,128)}, u32[]{:S(2)}, u32[]{:S(2)}) async-start(f32[8,4,128,256]{3,1,2,0:T(4,128)} %copy.58), calls=%async_computation | async-start | bytes 8388608 | tf_op jit(solution)/shard_map/all_to_all | solution.py:343
  122.6 28.5 %copy-start.4 = (bf16[1024,256]{1,0:T(8,128)(2,1)S(1)}, bf16[1024,256]{1,0:T(8,128)(2,1)}, u32[]{:S(2)}) copy-start(bf16[1024,256]{1,0:T(8,128)(2,1)} %param.14) | copy-start | bytes 1572868
  152.5 32.4 %copy-start.2 = (bf16[1024,256]{1,0:T(8,128)(2,1)S(1)}, bf16[1024,256]{1,0:T(8,128)(2,1)}, u32[]{:S(2)}) copy-start(bf16[1024,256]{1,0:T(8,128)(2,1)} %get-tuple-element.7) | copy-start | bytes 1572868
  184.9 13.5 %collective-permute-start = (f32[8,8,128,256]{3,2,1,0:T(8,128)}, f32[8,8,128,256]{3,2,1,0:T(8,128)}, u32[]{:S(2)}, u32[]{:S(2)}) collective-permute-start(f32[8,8,128,256]{3,2,1,0:T(8,128)} %get-tuple-element.6), channel_id=1, source_target_pairs={{0,1},{1,0},{2,3},{3,2},{4,5},{5,4},{6,7},{7,6},{8,9},{9,8},{10,11... | collective-permute-start | bytes 25165832 | tf_op jit(solution)/shard_map/ppermute | solution.py:360
  187.5 33.9 %all-to-all-start.2 = ((bf16[8,4,128,256]{3,2,1,0:T(8,128)(2,1)}), bf16[8,4,128,256]{3,2,1,0:T(8,128)(2,1)S(1)}, u32[]{:S(2)}, u32[]{:S(2)}) async-start(bf16[8,4,128,256]{3,2,1,0:T(8,128)(2,1)} %copy.63), calls=%async_computation.2 | async-start | bytes 4194304 | tf_op jit(solution)/shard_map/all_to_all | solution.py:373
  221.3 55.6 %all-to-all-start.1 = ((bf16[8,8,128,256]{3,2,1,0:T(8,128)(2,1)}), bf16[8,8,128,256]{3,2,1,0:T(8,128)(2,1)}, u32[]{:S(2)}, u32[]{:S(2)}) async-start(bf16[8,8,128,256]{3,2,1,0:T(8,128)(2,1)} %add_convert_fusion), calls=%async_computation.1 | async-start | bytes 8388608 | tf_op jit(solution)/shard_map/all_to_all | solution.py:362
  227.9 52.1 %copy-start.10 = (s32[1,1,16]{2,1,0:T(1,128)S(1)}, s32[1,1,16]{2,1,0:T(1,128)}, u32[]{:S(2)}) copy-start(s32[1,1,16]{2,1,0:T(1,128)} %param.21) | copy-start | bytes 196
  230.0 50.0 %copy-start.1 = (f32[16,128,256]{2,0,1:T(8,128)S(1)}, f32[16,128,256]{2,0,1:T(8,128)}, u32[]{:S(2)}) copy-start(f32[16,128,256]{2,0,1:T(8,128)} %copy.66) | copy-start | bytes 6291460
  230.0 51.5 %copy-start.5 = (bf16[256,256]{1,0:T(8,128)(2,1)S(1)}, bf16[256,256]{1,0:T(8,128)(2,1)}, u32[]{:S(2)}) copy-start(bf16[256,256]{1,0:T(8,128)(2,1)} %param.13) | copy-start | bytes 393220
  280.0 2.6 copy-start.3
Sparse Core Ops, SparseCore 0:
  11.0 111.4 all-gather.1

commit v8 on v7

--- a/solution.py
+++ b/solution.py
@@ -42,7 +42,7 @@
         for t, valid in terms:
             r = clamp_tile(rows_ref[c * slots + t], row_tiles)
             k = clamp_tile(cols_ref[c * slots + t], row_tiles)
-            prod = jnp.dot(vals_ref[0, t], panel_ref[0, k], preferred_element_type=jnp.float32)
+            prod = jnp.dot(vals_ref[0, t], panel_ref[0, 0, k], preferred_element_type=jnp.float32)
             parts.append((r, jnp.where(valid, prod, 0.0)))
         for r, prod in parts:
             out_ref[r] += prod
@@ -84,13 +84,13 @@
 
 def tile_forward(rows, cols, count, vals, panels):
     n_src, slots, tile, _ = vals.shape
-    row_tiles, width = panels.shape[1], panels.shape[3]
+    row_tiles, width = panels.shape[2], panels.shape[4]
     grid_spec = pltpu.PrefetchScalarGridSpec(
         num_scalar_prefetch=3,
         grid=(n_src,),
         in_specs=[
             pl.BlockSpec((1, slots, tile, tile), lambda c, *_: (c, 0, 0, 0)),
-            pl.BlockSpec((1, row_tiles, tile, width), lambda c, *_: (c, 0, 0, 0)),
+            pl.BlockSpec((1, 1, row_tiles, tile, width), lambda c, *_: (c % 2, c // 2, 0, 0, 0)),
         ],
         out_specs=pl.BlockSpec((row_tiles, tile, width), lambda c, *_: (0, 0, 0)),
     )
@@ -318,9 +318,8 @@
     core = lax.axis_index("blk") % 2
     core_groups = [[i for i in range(n_blocks) if i % 2 == k] for k in range(2)]
     sibling = [(i, i ^ 1) for i in range(n_blocks)]
-    panels = lax.all_gather(proj, "blk", axis=0, tiled=True)
-    panels = panels.reshape(n_blocks, row_tiles, tile_size, width)
-    agg_sum = tile_forward(dev_rows, dev_cols, dev_count, dev_vals, panels)
+    pair_groups = [[i, i + 1] for i in range(0, n_blocks, 2)]
+    same_core = lax.all_gather(own_panel, "blk", axis=0, tiled=False, axis_index_groups=core_groups)
 
     dest_all = hub_dest[:, 0, :, 0]
     hub_rows_all = hub_row[:, 0, :]
@@ -341,6 +340,9 @@
     send_buf = jnp.einsum("hs,hif->sif", send_place, hub_part, precision=highest)
     send_buf = send_buf.reshape(n_groups, capacity, tile_size, width)
     received = lax.all_to_all(send_buf, "grp", split_axis=0, concat_axis=0, tiled=True)
+    same_core, received = lax.optimization_barrier((same_core, received))
+    panels = lax.all_gather(same_core, "blk", axis=0, tiled=False, axis_index_groups=pair_groups)
+    agg_sum = tile_forward(dev_rows, dev_cols, dev_count, dev_vals, panels)
     chosen = (dest_all == my_group).astype(jnp.float32)
     slot_hot = (rank_all[..., None] == jnp.arange(capacity, dtype=jnp.int32)).astype(
         jnp.float32

time: 333 us -> 353 us (1.060)
  blocking collectives: 0 us -> 57.5 us
  waiting for transfers between devices: 142 us -> 111 us
  Pallas kernels: 98.6 us -> 94.3 us
    all_to_all x0 -> x1, blocking collectives: none -> 57.5 us  [local(): lax.all_to_all(send_buf, 'grp', split_axis=0, concat_axis=0, tiled=True)]
    all_to_all x1 -> x0, waiting for transfers between devices: 48.1 us -> none  [local(): lax.all_to_all(send_buf, 'grp', split_axis=0, concat_axis=0, tiled=True)]
    all_gather x1 -> x2, waiting for transfers between devices: 29 us -> 46.4 us  [the longest x1 32.2 us: local(): lax.all_gather(own_panel, 'blk', axis=0, tiled=False, axis_index_groups=c...]
    all_to_all x1 -> x0, starting transfers between devices: 6.37 us -> none  [local(): lax.all_to_all(send_buf, 'grp', split_axis=0, concat_axis=0, tiled=True)]
    all_to_all x1, starting transfers between devices: 4.74 us -> 8.38 us  [local(): lax.all_to_all(pair_sum, 'blk', split_axis=0, concat_axis=0, tiled=True,...]
  transfers between devices with their start and end apart: 5 -> 5, of which waited for: 5 -> 5; matrix products, arithmetic and copies ran while one was open for 14% -> 12% of each run, Pallas kernels for 0% -> 0%
where the time goes in v8:
time: 353 us; the launch traced here: 352 us
  waiting for transfers between devices  111 us (31%)
  Pallas kernels  94.3 us (27%)
  blocking collectives  57.5 us (16%)
  matrix products  20 us (6%)
  local copies, waits for them, and re-layouts  19.2 us (5%)
  other arithmetic  17.9 us (5%)
  starting transfers between devices  17.4 us (5%)
  between operations  14.3 us (4%)
    all_to_all x1, blocking collectives, local(): lax.all_to_all(send_buf, 'grp', split_axis=0, concat_axis=0, tiled=True)  57.5 us
    all_to_all x1, waiting for transfers between devices, local(): lax.all_to_all(pair_sum, 'blk', split_axis=0, concat_axis=0, tiled=True,...  47.2 us
    pallas_call x1, Pallas kernels, weight_sum(): pl.pallas_call(functools.partial(weight_sum_kernel, n_grp, n_blk), out_sh...  38 us
    all_gather x1, waiting for transfers between devices, local(): lax.all_gather(own_panel, 'blk', axis=0, tiled=False, axis_index_groups=c...  32.2 us
    pallas_call x1, Pallas kernels, tile_backward(): pl.pallas_call(backward_kernel, out_shape=(part, part), grid_spec=grid_sp...  30.1 us
    pallas_call x1, Pallas kernels, tile_forward(): pl.pallas_call(forward_kernel, out_shape=jax.ShapeDtypeStruct((row_tiles,...  26.2 us
    all_to_all x1, waiting for transfers between devices, local(): lax.all_to_all(back_send, 'grp', split_axis=0, concat_axis=0, tiled=True)  15.8 us
    all_gather x1, waiting for transfers between devices, local(): lax.all_gather(same_core, 'blk', axis=0, tiled=False, axis_index_groups=p...  14.2 us
  transfers between devices with their start and end apart: 5, of which 5 were waited for; matrix products, arithmetic and copies ran while one was open for 12% of the time, Pallas kernels for 0%

profile of v8, /device:TPU:1, one launch (start us, length us, event | category | flops | bytes accessed | tf_op | source)
XLA Modules:
  0.0 352.0 jit_solution(9385773169562633454)
XLA Ops:
  7.2 2.2 convolution_convert_fusion.2
  10.2 1.7 gather_fusion
  12.5 1.9 convolution_bitcast_fusion.1
  14.4 2.2 copy.57
  17.0 3.6 %fusion.31 = f32[32,128,256]{2,0,1:T(8,128)} fusion(f32[16,128,256]{2,0,1:T(8,128)S(1)} %copy.57, s32[16]{0:T(128)S(1)} %bitcast_add_fusion), kind=kOutput, calls=%fused_computation.52 | convolution fusion | flops 201327104 | bytes 6291520 | tf_op jit(solution)/shard_map/hs,hif->sif/dot_general | solution.py:340
  20.6 5.3 %reshape.105 = f32[8,4,128,256]{3,1,0,2:T(4,128)} reshape(f32[32,128,256]{2,0,1:T(8,128)} %fusion.31) | data formatting | bytes 8388608 | tf_op jit(solution)/shard_map/reshape | solution.py:341
  25.9 2.9 copy.58
  28.9 57.5 %all_to_all.15 = f32[8,4,128,256]{3,1,2,0:T(4,128)} all-to-all(f32[8,4,128,256]{3,1,2,0:T(4,128)S(1)} %copy.58), channel_id=1, replica_groups=mesh['grp'=8,'blk'=16] {'grp'}, dimensions={0} | all-to-all | bytes 8388608 | tf_op jit(solution)/shard_map/all_to_all | solution.py:342
  86.4 32.2 %all-gather.4.cloned.1.call-done = bf16[8,8,128,256]{3,2,1,0:T(8,128)(2,1)} async-done(((bf16[1,8,128,256]{3,2,1,0:T(8,128)(2,1)}), bf16[8,8,128,256]{3,2,1,0:T(8,128)(2,1)}) %all-gather.4.cloned.1.call-update) | async-done | bytes 4194320 | tf_op jit(solution)/shard_map/all_gather | solution.py:322
  120.1 6.8 %convolution_bitcast_fusion.2 = f32[8,128,256]{2,0,1:T(8,128)S(1)} fusion(f32[8,4,128,256]{3,1,2,0:T(4,128)} %all_to_all.15, f32[8,4,8]{2,1,0:T(4,128)S(1)} %fusion.22), kind=kOutput, calls=%fused_computation.9 | convolution fusion | flops 100663296 | bytes 5243904 | tf_op jit(solution)/shard_map/scr,scif->rif/dot_general | solution.py:352
  127.0 14.2 %all-gather.6.cloned.1.call-done = bf16[16,8,128,256]{3,2,1,0:T(8,128)(2,1)} async-done(((bf16[8,8,128,256]{3,2,1,0:T(8,128)(2,1)}), bf16[16,8,128,256]{3,2,1,0:T(8,128)(2,1)}) %all-gather.6.cloned.1.call-update) | async-done | bytes 8388624 | tf_op jit(solution)/shard_map/all_gather | solution.py:344
  141.1 26.2 %shard_map.139 = f32[8,128,256]{2,1,0:T(8,128)} custom-call(s32[512]{0:T(512)} %reshape_squeeze.6.rows_ref, s32[512]{0:T(512)} %reshape_squeeze.7.cols_ref, s32[16]{0:T(128)} %bitcast.109, bf16[16,32,128,128]{3,2,1,0:T(8,128)(2,1)} %bitcast.97, bf16[2,8,8,128,256]{4,3,2,1,0:T(8,128)(2,1)} %bitcast.101), custom_call_target="tpu_custom_call" | custom-call | flops 4294967296 | bytes 25165824 | tf_op jit(solution)/shard_map/pallas_call | solution.py:98
  167.3 1.6 copy_add_fusion.1
  168.9 1.4 fusion.12
  170.4 30.1 %shard_map.140 = (f32[8,8,128,256]{3,2,1,0:T(8,128)}, f32[8,8,128,256]{3,2,1,0:T(8,128)}) custom-call(s32[512]{0:T(512)} %reshape_squeeze.6.rows_ref, s32[512]{0:T(512)} %reshape_squeeze.7.cols_ref, s32[16]{0:T(128)} %bitcast.110, s32[1]{0:T(128)} %bitcast.19.core_ref, bf16[16,32,128,128]{3,2,1,0:T(8,128)(2,1)} %bitcast.98, bf16[8,128,256]{2,1,0:T(8,128)(2,1)} %bitcast.103), custom_call_target="tpu_custom_call" | custom-call | flops 4294967296 | bytes 33554432 | tf_op jit(solution)/shard_map/pallas_call | solution.py:131
  200.6 0.7 convolution_convert_fusion
  201.3 1.9 copy.63
  203.2 8.8 %all-to-all-start.2 = ((bf16[8,4,128,256]{3,2,1,0:T(8,128)(2,1)}), bf16[8,4,128,256]{3,2,1,0:T(8,128)(2,1)S(1)}, u32[]{:S(2)}, u32[]{:S(2)}) async-start(bf16[8,4,128,256]{3,2,1,0:T(8,128)(2,1)} %copy.63), calls=%async_computation.2 | async-start | bytes 4194304 | tf_op jit(solution)/shard_map/all_to_all | solution.py:375
  212.0 2.0 collective-permute-done
  214.0 9.2 %add_convert_fusion = bf16[8,8,128,256]{3,2,1,0:T(8,128)(2,1)} fusion(f32[8,8,128,256]{3,2,1,0:T(8,128)} %get-tuple-element.9, f32[8,8,128,256]{3,2,1,0:T(8,128)} %collective-permute-done), kind=kLoop, calls=%fused_computation.2 | loop fusion | flops 4194304 | bytes 20971520 | tf_op jit(solution)/shard_map/convert_element_type | solution.py:363
  223.2 15.8 %all-to-all-done.2 = bf16[8,4,128,256]{3,2,1,0:T(8,128)(2,1)S(1)} async-done(((bf16[8,4,128,256]{3,2,1,0:T(8,128)(2,1)}), bf16[8,4,128,256]{3,2,1,0:T(8,128)(2,1)S(1)}, u32[]{:S(2)}, u32[]{:S(2)}) %all-to-all-start.2) | async-done | bytes 2097184 | tf_op jit(solution)/shard_map/all_to_all | solution.py:375
  239.1 8.4 %all-to-all-start.1 = ((bf16[8,8,128,256]{3,2,1,0:T(8,128)(2,1)}), bf16[8,8,128,256]{3,2,1,0:T(8,128)(2,1)}, u32[]{:S(2)}, u32[]{:S(2)}) async-start(bf16[8,8,128,256]{3,2,1,0:T(8,128)(2,1)} %add_convert_fusion), calls=%async_computation.1 | async-start | bytes 8388608 | tf_op jit(solution)/shard_map/all_to_all | solution.py:364
  247.4 1.3 fusion.2
  249.3 2.1 copy.66
  251.4 47.2 %all-to-all-done.1 = bf16[8,8,128,256]{3,2,1,0:T(8,128)(2,1)} async-done(((bf16[8,8,128,256]{3,2,1,0:T(8,128)(2,1)}), bf16[8,8,128,256]{3,2,1,0:T(8,128)(2,1)}, u32[]{:S(2)}, u32[]{:S(2)}) %all-to-all-start.1) | async-done | bytes 4194336 | tf_op jit(solution)/shard_map/all_to_all | solution.py:364
  298.6 3.0 convert_reduce_fusion
  301.6 1.3 fusion.13
  303.1 1.1 convolution_convert_fusion.1
  304.7 0.7 reshape.110.x_ref
  305.4 38.0 %shard_map.141 = f32[16,32,128]{2,1,0:T(8,128)} custom-call(f32[16,32,128]{2,1,0:T(8,128)} %reshape.110.x_ref), custom_call_target="tpu_custom_call" | custom-call | tf_op jit(solution)/shard_map/pallas_call | solution.py:219
  343.4 1.0 broadcast_multiply_fusion
  344.3 0.8 mul.60
  (45 shorter events, 4.5 us)
Async XLA Ops:
  7.2 5.4 %copy-start = (bf16[1,1,16,128,128]{4,3,2,1,0:T(8,128)(2,1)S(1)}, bf16[1,1,16,128,128]{4,3,2,1,0:T(8,128)(2,1)}, u32[]{:S(2)}) copy-start(bf16[1,1,16,128,128]{4,3,2,1,0:T(8,128)(2,1)} %param.20) | copy-start | bytes 1572868
  7.2 111.4 %all-gather.4.cloned.1.call-start = ((), (), s32[]{:S(2)}) async-start(), calls=%async_computation.3 | async-start | bytes 4718592 | tf_op jit(solution)/shard_map/all_gather | solution.py:322
  9.5 131.7 %all-gather.6.cloned.1.call-start = ((), (), s32[]{:S(2)}) async-start(), calls=%async_computation.4 | async-start | bytes 12582912 | tf_op jit(solution)/shard_map/all_gather | solution.py:344
  11.8 4.8 %copy-start.6 = (s32[8,1,16,1]{2,3,1,0:T(1,128)S(1)}, s32[8,1,16,1]{2,3,1,0:T(1,128)}, u32[]{:S(2)}) copy-start(s32[8,1,16,1]{2,3,1,0:T(1,128)} %param.22) | copy-start | bytes 1540
  86.4 32.2 %copy-start.7 = (s32[1,1,16,32]{3,2,1,0:T(8,128)S(1)}, s32[1,1,16,32]{3,2,1,0:T(8,128)}, u32[]{:S(2)}) copy-start(s32[1,1,16,32]{3,2,1,0:T(8,128)} %param.17) | copy-start | bytes 6148
  86.4 32.9 %copy-start.8 = (s32[1,1,16,32]{3,2,1,0:T(8,128)S(1)}, s32[1,1,16,32]{3,2,1,0:T(8,128)}, u32[]{:S(2)}) copy-start(s32[1,1,16,32]{3,2,1,0:T(8,128)} %param.18) | copy-start | bytes 6148
  86.4 33.6 %copy-start.9 = (s32[1024]{0:T(1024)S(1)}, s32[1024]{0:T(1024)}, u32[]{:S(2)}) copy-start(s32[1024]{0:T(1024)} %param.15) | copy-start | bytes 12292
  86.4 33.6 %copy-start.11 = (s32[8,1,16]{2,1,0:T(1,128)S(1)}, s32[8,1,16]{2,1,0:T(1,128)}, u32[]{:S(2)}) copy-start(s32[8,1,16]{2,1,0:T(1,128)} %param.23) | copy-start | bytes 1540
  141.1 27.8 %copy-start.4 = (bf16[1024,256]{1,0:T(8,128)(2,1)S(1)}, bf16[1024,256]{1,0:T(8,128)(2,1)}, u32[]{:S(2)}) copy-start(bf16[1024,256]{1,0:T(8,128)(2,1)} %param.14) | copy-start | bytes 1572868
  170.4 30.2 %copy-start.2 = (bf16[1024,256]{1,0:T(8,128)(2,1)S(1)}, bf16[1024,256]{1,0:T(8,128)(2,1)}, u32[]{:S(2)}) copy-start(bf16[1024,256]{1,0:T(8,128)(2,1)} %get-tuple-element.11) | copy-start | bytes 1572868
  200.5 13.5 %collective-permute-start = (f32[8,8,128,256]{3,2,1,0:T(8,128)}, f32[8,8,128,256]{3,2,1,0:T(8,128)}, u32[]{:S(2)}, u32[]{:S(2)}) collective-permute-start(f32[8,8,128,256]{3,2,1,0:T(8,128)} %get-tuple-element.10), channel_id=1, source_target_pairs={{0,1},{1,0},{2,3},{3,2},{4,5},{5,4},{6,7},{7,6},{8,9},{9,8},{10,11... | collective-permute-start | bytes 25165832 | tf_op jit(solution)/shard_map/ppermute | solution.py:362
  203.2 35.9 %all-to-all-start.2 = ((bf16[8,4,128,256]{3,2,1,0:T(8,128)(2,1)}), bf16[8,4,128,256]{3,2,1,0:T(8,128)(2,1)S(1)}, u32[]{:S(2)}, u32[]{:S(2)}) async-start(bf16[8,4,128,256]{3,2,1,0:T(8,128)(2,1)} %copy.63), calls=%async_computation.2 | async-start | bytes 4194304 | tf_op jit(solution)/shard_map/all_to_all | solution.py:375
  239.1 59.5 %all-to-all-start.1 = ((bf16[8,8,128,256]{3,2,1,0:T(8,128)(2,1)}), bf16[8,8,128,256]{3,2,1,0:T(8,128)(2,1)}, u32[]{:S(2)}, u32[]{:S(2)}) async-start(bf16[8,8,128,256]{3,2,1,0:T(8,128)(2,1)} %add_convert_fusion), calls=%async_computation.1 | async-start | bytes 8388608 | tf_op jit(solution)/shard_map/all_to_all | solution.py:364
  249.3 52.3 %copy-start.10 = (s32[1,1,16]{2,1,0:T(1,128)S(1)}, s32[1,1,16]{2,1,0:T(1,128)}, u32[]{:S(2)}) copy-start(s32[1,1,16]{2,1,0:T(1,128)} %param.21) | copy-start | bytes 196
  251.4 50.3 %copy-start.1 = (f32[16,128,256]{2,0,1:T(8,128)S(1)}, f32[16,128,256]{2,0,1:T(8,128)}, u32[]{:S(2)}) copy-start(f32[16,128,256]{2,0,1:T(8,128)} %copy.66) | copy-start | bytes 6291460
  251.4 51.7 %copy-start.5 = (bf16[256,256]{1,0:T(8,128)(2,1)S(1)}, bf16[256,256]{1,0:T(8,128)(2,1)}, u32[]{:S(2)}) copy-start(bf16[256,256]{1,0:T(8,128)(2,1)} %param.13) | copy-start | bytes 393220
  301.6 2.6 copy-start.3
Sparse Core Ops, SparseCore 0:
  10.9 107.5 all-gather.3
  120.2 20.8 all-gather.5

commit v9 on v7

--- a/solution.py
+++ b/solution.py
@@ -338,7 +338,10 @@
     hub_cols = hub_col[0, 0]
     hub_src = jnp.take(own_panel, hub_cols, axis=0)
     hub_part = jnp.einsum("hij,hjf->hif", hub_tiles, hub_src, preferred_element_type=jnp.float32)
-    send_buf = jnp.einsum("hs,hif->sif", send_place, hub_part, precision=highest)
+    send_buf = jnp.einsum(
+        "hs,hif->sif", send_place.astype(jnp.bfloat16), hub_part.astype(jnp.bfloat16),
+        preferred_element_type=jnp.float32,
+    ).astype(jnp.bfloat16)
     send_buf = send_buf.reshape(n_groups, capacity, tile_size, width)
     received = lax.all_to_all(send_buf, "grp", split_axis=0, concat_axis=0, tiled=True)
     chosen = (dest_all == my_group).astype(jnp.float32)
@@ -347,7 +350,9 @@
     ) * chosen[..., None]
     row_hot = (hub_rows_all[..., None] == tile_range).astype(jnp.float32)
     routing = jnp.einsum("shc,shr->scr", slot_hot, row_hot, precision=highest)
-    agg_sum = agg_sum + jnp.einsum("scr,scif->rif", routing, received, precision=highest)
+    agg_sum = agg_sum + jnp.einsum(
+        "scr,scif->rif", routing.astype(jnp.bfloat16), received, preferred_element_type=jnp.float32
+    )
     agg_rows = agg_sum.reshape(rows_dev, width)
     layer_out = jax.nn.silu(agg_rows).astype(jnp.bfloat16)
     sigmoid_z = jax.nn.sigmoid(agg_rows)

time: 333 us -> 313 us (0.940)
  matrix products: 20 us -> 12.5 us
  waiting for transfers between devices: 142 us -> 137 us
  local copies, waits for them, and re-layouts: 21.1 us -> 16.2 us
  Pallas kernels: 98.6 us -> 94.3 us
    all_to_all x1, waiting for transfers between devices: 48.1 us -> 25.5 us  [local(): lax.all_to_all(send_buf, 'grp', split_axis=0, concat_axis=0, tiled=True)]
    all_gather x1, waiting for transfers between devices: 29 us -> 46.7 us  [local(): panels = lax.all_gather(proj, 'blk', axis=0, tiled=True)]
    dot_general x2, matrix products: 10.4 us -> 4.35 us  [the longest x1 2.33 us: local(): jnp.einsum('scr,scif->rif', routing.astype(jnp.bfloat16), received, prefe...]
    reshape x2, local copies, waits for them, and re-layouts: 10.2 us -> 5.77 us  [local(): send_buf = send_buf.reshape(n_groups, capacity, tile_size, width)]
  transfers between devices with their start and end apart: 5 -> 5, of which waited for: 5 -> 5; matrix products, arithmetic and copies ran while one was open for 14% -> 10% of each run, Pallas kernels for 0% -> 0%
where the time goes in v9:
time: 313 us; the launch traced here: 312 us
  waiting for transfers between devices  137 us (44%)
  Pallas kernels  94.3 us (30%)
  starting transfers between devices  19.9 us (6%)
  other arithmetic  17.3 us (6%)
  local copies, waits for them, and re-layouts  16.2 us (5%)
  between operations  14.3 us (5%)
  matrix products  12.5 us (4%)
    all_to_all x1, waiting for transfers between devices, local(): lax.all_to_all(pair_sum, 'blk', split_axis=0, concat_axis=0, tiled=True,...  47 us
    all_gather x1, waiting for transfers between devices, local(): panels = lax.all_gather(proj, 'blk', axis=0, tiled=True)  46.7 us
    pallas_call x1, Pallas kernels, weight_sum(): pl.pallas_call(functools.partial(weight_sum_kernel, n_grp, n_blk), out_sh...  38 us
    pallas_call x1, Pallas kernels, tile_backward(): pl.pallas_call(backward_kernel, out_shape=(part, part), grid_spec=grid_sp...  30.3 us
    pallas_call x1, Pallas kernels, tile_forward(): pl.pallas_call(forward_kernel, out_shape=jax.ShapeDtypeStruct((row_tiles,...  26 us
    all_to_all x1, waiting for transfers between devices, local(): lax.all_to_all(send_buf, 'grp', split_axis=0, concat_axis=0, tiled=True)  25.5 us
    all_to_all x1, waiting for transfers between devices, local(): lax.all_to_all(back_send, 'grp', split_axis=0, concat_axis=0, tiled=True)  15.7 us
    convert_element_type x1, other arithmetic, local(): pair_sum = (keep + from_sibling).astype(jnp.bfloat16)  9.21 us
  transfers between devices with their start and end apart: 5, of which 5 were waited for; matrix products, arithmetic and copies ran while one was open for 10% of the time, Pallas kernels for 0%

profile of v9, /device:TPU:1, one launch (start us, length us, event | category | flops | bytes accessed | tf_op | source)
XLA Modules:
  0.0 311.6 jit_solution(11221176596347312715)
XLA Ops:
  7.2 2.2 convolution_convert_fusion.4
  10.1 1.7 gather_fusion
  12.4 1.7 copy.57
  14.4 2.0 convolution_convert_fusion
  16.5 2.1 reshape.109
  18.5 3.7 %copy.58 = bf16[8,4,128,256]{3,1,2,0:T(4,128)(2,1)} copy(bf16[8,4,128,256]{3,1,0,2:T(4,128)(2,1)} %reshape.109) | data formatting | bytes 4194304 | tf_op jit(solution)/shard_map/reshape | solution.py:345
  22.2 6.3 %all-to-all-start = ((bf16[8,4,128,256]{3,1,2,0:T(4,128)(2,1)}), bf16[8,4,128,256]{3,1,2,0:T(4,128)(2,1)S(1)}, u32[]{:S(2)}, u32[]{:S(2)}) async-start(bf16[8,4,128,256]{3,1,2,0:T(4,128)(2,1)} %copy.58), calls=%async_computation | async-start | bytes 4194304 | tf_op jit(solution)/shard_map/all_to_all | solution.py:346
  29.2 0.7 reshape_squeeze.7.cols_ref
  30.1 25.5 %all-to-all-done = bf16[8,4,128,256]{3,1,2,0:T(4,128)(2,1)S(1)} async-done(((bf16[8,4,128,256]{3,1,2,0:T(4,128)(2,1)}), bf16[8,4,128,256]{3,1,2,0:T(4,128)(2,1)S(1)}, u32[]{:S(2)}, u32[]{:S(2)}) %all-to-all-start) | async-done | bytes 2097184 | tf_op jit(solution)/shard_map/all_to_all | solution.py:346
  55.6 2.3 convolution_bitcast_fusion.1
  58.0 46.7 %all-gather.2.cloned.1.call-done = bf16[16384,256]{1,0:T(8,128)(2,1)} async-done(((bf16[1024,256]{1,0:T(8,128)(2,1)}), bf16[16384,256]{1,0:T(8,128)(2,1)}) %all-gather.2.cloned.1.call-update) | async-done | bytes 8388624 | tf_op jit(solution)/shard_map/all_gather | solution.py:321
  104.7 26.0 %shard_map.139 = f32[8,128,256]{2,1,0:T(8,128)} custom-call(s32[512]{0:T(512)} %reshape_squeeze.6.rows_ref, s32[512]{0:T(512)} %reshape_squeeze.7.cols_ref, s32[16]{0:T(128)} %bitcast.105, bf16[16,32,128,128]{3,2,1,0:T(8,128)(2,1)} %bitcast.93, bf16[16,8,128,256]{3,2,1,0:T(8,128)(2,1)} %bitcast.96), custom_call_target="tpu_custom_call" | custom-call | flops 4294967296 | bytes 25165824 | tf_op jit(solution)/shard_map/pallas_call | solution.py:98
  130.7 1.7 copy_add_fusion.1
  132.4 1.4 fusion.13
  133.8 30.3 %shard_map.140 = (f32[8,8,128,256]{3,2,1,0:T(8,128)}, f32[8,8,128,256]{3,2,1,0:T(8,128)}) custom-call(s32[512]{0:T(512)} %reshape_squeeze.6.rows_ref, s32[512]{0:T(512)} %reshape_squeeze.7.cols_ref, s32[16]{0:T(128)} %bitcast.106, s32[1]{0:T(128)} %bitcast.18.core_ref, bf16[16,32,128,128]{3,2,1,0:T(8,128)(2,1)} %bitcast.94, bf16[8,128,256]{2,1,0:T(8,128)(2,1)} %bitcast.98), custom_call_target="tpu_custom_call" | custom-call | flops 4294967296 | bytes 33554432 | tf_op jit(solution)/shard_map/pallas_call | solution.py:131
  164.2 0.7 convolution_convert_fusion.1
  164.8 1.9 copy.63
  166.7 8.8 %all-to-all-start.2 = ((bf16[8,4,128,256]{3,2,1,0:T(8,128)(2,1)}), bf16[8,4,128,256]{3,2,1,0:T(8,128)(2,1)S(1)}, u32[]{:S(2)}, u32[]{:S(2)}) async-start(bf16[8,4,128,256]{3,2,1,0:T(8,128)(2,1)} %copy.63), calls=%async_computation.2 | async-start | bytes 4194304 | tf_op jit(solution)/shard_map/all_to_all | solution.py:378
  175.5 2.1 collective-permute-done
  177.6 9.2 %add_convert_fusion = bf16[8,8,128,256]{3,2,1,0:T(8,128)(2,1)} fusion(f32[8,8,128,256]{3,2,1,0:T(8,128)} %get-tuple-element.5, f32[8,8,128,256]{3,2,1,0:T(8,128)} %collective-permute-done), kind=kLoop, calls=%fused_computation.2 | loop fusion | flops 4194304 | bytes 20971520 | tf_op jit(solution)/shard_map/convert_element_type | solution.py:366
  186.9 15.7 %all-to-all-done.2 = bf16[8,4,128,256]{3,2,1,0:T(8,128)(2,1)S(1)} async-done(((bf16[8,4,128,256]{3,2,1,0:T(8,128)(2,1)}), bf16[8,4,128,256]{3,2,1,0:T(8,128)(2,1)S(1)}, u32[]{:S(2)}, u32[]{:S(2)}) %all-to-all-start.2) | async-done | bytes 2097184 | tf_op jit(solution)/shard_map/all_to_all | solution.py:378
  202.6 4.7 %all-to-all-start.1 = ((bf16[8,8,128,256]{3,2,1,0:T(8,128)(2,1)}), bf16[8,8,128,256]{3,2,1,0:T(8,128)(2,1)}, u32[]{:S(2)}, u32[]{:S(2)}) async-start(bf16[8,8,128,256]{3,2,1,0:T(8,128)(2,1)} %add_convert_fusion), calls=%async_computation.1 | async-start | bytes 8388608 | tf_op jit(solution)/shard_map/all_to_all | solution.py:367
  207.3 1.3 fusion.2
  209.1 2.1 copy.66
  211.2 47.0 %all-to-all-done.1 = bf16[8,8,128,256]{3,2,1,0:T(8,128)(2,1)} async-done(((bf16[8,8,128,256]{3,2,1,0:T(8,128)(2,1)}), bf16[8,8,128,256]{3,2,1,0:T(8,128)(2,1)}, u32[]{:S(2)}, u32[]{:S(2)}) %all-to-all-start.1) | async-done | bytes 4194336 | tf_op jit(solution)/shard_map/all_to_all | solution.py:367
  258.2 3.0 convert_reduce_fusion
  261.3 1.3 fusion.14
  262.7 1.1 convolution_convert_fusion.3
  264.3 0.7 reshape.114.x_ref
  265.0 38.0 %shard_map.141 = f32[16,32,128]{2,1,0:T(8,128)} custom-call(f32[16,32,128]{2,1,0:T(8,128)} %reshape.114.x_ref), custom_call_target="tpu_custom_call" | custom-call | tf_op jit(solution)/shard_map/pallas_call | solution.py:219
  303.0 1.0 broadcast_multiply_fusion
  304.0 0.8 mul.60
  (44 shorter events, 3.6 us)
Async XLA Ops:
  7.2 4.7 %copy-start = (bf16[1,1,16,128,128]{4,3,2,1,0:T(8,128)(2,1)S(1)}, bf16[1,1,16,128,128]{4,3,2,1,0:T(8,128)(2,1)}, u32[]{:S(2)}) copy-start(bf16[1,1,16,128,128]{4,3,2,1,0:T(8,128)(2,1)} %param.20) | copy-start | bytes 1572868
  7.2 4.6 %copy-start.11 = (s32[1,1,16]{2,1,0:T(1,128)S(1)}, s32[1,1,16]{2,1,0:T(1,128)}, u32[]{:S(2)}) copy-start(s32[1,1,16]{2,1,0:T(1,128)} %param.21) | copy-start | bytes 196
  7.2 97.5 %all-gather.2.cloned.1.call-start = ((), (), s32[]{:S(2)}) async-start(), calls=%async_computation.3 | async-start | bytes 8912896 | tf_op jit(solution)/shard_map/all_gather | solution.py:321
  11.8 2.3 copy-start.7
  22.2 6.3 %copy-start.8 = (s32[1,1,16,32]{3,2,1,0:T(8,128)S(1)}, s32[1,1,16,32]{3,2,1,0:T(8,128)}, u32[]{:S(2)}) copy-start(s32[1,1,16,32]{3,2,1,0:T(8,128)} %param.17) | copy-start | bytes 6148
  22.2 7.0 %copy-start.9 = (s32[1,1,16,32]{3,2,1,0:T(8,128)S(1)}, s32[1,1,16,32]{3,2,1,0:T(8,128)}, u32[]{:S(2)}) copy-start(s32[1,1,16,32]{3,2,1,0:T(8,128)} %param.18) | copy-start | bytes 6148
  22.2 7.7 %copy-start.10 = (s32[1024]{0:T(1024)S(1)}, s32[1024]{0:T(1024)}, u32[]{:S(2)}) copy-start(s32[1024]{0:T(1024)} %param.15) | copy-start | bytes 12292
  22.2 7.7 %copy-start.12 = (s32[8,1,16]{2,1,0:T(1,128)S(1)}, s32[8,1,16]{2,1,0:T(1,128)}, u32[]{:S(2)}) copy-start(s32[8,1,16]{2,1,0:T(1,128)} %param.23) | copy-start | bytes 1540
  22.2 33.4 %all-to-all-start = ((bf16[8,4,128,256]{3,1,2,0:T(4,128)(2,1)}), bf16[8,4,128,256]{3,1,2,0:T(4,128)(2,1)S(1)}, u32[]{:S(2)}, u32[]{:S(2)}) async-start(bf16[8,4,128,256]{3,1,2,0:T(4,128)(2,1)} %copy.58), calls=%async_computation | async-start | bytes 4194304 | tf_op jit(solution)/shard_map/all_to_all | solution.py:346
  104.7 26.0 %copy-start.4 = (f32[8,128,256]{2,0,1:T(8,128)S(1)}, f32[8,128,256]{2,0,1:T(8,128)}, u32[]{:S(2)}) copy-start(f32[8,128,256]{2,0,1:T(8,128)} %convolution_bitcast_fusion.1) | copy-start | bytes 3145732
  130.7 1.7 copy-start.5
  133.8 30.3 %copy-start.2 = (bf16[1024,256]{1,0:T(8,128)(2,1)S(1)}, bf16[1024,256]{1,0:T(8,128)(2,1)}, u32[]{:S(2)}) copy-start(bf16[1024,256]{1,0:T(8,128)(2,1)} %get-tuple-element.7) | copy-start | bytes 1572868
  164.1 13.5 %collective-permute-start = (f32[8,8,128,256]{3,2,1,0:T(8,128)}, f32[8,8,128,256]{3,2,1,0:T(8,128)}, u32[]{:S(2)}, u32[]{:S(2)}) collective-permute-start(f32[8,8,128,256]{3,2,1,0:T(8,128)} %get-tuple-element.6), channel_id=1, source_target_pairs={{0,1},{1,0},{2,3},{3,2},{4,5},{5,4},{6,7},{7,6},{8,9},{9,8},{10,11... | collective-permute-start | bytes 25165832 | tf_op jit(solution)/shard_map/ppermute | solution.py:365
  166.7 35.9 %all-to-all-start.2 = ((bf16[8,4,128,256]{3,2,1,0:T(8,128)(2,1)}), bf16[8,4,128,256]{3,2,1,0:T(8,128)(2,1)S(1)}, u32[]{:S(2)}, u32[]{:S(2)}) async-start(bf16[8,4,128,256]{3,2,1,0:T(8,128)(2,1)} %copy.63), calls=%async_computation.2 | async-start | bytes 4194304 | tf_op jit(solution)/shard_map/all_to_all | solution.py:378
  202.6 55.6 %all-to-all-start.1 = ((bf16[8,8,128,256]{3,2,1,0:T(8,128)(2,1)}), bf16[8,8,128,256]{3,2,1,0:T(8,128)(2,1)}, u32[]{:S(2)}, u32[]{:S(2)}) async-start(bf16[8,8,128,256]{3,2,1,0:T(8,128)(2,1)} %add_convert_fusion), calls=%async_computation.1 | async-start | bytes 8388608 | tf_op jit(solution)/shard_map/all_to_all | solution.py:367
  211.2 50.0 %copy-start.1 = (f32[16,128,256]{2,0,1:T(8,128)S(1)}, f32[16,128,256]{2,0,1:T(8,128)}, u32[]{:S(2)}) copy-start(f32[16,128,256]{2,0,1:T(8,128)} %copy.66) | copy-start | bytes 6291460
  261.2 1.5 copy-start.6
  261.2 2.6 copy-start.3
Sparse Core Ops, SparseCore 0:
  11.0 93.5 all-gather.1

commit v10 on v9

--- a/solution.py
+++ b/solution.py
@@ -9,7 +9,7 @@
 from jax.sharding import PartitionSpec as P
 
 
-UNROLL = 4
+UNROLL = 8
 
 
 def grouped_slots(count, slots, visit):

time: 313 us -> 303 us (0.968)
  starting transfers between devices: 19.9 us -> 14.7 us
  Pallas kernels: 94.3 us -> 89.5 us
    all_to_all x1, waiting for transfers between devices: 15.7 us -> 10.5 us  [local(): lax.all_to_all(back_send, 'grp', split_axis=0, concat_axis=0, tiled=True)]
    all_to_all x1, starting transfers between devices: 8.8 us -> 3.6 us  [local(): lax.all_to_all(back_send, 'grp', split_axis=0, concat_axis=0, tiled=True)]
    ppermute x1, waiting for transfers between devices: 2.14 us -> 7.34 us  [local(): from_sibling = lax.ppermute(send, 'blk', sibling)]
  transfers between devices with their start and end apart: 5 -> 5, of which waited for: 5 -> 5; matrix products, arithmetic and copies ran while one was open for 10% -> 11% of each run, Pallas kernels for 0% -> 0%
where the time goes in v10:
time: 303 us; the launch traced here: 302 us
  waiting for transfers between devices  137 us (45%)
  Pallas kernels  89.5 us (30%)
  other arithmetic  17.3 us (6%)
  local copies, waits for them, and re-layouts  16.2 us (5%)
  starting transfers between devices  14.7 us (5%)
  between operations  14.3 us (5%)
  matrix products  12.5 us (4%)
    all_to_all x1, waiting for transfers between devices, local(): lax.all_to_all(pair_sum, 'blk', split_axis=0, concat_axis=0, tiled=True,...  47 us
    all_gather x1, waiting for transfers between devices, local(): panels = lax.all_gather(proj, 'blk', axis=0, tiled=True)  46.7 us
    pallas_call x1, Pallas kernels, weight_sum(): pl.pallas_call(functools.partial(weight_sum_kernel, n_grp, n_blk), out_sh...  37.7 us
    pallas_call x1, Pallas kernels, tile_backward(): pl.pallas_call(backward_kernel, out_shape=(part, part), grid_spec=grid_sp...  28.2 us
    all_to_all x1, waiting for transfers between devices, local(): lax.all_to_all(send_buf, 'grp', split_axis=0, concat_axis=0, tiled=True)  25.5 us
    pallas_call x1, Pallas kernels, tile_forward(): pl.pallas_call(forward_kernel, out_shape=jax.ShapeDtypeStruct((row_tiles,...  23.7 us
    all_to_all x1, waiting for transfers between devices, local(): lax.all_to_all(back_send, 'grp', split_axis=0, concat_axis=0, tiled=True)  10.5 us
    convert_element_type x1, other arithmetic, local(): pair_sum = (keep + from_sibling).astype(jnp.bfloat16)  9.21 us
  transfers between devices with their start and end apart: 5, of which 5 were waited for; matrix products, arithmetic and copies ran while one was open for 11% of the time, Pallas kernels for 0%

profile of v10, /device:TPU:1, one launch (start us, length us, event | category | flops | bytes accessed | tf_op | source)
XLA Modules:
  0.0 301.6 jit_solution(994596383838975712)
XLA Ops:
  7.2 2.2 convolution_convert_fusion.4
  10.1 1.7 gather_fusion
  12.4 1.7 copy.57
  14.4 2.0 convolution_convert_fusion
  16.5 2.1 reshape.109
  18.5 3.7 %copy.58 = bf16[8,4,128,256]{3,1,2,0:T(4,128)(2,1)} copy(bf16[8,4,128,256]{3,1,0,2:T(4,128)(2,1)} %reshape.109) | data formatting | bytes 4194304 | tf_op jit(solution)/shard_map/reshape | solution.py:345
  22.2 6.3 %all-to-all-start = ((bf16[8,4,128,256]{3,1,2,0:T(4,128)(2,1)}), bf16[8,4,128,256]{3,1,2,0:T(4,128)(2,1)S(1)}, u32[]{:S(2)}, u32[]{:S(2)}) async-start(bf16[8,4,128,256]{3,1,2,0:T(4,128)(2,1)} %copy.58), calls=%async_computation | async-start | bytes 4194304 | tf_op jit(solution)/shard_map/all_to_all | solution.py:346
  29.2 0.7 reshape_squeeze.7.cols_ref
  30.1 25.5 %all-to-all-done = bf16[8,4,128,256]{3,1,2,0:T(4,128)(2,1)S(1)} async-done(((bf16[8,4,128,256]{3,1,2,0:T(4,128)(2,1)}), bf16[8,4,128,256]{3,1,2,0:T(4,128)(2,1)S(1)}, u32[]{:S(2)}, u32[]{:S(2)}) %all-to-all-start) | async-done | bytes 2097184 | tf_op jit(solution)/shard_map/all_to_all | solution.py:346
  55.6 2.3 convolution_bitcast_fusion.1
  58.0 46.7 %all-gather.2.cloned.1.call-done = bf16[16384,256]{1,0:T(8,128)(2,1)} async-done(((bf16[1024,256]{1,0:T(8,128)(2,1)}), bf16[16384,256]{1,0:T(8,128)(2,1)}) %all-gather.2.cloned.1.call-update) | async-done | bytes 8388624 | tf_op jit(solution)/shard_map/all_gather | solution.py:321
  104.7 23.7 %shard_map.139 = f32[8,128,256]{2,1,0:T(8,128)} custom-call(s32[512]{0:T(512)} %reshape_squeeze.6.rows_ref, s32[512]{0:T(512)} %reshape_squeeze.7.cols_ref, s32[16]{0:T(128)} %bitcast.105, bf16[16,32,128,128]{3,2,1,0:T(8,128)(2,1)} %bitcast.93, bf16[16,8,128,256]{3,2,1,0:T(8,128)(2,1)} %bitcast.96), custom_call_target="tpu_custom_call" | custom-call | flops 4294967296 | bytes 25165824 | tf_op jit(solution)/shard_map/pallas_call | solution.py:98
  128.4 1.7 copy_add_fusion.1
  130.0 1.4 fusion.13
  131.5 28.2 %shard_map.140 = (f32[8,8,128,256]{3,2,1,0:T(8,128)}, f32[8,8,128,256]{3,2,1,0:T(8,128)}) custom-call(s32[512]{0:T(512)} %reshape_squeeze.6.rows_ref, s32[512]{0:T(512)} %reshape_squeeze.7.cols_ref, s32[16]{0:T(128)} %bitcast.106, s32[1]{0:T(128)} %bitcast.18.core_ref, bf16[16,32,128,128]{3,2,1,0:T(8,128)(2,1)} %bitcast.94, bf16[8,128,256]{2,1,0:T(8,128)(2,1)} %bitcast.98), custom_call_target="tpu_custom_call" | custom-call | flops 4294967296 | bytes 33554432 | tf_op jit(solution)/shard_map/pallas_call | solution.py:131
  159.6 0.7 convolution_convert_fusion.1
  160.3 1.9 copy.63
  162.2 3.6 %all-to-all-start.2 = ((bf16[8,4,128,256]{3,2,1,0:T(8,128)(2,1)}), bf16[8,4,128,256]{3,2,1,0:T(8,128)(2,1)S(1)}, u32[]{:S(2)}, u32[]{:S(2)}) async-start(bf16[8,4,128,256]{3,2,1,0:T(8,128)(2,1)} %copy.63), calls=%async_computation.2 | async-start | bytes 4194304 | tf_op jit(solution)/shard_map/all_to_all | solution.py:378
  165.8 7.3 %collective-permute-done = f32[8,8,128,256]{3,2,1,0:T(8,128)} collective-permute-done((f32[8,8,128,256]{3,2,1,0:T(8,128)}, f32[8,8,128,256]{3,2,1,0:T(8,128)}, u32[]{:S(2)}, u32[]{:S(2)}) %collective-permute-start) | collective-permute-done | bytes 8388640 | tf_op jit(solution)/shard_map/ppermute | solution.py:365
  173.1 9.2 %add_convert_fusion = bf16[8,8,128,256]{3,2,1,0:T(8,128)(2,1)} fusion(f32[8,8,128,256]{3,2,1,0:T(8,128)} %get-tuple-element.5, f32[8,8,128,256]{3,2,1,0:T(8,128)} %collective-permute-done), kind=kLoop, calls=%fused_computation.2 | loop fusion | flops 4194304 | bytes 20971520 | tf_op jit(solution)/shard_map/convert_element_type | solution.py:366
  182.3 10.5 %all-to-all-done.2 = bf16[8,4,128,256]{3,2,1,0:T(8,128)(2,1)S(1)} async-done(((bf16[8,4,128,256]{3,2,1,0:T(8,128)(2,1)}), bf16[8,4,128,256]{3,2,1,0:T(8,128)(2,1)S(1)}, u32[]{:S(2)}, u32[]{:S(2)}) %all-to-all-start.2) | async-done | bytes 2097184 | tf_op jit(solution)/shard_map/all_to_all | solution.py:378
  192.8 4.7 %all-to-all-start.1 = ((bf16[8,8,128,256]{3,2,1,0:T(8,128)(2,1)}), bf16[8,8,128,256]{3,2,1,0:T(8,128)(2,1)}, u32[]{:S(2)}, u32[]{:S(2)}) async-start(bf16[8,8,128,256]{3,2,1,0:T(8,128)(2,1)} %add_convert_fusion), calls=%async_computation.1 | async-start | bytes 8388608 | tf_op jit(solution)/shard_map/all_to_all | solution.py:367
  197.6 1.3 fusion.2
  199.4 2.1 copy.66
  201.5 47.0 %all-to-all-done.1 = bf16[8,8,128,256]{3,2,1,0:T(8,128)(2,1)} async-done(((bf16[8,8,128,256]{3,2,1,0:T(8,128)(2,1)}), bf16[8,8,128,256]{3,2,1,0:T(8,128)(2,1)}, u32[]{:S(2)}, u32[]{:S(2)}) %all-to-all-start.1) | async-done | bytes 4194336 | tf_op jit(solution)/shard_map/all_to_all | solution.py:367
  248.5 3.0 %convert_reduce_fusion = f32[8,128,256]{2,1,0:T(8,128)S(1)} fusion(bf16[8,8,128,256]{3,2,1,0:T(8,128)(2,1)} %all-to-all-done.1), kind=kLoop, calls=%fused_computation.1 | loop fusion | flops 3932160 | bytes 5242880 | tf_op jit(solution)/shard_map/reduce_sum | solution.py:370
  251.5 1.3 fusion.14
  253.0 1.1 convolution_convert_fusion.3
  254.6 0.7 reshape.114.x_ref
  255.3 37.7 %shard_map.141 = f32[16,32,128]{2,1,0:T(8,128)} custom-call(f32[16,32,128]{2,1,0:T(8,128)} %reshape.114.x_ref), custom_call_target="tpu_custom_call" | custom-call | tf_op jit(solution)/shard_map/pallas_call | solution.py:219
  293.0 1.0 broadcast_multiply_fusion
  294.0 0.8 mul.60
  (44 shorter events, 3.6 us)
Async XLA Ops:
  7.2 4.7 %copy-start = (bf16[1,1,16,128,128]{4,3,2,1,0:T(8,128)(2,1)S(1)}, bf16[1,1,16,128,128]{4,3,2,1,0:T(8,128)(2,1)}, u32[]{:S(2)}) copy-start(bf16[1,1,16,128,128]{4,3,2,1,0:T(8,128)(2,1)} %param.20) | copy-start | bytes 1572868
  7.2 4.6 %copy-start.11 = (s32[1,1,16]{2,1,0:T(1,128)S(1)}, s32[1,1,16]{2,1,0:T(1,128)}, u32[]{:S(2)}) copy-start(s32[1,1,16]{2,1,0:T(1,128)} %param.21) | copy-start | bytes 196
  7.2 97.5 %all-gather.2.cloned.1.call-start = ((), (), s32[]{:S(2)}) async-start(), calls=%async_computation.3 | async-start | bytes 8912896 | tf_op jit(solution)/shard_map/all_gather | solution.py:321
  11.8 2.3 copy-start.7
  22.2 6.3 %copy-start.8 = (s32[1,1,16,32]{3,2,1,0:T(8,128)S(1)}, s32[1,1,16,32]{3,2,1,0:T(8,128)}, u32[]{:S(2)}) copy-start(s32[1,1,16,32]{3,2,1,0:T(8,128)} %param.17) | copy-start | bytes 6148
  22.2 7.0 %copy-start.9 = (s32[1,1,16,32]{3,2,1,0:T(8,128)S(1)}, s32[1,1,16,32]{3,2,1,0:T(8,128)}, u32[]{:S(2)}) copy-start(s32[1,1,16,32]{3,2,1,0:T(8,128)} %param.18) | copy-start | bytes 6148
  22.2 7.7 %copy-start.10 = (s32[1024]{0:T(1024)S(1)}, s32[1024]{0:T(1024)}, u32[]{:S(2)}) copy-start(s32[1024]{0:T(1024)} %param.15) | copy-start | bytes 12292
  22.2 7.7 %copy-start.12 = (s32[8,1,16]{2,1,0:T(1,128)S(1)}, s32[8,1,16]{2,1,0:T(1,128)}, u32[]{:S(2)}) copy-start(s32[8,1,16]{2,1,0:T(1,128)} %param.23) | copy-start | bytes 1540
  22.2 33.4 %all-to-all-start = ((bf16[8,4,128,256]{3,1,2,0:T(4,128)(2,1)}), bf16[8,4,128,256]{3,1,2,0:T(4,128)(2,1)S(1)}, u32[]{:S(2)}, u32[]{:S(2)}) async-start(bf16[8,4,128,256]{3,1,2,0:T(4,128)(2,1)} %copy.58), calls=%async_computation | async-start | bytes 4194304 | tf_op jit(solution)/shard_map/all_to_all | solution.py:346
  104.7 23.7 %copy-start.4 = (f32[8,128,256]{2,0,1:T(8,128)S(1)}, f32[8,128,256]{2,0,1:T(8,128)}, u32[]{:S(2)}) copy-start(f32[8,128,256]{2,0,1:T(8,128)} %convolution_bitcast_fusion.1) | copy-start | bytes 3145732
  128.4 1.7 copy-start.5
  131.5 28.2 %copy-start.2 = (bf16[1024,256]{1,0:T(8,128)(2,1)S(1)}, bf16[1024,256]{1,0:T(8,128)(2,1)}, u32[]{:S(2)}) copy-start(bf16[1024,256]{1,0:T(8,128)(2,1)} %get-tuple-element.7) | copy-start | bytes 1572868
  159.6 13.5 %collective-permute-start = (f32[8,8,128,256]{3,2,1,0:T(8,128)}, f32[8,8,128,256]{3,2,1,0:T(8,128)}, u32[]{:S(2)}, u32[]{:S(2)}) collective-permute-start(f32[8,8,128,256]{3,2,1,0:T(8,128)} %get-tuple-element.6), channel_id=1, source_target_pairs={{0,1},{1,0},{2,3},{3,2},{4,5},{5,4},{6,7},{7,6},{8,9},{9,8},{10,11... | collective-permute-start | bytes 25165832 | tf_op jit(solution)/shard_map/ppermute | solution.py:365
  162.2 30.7 %all-to-all-start.2 = ((bf16[8,4,128,256]{3,2,1,0:T(8,128)(2,1)}), bf16[8,4,128,256]{3,2,1,0:T(8,128)(2,1)S(1)}, u32[]{:S(2)}, u32[]{:S(2)}) async-start(bf16[8,4,128,256]{3,2,1,0:T(8,128)(2,1)} %copy.63), calls=%async_computation.2 | async-start | bytes 4194304 | tf_op jit(solution)/shard_map/all_to_all | solution.py:378
  192.8 55.6 %all-to-all-start.1 = ((bf16[8,8,128,256]{3,2,1,0:T(8,128)(2,1)}), bf16[8,8,128,256]{3,2,1,0:T(8,128)(2,1)}, u32[]{:S(2)}, u32[]{:S(2)}) async-start(bf16[8,8,128,256]{3,2,1,0:T(8,128)(2,1)} %add_convert_fusion), calls=%async_computation.1 | async-start | bytes 8388608 | tf_op jit(solution)/shard_map/all_to_all | solution.py:367
  201.5 50.0 %copy-start.1 = (f32[16,128,256]{2,0,1:T(8,128)S(1)}, f32[16,128,256]{2,0,1:T(8,128)}, u32[]{:S(2)}) copy-start(f32[16,128,256]{2,0,1:T(8,128)} %copy.66) | copy-start | bytes 6291460
  251.5 1.5 copy-start.6
  251.5 2.6 copy-start.3
Sparse Core Ops, SparseCore 0:
  11.0 93.5 all-gather.1

commit v11 on v10

--- a/solution.py
+++ b/solution.py
@@ -9,7 +9,7 @@
 from jax.sharding import PartitionSpec as P
 
 
-UNROLL = 8
+UNROLL = 16
 
 
 def grouped_slots(count, slots, visit):

time: 303 us -> 299 us (0.987)
  Pallas kernels: 89.5 us -> 84.6 us
    pallas_call x1, Pallas kernels: 28.2 us -> 24 us  [tile_backward(): pl.pallas_call(backward_kernel, out_shape=(part, part), grid_spec=grid_sp...]
where the time goes in v11:
time: 299 us; the launch traced here: 298 us
  waiting for transfers between devices  137 us (46%)
  Pallas kernels  84.6 us (28%)
  other arithmetic  17.3 us (6%)
  local copies, waits for them, and re-layouts  16.2 us (5%)
  starting transfers between devices  15.4 us (5%)
  between operations  14.3 us (5%)
  matrix products  12.5 us (4%)
    all_to_all x1, waiting for transfers between devices, local(): lax.all_to_all(pair_sum, 'blk', split_axis=0, concat_axis=0, tiled=True,...  47.1 us
    all_gather x1, waiting for transfers between devices, local(): panels = lax.all_gather(proj, 'blk', axis=0, tiled=True)  46.7 us
    pallas_call x1, Pallas kernels, weight_sum(): pl.pallas_call(functools.partial(weight_sum_kernel, n_grp, n_blk), out_sh...  39.3 us
    all_to_all x1, waiting for transfers between devices, local(): lax.all_to_all(send_buf, 'grp', split_axis=0, concat_axis=0, tiled=True)  25.5 us
    pallas_call x1, Pallas kernels, tile_backward(): pl.pallas_call(backward_kernel, out_shape=(part, part), grid_spec=grid_sp...  24 us
    pallas_call x1, Pallas kernels, tile_forward(): pl.pallas_call(forward_kernel, out_shape=jax.ShapeDtypeStruct((row_tiles,...  21.3 us
    all_to_all x1, waiting for transfers between devices, local(): lax.all_to_all(back_send, 'grp', split_axis=0, concat_axis=0, tiled=True)  11.3 us
    convert_element_type x1, other arithmetic, local(): pair_sum = (keep + from_sibling).astype(jnp.bfloat16)  9.21 us
  transfers between devices with their start and end apart: 5, of which 5 were waited for; matrix products, arithmetic and copies ran while one was open for 11% of the time, Pallas kernels for 0%

profile of v11, /device:TPU:1, one launch (start us, length us, event | category | flops | bytes accessed | tf_op | source)
XLA Modules:
  0.0 297.5 jit_solution(4920580282897752418)
XLA Ops:
  7.2 2.2 convolution_convert_fusion.4
  10.1 1.7 gather_fusion
  12.4 1.7 copy.57
  14.4 2.0 convolution_convert_fusion
  16.5 2.1 reshape.109
  18.5 3.7 %copy.58 = bf16[8,4,128,256]{3,1,2,0:T(4,128)(2,1)} copy(bf16[8,4,128,256]{3,1,0,2:T(4,128)(2,1)} %reshape.109) | data formatting | bytes 4194304 | tf_op jit(solution)/shard_map/reshape | solution.py:345
  22.2 6.3 %all-to-all-start = ((bf16[8,4,128,256]{3,1,2,0:T(4,128)(2,1)}), bf16[8,4,128,256]{3,1,2,0:T(4,128)(2,1)S(1)}, u32[]{:S(2)}, u32[]{:S(2)}) async-start(bf16[8,4,128,256]{3,1,2,0:T(4,128)(2,1)} %copy.58), calls=%async_computation | async-start | bytes 4194304 | tf_op jit(solution)/shard_map/all_to_all | solution.py:346
  29.2 0.7 reshape_squeeze.7.cols_ref
  30.1 25.5 %all-to-all-done = bf16[8,4,128,256]{3,1,2,0:T(4,128)(2,1)S(1)} async-done(((bf16[8,4,128,256]{3,1,2,0:T(4,128)(2,1)}), bf16[8,4,128,256]{3,1,2,0:T(4,128)(2,1)S(1)}, u32[]{:S(2)}, u32[]{:S(2)}) %all-to-all-start) | async-done | bytes 2097184 | tf_op jit(solution)/shard_map/all_to_all | solution.py:346
  55.6 2.3 convolution_bitcast_fusion.1
  58.0 46.7 %all-gather.2.cloned.1.call-done = bf16[16384,256]{1,0:T(8,128)(2,1)} async-done(((bf16[1024,256]{1,0:T(8,128)(2,1)}), bf16[16384,256]{1,0:T(8,128)(2,1)}) %all-gather.2.cloned.1.call-update) | async-done | bytes 8388624 | tf_op jit(solution)/shard_map/all_gather | solution.py:321
  104.7 21.3 %shard_map.139 = f32[8,128,256]{2,1,0:T(8,128)} custom-call(s32[512]{0:T(512)} %reshape_squeeze.6.rows_ref, s32[512]{0:T(512)} %reshape_squeeze.7.cols_ref, s32[16]{0:T(128)} %bitcast.105, bf16[16,32,128,128]{3,2,1,0:T(8,128)(2,1)} %bitcast.93, bf16[16,8,128,256]{3,2,1,0:T(8,128)(2,1)} %bitcast.96), custom_call_target="tpu_custom_call" | custom-call | flops 4294967296 | bytes 25165824 | tf_op jit(solution)/shard_map/pallas_call | solution.py:98
  126.0 1.7 copy_add_fusion.1
  127.7 1.4 fusion.13
  129.1 24.0 %shard_map.140 = (f32[8,8,128,256]{3,2,1,0:T(8,128)}, f32[8,8,128,256]{3,2,1,0:T(8,128)}) custom-call(s32[512]{0:T(512)} %reshape_squeeze.6.rows_ref, s32[512]{0:T(512)} %reshape_squeeze.7.cols_ref, s32[16]{0:T(128)} %bitcast.106, s32[1]{0:T(128)} %bitcast.18.core_ref, bf16[16,32,128,128]{3,2,1,0:T(8,128)(2,1)} %bitcast.94, bf16[8,128,256]{2,1,0:T(8,128)(2,1)} %bitcast.98), custom_call_target="tpu_custom_call" | custom-call | flops 4294967296 | bytes 33554432 | tf_op jit(solution)/shard_map/pallas_call | solution.py:131
  153.3 0.7 convolution_convert_fusion.1
  154.0 1.9 copy.63
  155.8 4.1 %all-to-all-start.2 = ((bf16[8,4,128,256]{3,2,1,0:T(8,128)(2,1)}), bf16[8,4,128,256]{3,2,1,0:T(8,128)(2,1)S(1)}, u32[]{:S(2)}, u32[]{:S(2)}) async-start(bf16[8,4,128,256]{3,2,1,0:T(8,128)(2,1)} %copy.63), calls=%async_computation.2 | async-start | bytes 4194304 | tf_op jit(solution)/shard_map/all_to_all | solution.py:378
  160.0 6.6 %collective-permute-done = f32[8,8,128,256]{3,2,1,0:T(8,128)} collective-permute-done((f32[8,8,128,256]{3,2,1,0:T(8,128)}, f32[8,8,128,256]{3,2,1,0:T(8,128)}, u32[]{:S(2)}, u32[]{:S(2)}) %collective-permute-start) | collective-permute-done | bytes 8388640 | tf_op jit(solution)/shard_map/ppermute | solution.py:365
  166.6 9.2 %add_convert_fusion = bf16[8,8,128,256]{3,2,1,0:T(8,128)(2,1)} fusion(f32[8,8,128,256]{3,2,1,0:T(8,128)} %get-tuple-element.5, f32[8,8,128,256]{3,2,1,0:T(8,128)} %collective-permute-done), kind=kLoop, calls=%fused_computation.2 | loop fusion | flops 4194304 | bytes 20971520 | tf_op jit(solution)/shard_map/convert_element_type | solution.py:366
  175.8 11.3 %all-to-all-done.2 = bf16[8,4,128,256]{3,2,1,0:T(8,128)(2,1)S(1)} async-done(((bf16[8,4,128,256]{3,2,1,0:T(8,128)(2,1)}), bf16[8,4,128,256]{3,2,1,0:T(8,128)(2,1)S(1)}, u32[]{:S(2)}, u32[]{:S(2)}) %all-to-all-start.2) | async-done | bytes 2097184 | tf_op jit(solution)/shard_map/all_to_all | solution.py:378
  187.1 4.7 %all-to-all-start.1 = ((bf16[8,8,128,256]{3,2,1,0:T(8,128)(2,1)}), bf16[8,8,128,256]{3,2,1,0:T(8,128)(2,1)}, u32[]{:S(2)}, u32[]{:S(2)}) async-start(bf16[8,8,128,256]{3,2,1,0:T(8,128)(2,1)} %add_convert_fusion), calls=%async_computation.1 | async-start | bytes 8388608 | tf_op jit(solution)/shard_map/all_to_all | solution.py:367
  191.8 1.3 fusion.2
  193.6 2.1 copy.66
  195.7 47.1 %all-to-all-done.1 = bf16[8,8,128,256]{3,2,1,0:T(8,128)(2,1)} async-done(((bf16[8,8,128,256]{3,2,1,0:T(8,128)(2,1)}), bf16[8,8,128,256]{3,2,1,0:T(8,128)(2,1)}, u32[]{:S(2)}, u32[]{:S(2)}) %all-to-all-start.1) | async-done | bytes 4194336 | tf_op jit(solution)/shard_map/all_to_all | solution.py:367
  242.8 3.0 %convert_reduce_fusion = f32[8,128,256]{2,1,0:T(8,128)S(1)} fusion(bf16[8,8,128,256]{3,2,1,0:T(8,128)(2,1)} %all-to-all-done.1), kind=kLoop, calls=%fused_computation.1 | loop fusion | flops 3932160 | bytes 5242880 | tf_op jit(solution)/shard_map/reduce_sum | solution.py:370
  245.9 1.3 fusion.14
  247.3 1.1 convolution_convert_fusion.3
  248.9 0.7 reshape.114.x_ref
  249.6 39.3 %shard_map.141 = f32[16,32,128]{2,1,0:T(8,128)} custom-call(f32[16,32,128]{2,1,0:T(8,128)} %reshape.114.x_ref), custom_call_target="tpu_custom_call" | custom-call | tf_op jit(solution)/shard_map/pallas_call | solution.py:219
  288.9 1.0 broadcast_multiply_fusion
  289.9 0.8 mul.60
  (44 shorter events, 3.8 us)
Async XLA Ops:
  7.2 4.7 %copy-start = (bf16[1,1,16,128,128]{4,3,2,1,0:T(8,128)(2,1)S(1)}, bf16[1,1,16,128,128]{4,3,2,1,0:T(8,128)(2,1)}, u32[]{:S(2)}) copy-start(bf16[1,1,16,128,128]{4,3,2,1,0:T(8,128)(2,1)} %param.20) | copy-start | bytes 1572868
  7.2 4.6 %copy-start.11 = (s32[1,1,16]{2,1,0:T(1,128)S(1)}, s32[1,1,16]{2,1,0:T(1,128)}, u32[]{:S(2)}) copy-start(s32[1,1,16]{2,1,0:T(1,128)} %param.21) | copy-start | bytes 196
  7.2 97.5 %all-gather.2.cloned.1.call-start = ((), (), s32[]{:S(2)}) async-start(), calls=%async_computation.3 | async-start | bytes 8912896 | tf_op jit(solution)/shard_map/all_gather | solution.py:321
  11.8 2.3 copy-start.7
  22.2 6.3 %copy-start.8 = (s32[1,1,16,32]{3,2,1,0:T(8,128)S(1)}, s32[1,1,16,32]{3,2,1,0:T(8,128)}, u32[]{:S(2)}) copy-start(s32[1,1,16,32]{3,2,1,0:T(8,128)} %param.17) | copy-start | bytes 6148
  22.2 7.0 %copy-start.9 = (s32[1,1,16,32]{3,2,1,0:T(8,128)S(1)}, s32[1,1,16,32]{3,2,1,0:T(8,128)}, u32[]{:S(2)}) copy-start(s32[1,1,16,32]{3,2,1,0:T(8,128)} %param.18) | copy-start | bytes 6148
  22.2 7.7 %copy-start.10 = (s32[1024]{0:T(1024)S(1)}, s32[1024]{0:T(1024)}, u32[]{:S(2)}) copy-start(s32[1024]{0:T(1024)} %param.15) | copy-start | bytes 12292
  22.2 7.7 %copy-start.12 = (s32[8,1,16]{2,1,0:T(1,128)S(1)}, s32[8,1,16]{2,1,0:T(1,128)}, u32[]{:S(2)}) copy-start(s32[8,1,16]{2,1,0:T(1,128)} %param.23) | copy-start | bytes 1540
  22.2 33.4 %all-to-all-start = ((bf16[8,4,128,256]{3,1,2,0:T(4,128)(2,1)}), bf16[8,4,128,256]{3,1,2,0:T(4,128)(2,1)S(1)}, u32[]{:S(2)}, u32[]{:S(2)}) async-start(bf16[8,4,128,256]{3,1,2,0:T(4,128)(2,1)} %copy.58), calls=%async_computation | async-start | bytes 4194304 | tf_op jit(solution)/shard_map/all_to_all | solution.py:346
  104.7 21.3 %copy-start.4 = (f32[8,128,256]{2,0,1:T(8,128)S(1)}, f32[8,128,256]{2,0,1:T(8,128)}, u32[]{:S(2)}) copy-start(f32[8,128,256]{2,0,1:T(8,128)} %convolution_bitcast_fusion.1) | copy-start | bytes 3145732
  126.0 1.7 copy-start.5
  129.1 24.2 %copy-start.2 = (bf16[1024,256]{1,0:T(8,128)(2,1)S(1)}, bf16[1024,256]{1,0:T(8,128)(2,1)}, u32[]{:S(2)}) copy-start(bf16[1024,256]{1,0:T(8,128)(2,1)} %get-tuple-element.7) | copy-start | bytes 1572868
  153.1 13.5 %collective-permute-start = (f32[8,8,128,256]{3,2,1,0:T(8,128)}, f32[8,8,128,256]{3,2,1,0:T(8,128)}, u32[]{:S(2)}, u32[]{:S(2)}) collective-permute-start(f32[8,8,128,256]{3,2,1,0:T(8,128)} %get-tuple-element.6), channel_id=1, source_target_pairs={{0,1},{1,0},{2,3},{3,2},{4,5},{5,4},{6,7},{7,6},{8,9},{9,8},{10,11... | collective-permute-start | bytes 25165832 | tf_op jit(solution)/shard_map/ppermute | solution.py:365
  155.8 31.3 %all-to-all-start.2 = ((bf16[8,4,128,256]{3,2,1,0:T(8,128)(2,1)}), bf16[8,4,128,256]{3,2,1,0:T(8,128)(2,1)S(1)}, u32[]{:S(2)}, u32[]{:S(2)}) async-start(bf16[8,4,128,256]{3,2,1,0:T(8,128)(2,1)} %copy.63), calls=%async_computation.2 | async-start | bytes 4194304 | tf_op jit(solution)/shard_map/all_to_all | solution.py:378
  187.1 55.7 %all-to-all-start.1 = ((bf16[8,8,128,256]{3,2,1,0:T(8,128)(2,1)}), bf16[8,8,128,256]{3,2,1,0:T(8,128)(2,1)}, u32[]{:S(2)}, u32[]{:S(2)}) async-start(bf16[8,8,128,256]{3,2,1,0:T(8,128)(2,1)} %add_convert_fusion), calls=%async_computation.1 | async-start | bytes 8388608 | tf_op jit(solution)/shard_map/all_to_all | solution.py:367
  195.7 50.1 %copy-start.1 = (f32[16,128,256]{2,0,1:T(8,128)S(1)}, f32[16,128,256]{2,0,1:T(8,128)}, u32[]{:S(2)}) copy-start(f32[16,128,256]{2,0,1:T(8,128)} %copy.66) | copy-start | bytes 6291460
  245.8 1.5 copy-start.6
  245.9 2.6 copy-start.3
Sparse Core Ops, SparseCore 0:
  11.0 93.5 all-gather.1

commit v12 on v11

--- a/solution.py
+++ b/solution.py
@@ -79,7 +79,7 @@
 
     @pl.when(p == 1)
     def _():
-        send_ref[0] = acc_ref[...]
+        send_ref[0] = acc_ref[...].astype(send_ref.dtype)
 
 
 def tile_forward(rows, cols, count, vals, panels):
@@ -128,9 +128,10 @@
     )
     flops = 2 * n_src * slots * tile * tile * width
     part = jax.ShapeDtypeStruct((half, row_tiles, tile, width), jnp.float32)
+    part_out = jax.ShapeDtypeStruct((half, row_tiles, tile, width), jnp.bfloat16)
     return pl.pallas_call(
         backward_kernel,
-        out_shape=(part, part),
+        out_shape=(part, part_out),
         grid_spec=grid_spec,
         cost_estimate=pl.CostEstimate(
             flops=flops, transcendentals=0, bytes_accessed=vals.size * 2 + n_src * row_tiles * tile * width * 4
@@ -363,7 +364,7 @@
 
     keep, send = tile_backward(dev_rows, dev_cols, dev_count, dev_vals, grad_tiles, core.reshape(1))
     from_sibling = lax.ppermute(send, "blk", sibling)
-    pair_sum = (keep + from_sibling).astype(jnp.bfloat16)
+    pair_sum = (keep + from_sibling.astype(jnp.float32)).astype(jnp.bfloat16)
     received_parts = lax.all_to_all(
         pair_sum, "blk", split_axis=0, concat_axis=0, tiled=True, axis_index_groups=core_groups
     )

time: 299 us -> 295 us (0.987)
  Pallas kernels: 84.6 us -> 80.7 us
    all_to_all x1, waiting for transfers between devices: 11.3 us -> 18.7 us  [local(): lax.all_to_all(back_send, 'grp', split_axis=0, concat_axis=0, tiled=True)]
    ppermute x1, waiting for transfers between devices: 6.64 us -> 0.3 us  [local(): from_sibling = lax.ppermute(send, 'blk', sibling)]
where the time goes in v12:
time: 295 us; the launch traced here: 294 us
  waiting for transfers between devices  138 us (47%)
  Pallas kernels  80.7 us (27%)
  local copies, waits for them, and re-layouts  16.2 us (5%)
  other arithmetic  16.2 us (5%)
  starting transfers between devices  15.8 us (5%)
  between operations  14.3 us (5%)
  matrix products  12.5 us (4%)
    all_to_all x1, waiting for transfers between devices, local(): lax.all_to_all(pair_sum, 'blk', split_axis=0, concat_axis=0, tiled=True,...  47 us
    all_gather x1, waiting for transfers between devices, local(): panels = lax.all_gather(proj, 'blk', axis=0, tiled=True)  46.7 us
    pallas_call x1, Pallas kernels, weight_sum(): pl.pallas_call(functools.partial(weight_sum_kernel, n_grp, n_blk), out_sh...  36.4 us
    all_to_all x1, waiting for transfers between devices, local(): lax.all_to_all(send_buf, 'grp', split_axis=0, concat_axis=0, tiled=True)  25.5 us
    pallas_call x1, Pallas kernels, tile_backward(): pl.pallas_call(backward_kernel, out_shape=(part, part_out), grid_spec=gri...  23.3 us
    pallas_call x1, Pallas kernels, tile_forward(): pl.pallas_call(forward_kernel, out_shape=jax.ShapeDtypeStruct((row_tiles,...  20.9 us
    all_to_all x1, waiting for transfers between devices, local(): lax.all_to_all(back_send, 'grp', split_axis=0, concat_axis=0, tiled=True)  18.7 us
    convert_element_type x1, other arithmetic, local(): pair_sum = (keep + from_sibling.astype(jnp.float32)).astype(jnp.bfloat16)  8.1 us
  transfers between devices with their start and end apart: 5, of which 5 were waited for; matrix products, arithmetic and copies ran while one was open for 11% of the time, Pallas kernels for 0%

profile of v12, /device:TPU:1, one launch (start us, length us, event | category | flops | bytes accessed | tf_op | source)
XLA Modules:
  0.0 293.8 jit_solution(17739925556980047977)
XLA Ops:
  7.2 2.2 convolution_convert_fusion.4
  9.5 0.7 fusion.41
  10.1 1.7 gather_fusion
  12.4 1.7 copy.57
  14.4 2.0 convolution_convert_fusion
  16.5 2.1 reshape.109
  18.5 3.7 %copy.58 = bf16[8,4,128,256]{3,1,2,0:T(4,128)(2,1)} copy(bf16[8,4,128,256]{3,1,0,2:T(4,128)(2,1)} %reshape.109) | data formatting | bytes 4194304 | tf_op jit(solution)/shard_map/reshape | solution.py:346
  22.2 6.3 %all-to-all-start = ((bf16[8,4,128,256]{3,1,2,0:T(4,128)(2,1)}), bf16[8,4,128,256]{3,1,2,0:T(4,128)(2,1)S(1)}, u32[]{:S(2)}, u32[]{:S(2)}) async-start(bf16[8,4,128,256]{3,1,2,0:T(4,128)(2,1)} %copy.58), calls=%async_computation | async-start | bytes 4194304 | tf_op jit(solution)/shard_map/all_to_all | solution.py:347
  29.2 0.7 reshape_squeeze.7.cols_ref
  30.1 25.5 %all-to-all-done = bf16[8,4,128,256]{3,1,2,0:T(4,128)(2,1)S(1)} async-done(((bf16[8,4,128,256]{3,1,2,0:T(4,128)(2,1)}), bf16[8,4,128,256]{3,1,2,0:T(4,128)(2,1)S(1)}, u32[]{:S(2)}, u32[]{:S(2)}) %all-to-all-start) | async-done | bytes 2097184 | tf_op jit(solution)/shard_map/all_to_all | solution.py:347
  55.6 2.3 convolution_bitcast_fusion.1
  58.0 46.7 %all-gather.2.cloned.1.call-done = bf16[16384,256]{1,0:T(8,128)(2,1)} async-done(((bf16[1024,256]{1,0:T(8,128)(2,1)}), bf16[16384,256]{1,0:T(8,128)(2,1)}) %all-gather.2.cloned.1.call-update) | async-done | bytes 8388624 | tf_op jit(solution)/shard_map/all_gather | solution.py:322
  104.7 20.9 %shard_map.139 = f32[8,128,256]{2,1,0:T(8,128)} custom-call(s32[512]{0:T(512)} %reshape_squeeze.6.rows_ref, s32[512]{0:T(512)} %reshape_squeeze.7.cols_ref, s32[16]{0:T(128)} %bitcast.105, bf16[16,32,128,128]{3,2,1,0:T(8,128)(2,1)} %bitcast.93, bf16[16,8,128,256]{3,2,1,0:T(8,128)(2,1)} %bitcast.96), custom_call_target="tpu_custom_call" | custom-call | flops 4294967296 | bytes 25165824 | tf_op jit(solution)/shard_map/pallas_call | solution.py:98
  125.6 1.7 copy_add_fusion.1
  127.3 1.4 fusion.13
  128.7 23.3 %shard_map.140 = (f32[8,8,128,256]{3,2,1,0:T(8,128)}, bf16[8,8,128,256]{3,2,1,0:T(8,128)(2,1)}) custom-call(s32[512]{0:T(512)} %reshape_squeeze.6.rows_ref, s32[512]{0:T(512)} %reshape_squeeze.7.cols_ref, s32[16]{0:T(128)} %bitcast.106, s32[1]{0:T(128)} %bitcast.18.core_ref, bf16[16,32,128,128]{3,2,1,0:T(8,128)(2,1)} %bitcast.94, bf16[8,128,256]{2,1,0:T(8,128)(2,1)} %bitcast.98), custom_call_target="tpu_custom_call" | custom-call | flops 4294967296 | bytes 33554432 | tf_op jit(solution)/shard_map/pallas_call | solution.py:132
  152.1 0.7 convolution_convert_fusion.1
  152.7 1.8 copy.63
  154.6 4.7 %all-to-all-start.2 = ((bf16[8,4,128,256]{3,2,1,0:T(8,128)(2,1)}), bf16[8,4,128,256]{3,2,1,0:T(8,128)(2,1)S(1)}, u32[]{:S(2)}, u32[]{:S(2)}) async-start(bf16[8,4,128,256]{3,2,1,0:T(8,128)(2,1)} %copy.63), calls=%async_computation.2 | async-start | bytes 4194304 | tf_op jit(solution)/shard_map/all_to_all | solution.py:379
  159.5 8.1 %add_convert_fusion = bf16[8,8,128,256]{3,2,1,0:T(8,128)(2,1)} fusion(f32[8,8,128,256]{3,2,1,0:T(8,128)} %get-tuple-element.5, bf16[8,8,128,256]{3,2,1,0:T(8,128)(2,1)} %collective-permute-done), kind=kLoop, calls=%fused_computation.2 | loop fusion | flops 6291456 | bytes 16777216 | tf_op jit(solution)/shard_map/convert_element_type | solution.py:367
  167.6 18.7 %all-to-all-done.2 = bf16[8,4,128,256]{3,2,1,0:T(8,128)(2,1)S(1)} async-done(((bf16[8,4,128,256]{3,2,1,0:T(8,128)(2,1)}), bf16[8,4,128,256]{3,2,1,0:T(8,128)(2,1)S(1)}, u32[]{:S(2)}, u32[]{:S(2)}) %all-to-all-start.2) | async-done | bytes 2097184 | tf_op jit(solution)/shard_map/all_to_all | solution.py:379
  186.3 4.7 %all-to-all-start.1 = ((bf16[8,8,128,256]{3,2,1,0:T(8,128)(2,1)}), bf16[8,8,128,256]{3,2,1,0:T(8,128)(2,1)}, u32[]{:S(2)}, u32[]{:S(2)}) async-start(bf16[8,8,128,256]{3,2,1,0:T(8,128)(2,1)} %add_convert_fusion), calls=%async_computation.1 | async-start | bytes 8388608 | tf_op jit(solution)/shard_map/all_to_all | solution.py:368
  191.1 1.3 fusion.2
  192.9 2.1 copy.66
  195.0 47.0 %all-to-all-done.1 = bf16[8,8,128,256]{3,2,1,0:T(8,128)(2,1)} async-done(((bf16[8,8,128,256]{3,2,1,0:T(8,128)(2,1)}), bf16[8,8,128,256]{3,2,1,0:T(8,128)(2,1)}, u32[]{:S(2)}, u32[]{:S(2)}) %all-to-all-start.1) | async-done | bytes 4194336 | tf_op jit(solution)/shard_map/all_to_all | solution.py:368
  241.9 3.0 %convert_reduce_fusion = f32[8,128,256]{2,1,0:T(8,128)S(1)} fusion(bf16[8,8,128,256]{3,2,1,0:T(8,128)(2,1)} %all-to-all-done.1), kind=kLoop, calls=%fused_computation.1 | loop fusion | flops 3932160 | bytes 5242880 | tf_op jit(solution)/shard_map/reduce_sum | solution.py:371
  245.0 1.3 fusion.14
  246.4 1.1 convolution_convert_fusion.3
  248.0 0.7 reshape.114.x_ref
  248.8 36.4 %shard_map.141 = f32[16,32,128]{2,1,0:T(8,128)} custom-call(f32[16,32,128]{2,1,0:T(8,128)} %reshape.114.x_ref), custom_call_target="tpu_custom_call" | custom-call | tf_op jit(solution)/shard_map/pallas_call | solution.py:220
  285.2 1.0 broadcast_multiply_fusion
  286.2 0.8 mul.60
  (44 shorter events, 3.2 us)
Async XLA Ops:
  7.2 4.7 %copy-start = (bf16[1,1,16,128,128]{4,3,2,1,0:T(8,128)(2,1)S(1)}, bf16[1,1,16,128,128]{4,3,2,1,0:T(8,128)(2,1)}, u32[]{:S(2)}) copy-start(bf16[1,1,16,128,128]{4,3,2,1,0:T(8,128)(2,1)} %param.20) | copy-start | bytes 1572868
  7.2 4.6 %copy-start.11 = (s32[1,1,16]{2,1,0:T(1,128)S(1)}, s32[1,1,16]{2,1,0:T(1,128)}, u32[]{:S(2)}) copy-start(s32[1,1,16]{2,1,0:T(1,128)} %param.21) | copy-start | bytes 196
  7.2 97.5 %all-gather.2.cloned.1.call-start = ((), (), s32[]{:S(2)}) async-start(), calls=%async_computation.3 | async-start | bytes 8912896 | tf_op jit(solution)/shard_map/all_gather | solution.py:322
  11.8 2.3 copy-start.7
  22.2 6.3 %copy-start.8 = (s32[1,1,16,32]{3,2,1,0:T(8,128)S(1)}, s32[1,1,16,32]{3,2,1,0:T(8,128)}, u32[]{:S(2)}) copy-start(s32[1,1,16,32]{3,2,1,0:T(8,128)} %param.17) | copy-start | bytes 6148
  22.2 7.0 %copy-start.9 = (s32[1,1,16,32]{3,2,1,0:T(8,128)S(1)}, s32[1,1,16,32]{3,2,1,0:T(8,128)}, u32[]{:S(2)}) copy-start(s32[1,1,16,32]{3,2,1,0:T(8,128)} %param.18) | copy-start | bytes 6148
  22.2 7.7 %copy-start.10 = (s32[1024]{0:T(1024)S(1)}, s32[1024]{0:T(1024)}, u32[]{:S(2)}) copy-start(s32[1024]{0:T(1024)} %param.15) | copy-start | bytes 12292
  22.2 7.7 %copy-start.12 = (s32[8,1,16]{2,1,0:T(1,128)S(1)}, s32[8,1,16]{2,1,0:T(1,128)}, u32[]{:S(2)}) copy-start(s32[8,1,16]{2,1,0:T(1,128)} %param.23) | copy-start | bytes 1540
  22.2 33.4 %all-to-all-start = ((bf16[8,4,128,256]{3,1,2,0:T(4,128)(2,1)}), bf16[8,4,128,256]{3,1,2,0:T(4,128)(2,1)S(1)}, u32[]{:S(2)}, u32[]{:S(2)}) async-start(bf16[8,4,128,256]{3,1,2,0:T(4,128)(2,1)} %copy.58), calls=%async_computation | async-start | bytes 4194304 | tf_op jit(solution)/shard_map/all_to_all | solution.py:347
  104.7 20.9 %copy-start.4 = (f32[8,128,256]{2,0,1:T(8,128)S(1)}, f32[8,128,256]{2,0,1:T(8,128)}, u32[]{:S(2)}) copy-start(f32[8,128,256]{2,0,1:T(8,128)} %convolution_bitcast_fusion.1) | copy-start | bytes 3145732
  125.6 1.7 copy-start.5
  128.7 23.4 %copy-start.2 = (bf16[1024,256]{1,0:T(8,128)(2,1)S(1)}, bf16[1024,256]{1,0:T(8,128)(2,1)}, u32[]{:S(2)}) copy-start(bf16[1024,256]{1,0:T(8,128)(2,1)} %get-tuple-element.7) | copy-start | bytes 1572868
  152.0 7.5 %collective-permute-start = (bf16[8,8,128,256]{3,2,1,0:T(8,128)(2,1)}, bf16[8,8,128,256]{3,2,1,0:T(8,128)(2,1)}, u32[]{:S(2)}, u32[]{:S(2)}) collective-permute-start(bf16[8,8,128,256]{3,2,1,0:T(8,128)(2,1)} %get-tuple-element.6), channel_id=1, source_target_pairs={{0,1},{1,0},{2,3},{3,2},{4,5},{5,4},{6,7},{7,6},{8,9},{9,8},{10,11... | collective-permute-start | bytes 12582920 | tf_op jit(solution)/shard_map/ppermute | solution.py:366
  154.6 31.8 %all-to-all-start.2 = ((bf16[8,4,128,256]{3,2,1,0:T(8,128)(2,1)}), bf16[8,4,128,256]{3,2,1,0:T(8,128)(2,1)S(1)}, u32[]{:S(2)}, u32[]{:S(2)}) async-start(bf16[8,4,128,256]{3,2,1,0:T(8,128)(2,1)} %copy.63), calls=%async_computation.2 | async-start | bytes 4194304 | tf_op jit(solution)/shard_map/all_to_all | solution.py:379
  186.3 55.6 %all-to-all-start.1 = ((bf16[8,8,128,256]{3,2,1,0:T(8,128)(2,1)}), bf16[8,8,128,256]{3,2,1,0:T(8,128)(2,1)}, u32[]{:S(2)}, u32[]{:S(2)}) async-start(bf16[8,8,128,256]{3,2,1,0:T(8,128)(2,1)} %add_convert_fusion), calls=%async_computation.1 | async-start | bytes 8388608 | tf_op jit(solution)/shard_map/all_to_all | solution.py:368
  195.0 50.0 %copy-start.1 = (f32[16,128,256]{2,0,1:T(8,128)S(1)}, f32[16,128,256]{2,0,1:T(8,128)}, u32[]{:S(2)}) copy-start(f32[16,128,256]{2,0,1:T(8,128)} %copy.66) | copy-start | bytes 6291460
  245.0 1.5 copy-start.6
  245.0 2.6 copy-start.3
Sparse Core Ops, SparseCore 0:
  11.0 93.5 all-gather.1

commit v13 on v12

--- a/solution.py
+++ b/solution.py
@@ -370,17 +370,25 @@
     )
     grad_sum = jnp.sum(received_parts.astype(jnp.float32), axis=0)
 
+    rotation = (my_group + jnp.arange(n_groups, dtype=jnp.int32)) % n_groups
     back_send = jnp.einsum(
         "scr,rif->scif",
-        routing.astype(jnp.bfloat16),
+        jnp.take(routing, rotation, axis=0).astype(jnp.bfloat16),
         grad_tiles,
         preferred_element_type=jnp.float32,
     ).astype(jnp.bfloat16)
-    back_recv = lax.all_to_all(back_send, "grp", split_axis=0, concat_axis=0, tiled=True)
-    back_flat = back_recv.reshape(n_groups * capacity, tile_size, width)
+    pieces = [back_send[0]] + [
+        lax.ppermute(back_send[k], "grp", [(i, (i + k) % n_groups) for i in range(n_groups)])
+        for k in range(1, n_groups)
+    ]
+    back_flat = jnp.stack(pieces).reshape(n_groups * capacity, tile_size, width)
+    back_slot = ((my_group - my_dest) % n_groups) * capacity + my_rank
+    back_place = (
+        back_slot[:, None] == jnp.arange(n_groups * capacity, dtype=jnp.int32)[None, :]
+    ).astype(jnp.bfloat16)
     own_pick = jnp.einsum(
         "hs,sif->hif",
-        send_place.astype(jnp.bfloat16),
+        back_place,
         back_flat,
         preferred_element_type=jnp.float32,
     ).astype(jnp.bfloat16)

time: 295 us -> 304 us (1.031)
  local copies, waits for them, and re-layouts: 16.2 us -> 38.9 us
  Pallas kernels: 80.7 us -> 71.4 us
  waiting for transfers between devices: 138 us -> 130 us
  starting transfers between devices: 15.8 us -> 19 us
    ppermute x0 -> x7, waiting for transfers between devices: none -> 50.8 us  [local(): lax.ppermute(back_send[k], 'grp', [(i, (i + k) % n_groups) for i in range...]
    all_to_all x1, waiting for transfers between devices: 47 us -> 0.01 us  [local(): lax.all_to_all(pair_sum, 'blk', split_axis=0, concat_axis=0, tiled=True,...]
    another operation x0 -> x9, local copies, waits for them, and re-layouts: none -> 19.3 us  [local(): back_flat = jnp.stack(pieces).reshape(n_groups * capacity, tile_size, width)]
    all_to_all x1 -> x0, waiting for transfers between devices: 18.7 us -> none  [local(): lax.all_to_all(back_send, 'grp', split_axis=0, concat_axis=0, tiled=True)]
    pallas_call x1, Pallas kernels: 36.4 us -> 27.6 us  [weight_sum(): pl.pallas_call(functools.partial(weight_sum_kernel, n_grp, n_blk), out_sh...]
    ppermute x0 -> x7, starting transfers between devices: none -> 7.8 us  [local(): lax.ppermute(back_send[k], 'grp', [(i, (i + k) % n_groups) for i in range...]
    ppermute x1, waiting for transfers between devices: 0.3 us -> 7.23 us  [local(): from_sibling = lax.ppermute(send, 'blk', sibling)]
    all_to_all x1 -> x0, starting transfers between devices: 4.7 us -> none  [local(): lax.all_to_all(back_send, 'grp', split_axis=0, concat_axis=0, tiled=True)]
  transfers between devices with their start and end apart: 5 -> 11, of which waited for: 5 -> 6; matrix products, arithmetic and copies ran while one was open for 11% -> 15% of each run, Pallas kernels for 0% -> 0%
where the time goes in v13:
time: 304 us; the launch traced here: 301 us
  waiting for transfers between devices  130 us (43%)
  Pallas kernels  71.4 us (23%)
  local copies, waits for them, and re-layouts  38.9 us (13%)
  starting transfers between devices  19 us (6%)
  other arithmetic  15.1 us (5%)
  between operations  14.3 us (5%)
  matrix products  12.5 us (4%)
    ppermute x7, waiting for transfers between devices, local(): lax.ppermute(back_send[k], 'grp', [(i, (i + k) % n_groups) for i in range...  50.8 us
    all_gather x1, waiting for transfers between devices, local(): panels = lax.all_gather(proj, 'blk', axis=0, tiled=True)  46.6 us
    pallas_call x1, Pallas kernels, weight_sum(): pl.pallas_call(functools.partial(weight_sum_kernel, n_grp, n_blk), out_sh...  27.6 us
    all_to_all x1, waiting for transfers between devices, local(): lax.all_to_all(send_buf, 'grp', split_axis=0, concat_axis=0, tiled=True)  25.5 us
    pallas_call x1, Pallas kernels, tile_backward(): pl.pallas_call(backward_kernel, out_shape=(part, part_out), grid_spec=gri...  23.7 us
    pallas_call x1, Pallas kernels, tile_forward(): pl.pallas_call(forward_kernel, out_shape=jax.ShapeDtypeStruct((row_tiles,...  20.2 us
    another operation x9, local copies, waits for them, and re-layouts, local(): back_flat = jnp.stack(pieces).reshape(n_groups * capacity, tile_size, width)  19.3 us
    ppermute x7, starting transfers between devices, local(): lax.ppermute(back_send[k], 'grp', [(i, (i + k) % n_groups) for i in range...  7.8 us
  transfers between devices with their start and end apart: 11, of which 6 were waited for; matrix products, arithmetic and copies ran while one was open for 15% of the time, Pallas kernels for 0%

profile of v13, /device:TPU:1, one launch (start us, length us, event | category | flops | bytes accessed | tf_op | source)
XLA Modules:
  0.0 301.4 jit_solution(7711046747476447082)
XLA Ops:
  7.2 2.2 convolution_convert_fusion.4
  10.1 1.7 gather_fusion
  12.4 1.7 copy.154
  14.4 2.0 convolution_convert_fusion
  16.5 2.1 reshape.187
  18.6 3.7 %copy.155 = bf16[8,4,128,256]{3,1,2,0:T(4,128)(2,1)} copy(bf16[8,4,128,256]{3,1,0,2:T(4,128)(2,1)} %reshape.187) | data formatting | bytes 4194304 | tf_op jit(solution)/shard_map/reshape | solution.py:346
  22.3 6.3 %all-to-all-start = ((bf16[8,4,128,256]{3,1,2,0:T(4,128)(2,1)}), bf16[8,4,128,256]{3,1,2,0:T(4,128)(2,1)S(1)}, u32[]{:S(2)}, u32[]{:S(2)}) async-start(bf16[8,4,128,256]{3,1,2,0:T(4,128)(2,1)} %copy.155), calls=%async_computation | async-start | bytes 4194304 | tf_op jit(solution)/shard_map/all_to_all | solution.py:347
  30.1 25.5 %all-to-all-done = bf16[8,4,128,256]{3,1,2,0:T(4,128)(2,1)S(1)} async-done(((bf16[8,4,128,256]{3,1,2,0:T(4,128)(2,1)}), bf16[8,4,128,256]{3,1,2,0:T(4,128)(2,1)S(1)}, u32[]{:S(2)}, u32[]{:S(2)}) %all-to-all-start) | async-done | bytes 2097184 | tf_op jit(solution)/shard_map/all_to_all | solution.py:347
  55.7 2.3 convolution_bitcast_fusion.1
  58.0 46.6 %all-gather.2.cloned.1.call-done = bf16[16384,256]{1,0:T(8,128)(2,1)} async-done(((bf16[1024,256]{1,0:T(8,128)(2,1)}), bf16[16384,256]{1,0:T(8,128)(2,1)}) %all-gather.2.cloned.1.call-update) | async-done | bytes 8388624 | tf_op jit(solution)/shard_map/all_gather | solution.py:322
  104.6 20.2 %shard_map.139 = f32[8,128,256]{2,1,0:T(8,128)} custom-call(s32[512]{0:T(512)} %reshape_squeeze.6.rows_ref, s32[512]{0:T(512)} %reshape_squeeze.7.cols_ref, s32[16]{0:T(128)} %bitcast.154, bf16[16,32,128,128]{3,2,1,0:T(8,128)(2,1)} %bitcast.129, bf16[16,8,128,256]{3,2,1,0:T(8,128)(2,1)} %bitcast.132), custom_call_target="tpu_custom_call" | custom-call | flops 4294967296 | bytes 25165824 | tf_op jit(solution)/shard_map/pallas_call | solution.py:98
  124.8 1.7 copy_add_fusion.1
  126.4 1.4 fusion.13
  127.9 23.7 %shard_map.140 = (f32[8,8,128,256]{3,2,1,0:T(8,128)}, bf16[8,8,128,256]{3,2,1,0:T(8,128)(2,1)}) custom-call(s32[512]{0:T(512)} %reshape_squeeze.6.rows_ref, s32[512]{0:T(512)} %reshape_squeeze.7.cols_ref, s32[16]{0:T(128)} %bitcast.155, s32[1]{0:T(128)} %bitcast.18.core_ref, bf16[16,32,128,128]{3,2,1,0:T(8,128)(2,1)} %bitcast.130, bf16[8,128,256]{2,1,0:T(8,128)(2,1)} %bitcast.134), custom_call_target="tpu_custom_call" | custom-call | flops 4294967296 | bytes 33554432 | tf_op jit(solution)/shard_map/pallas_call | solution.py:132
  151.7 7.2 %collective-permute-done = bf16[8,8,128,256]{3,2,1,0:T(8,128)(2,1)S(1)} collective-permute-done((bf16[8,8,128,256]{3,2,1,0:T(8,128)(2,1)}, bf16[8,8,128,256]{3,2,1,0:T(8,128)(2,1)S(1)}, u32[]{:S(2)}, u32[]{:S(2)}) %collective-permute-start) | collective-permute-done | bytes 4194336 | tf_op jit(solution)/shard_map/ppermute | solution.py:366
  158.9 6.8 %add_convert_fusion = bf16[8,8,128,256]{3,2,1,0:T(8,128)(2,1)} fusion(f32[8,8,128,256]{3,2,1,0:T(8,128)} %get-tuple-element.5, bf16[8,8,128,256]{3,2,1,0:T(8,128)(2,1)S(1)} %collective-permute-done), kind=kLoop, calls=%fused_computation.3 | loop fusion | flops 6291456 | bytes 16777216 | tf_op jit(solution)/shard_map/convert_element_type | solution.py:367
  165.7 4.7 %all-to-all-start.1 = ((bf16[8,8,128,256]{3,2,1,0:T(8,128)(2,1)}), bf16[8,8,128,256]{3,2,1,0:T(8,128)(2,1)}, u32[]{:S(2)}, u32[]{:S(2)}) async-start(bf16[8,8,128,256]{3,2,1,0:T(8,128)(2,1)} %add_convert_fusion), calls=%async_computation.1 | async-start | bytes 8388608 | tf_op jit(solution)/shard_map/all_to_all | solution.py:368
  171.8 4.4 %fusion.54 = (bf16[1,4,128,256]{3,0,2,1:T(2,128)(2,1)S(1)}, bf16[1,4,128,256]{3,0,2,1:T(2,128)(2,1)S(1)}, bf16[1,4,128,256]{3,0,2,1:T(2,128)(2,1)S(1)}, bf16[1,4...) fusion(bf16[8,4,128,256]{3,0,2,1:T(8,128)(2,1)S(1)} %convolutio, ...), kind=kLoop, calls=%fused_computation.103 | loop fusion | bytes 4194304 | tf_op jit(solution)/shard_map/slice | solution.py:381
  176.7 4.6 %collective-permute-start.2 = (bf16[4,128,256]{2,1,0:T(8,128)(2,1)S(1)}, bf16[4,128,256]{2,1,0:T(8,128)(2,1)S(1)}, u32[]{:S(2)}, u32[]{:S(2)}) collective-permute-start(bf16[4,128,256]{2,1,0:T(8,128)(2,1)S(1)} %bitcast.148), channel_id=1, source_target_pairs={{0,32},{16,48},{32,64},{48,80},{64,96},{80,112},{96,0},{112,16},{1... | collective-permute-start | bytes 786440 | tf_op jit(solution)/shard_map/ppermute | solution.py:381
  182.1 1.3 collective-permute-start.4
  184.3 21.9 %collective-permute-done.1 = bf16[4,128,256]{2,1,0:T(8,128)(2,1)S(1)} collective-permute-done((bf16[4,128,256]{2,1,0:T(8,128)(2,1)S(1)}, bf16[4,128,256]{2,1,0:T(8,128)(2,1)S(1)}, u32[]{:S(2)}, u32[]{:S(2)}) %collective-permute-start.1) | collective-permute-done | bytes 262176 | tf_op jit(solution)/shard_map/ppermute | solution.py:381
  207.4 1.2 copy.161
  208.6 5.1 %collective-permute-done.3 = bf16[4,128,256]{2,1,0:T(8,128)(2,1)S(1)} collective-permute-done((bf16[4,128,256]{2,1,0:T(8,128)(2,1)S(1)}, bf16[4,128,256]{2,1,0:T(8,128)(2,1)S(1)}, u32[]{:S(2)}, u32[]{:S(2)}) %collective-permute-start.3) | collective-permute-done | bytes 262176 | tf_op jit(solution)/shard_map/ppermute | solution.py:381
  213.7 1.2 copy.162
  214.9 23.8 %collective-permute-done.4 = bf16[4,128,256]{2,1,0:T(8,128)(2,1)S(1)} collective-permute-done((bf16[4,128,256]{2,1,0:T(8,128)(2,1)S(1)}, bf16[4,128,256]{2,1,0:T(8,128)(2,1)S(1)}, u32[]{:S(2)}, u32[]{:S(2)}) %collective-permute-start.4) | collective-permute-done | bytes 262176 | tf_op jit(solution)/shard_map/ppermute | solution.py:381
  238.7 1.2 copy.163
  243.5 10.4 %stack.31 = bf16[8,4,128,256]{3,0,2,1:T(8,128)(2,1)S(1)} concatenate(bf16[1,4,128,256]{3,0,2,1:T(2,128)(2,1)S(1)} %get-tuple-element.14, bf16[1,4,128,256]{3,0,2,1:T(2,128)(2,1)} %copy.160, bf16[1,4,128,256]{3,0,2,1:T(2,128)(2,1)} %copy.161, bf16[1,4,128,256]{3,0,2,1:T(2,128)(2,1)} %copy.162, bf16[1,4,128,256]{3,0,2,1:T(2,128)(2,1)} %copy.163, bf16[1,4,128,256]{3,0,2,1:T(2,128)(2,1)} %copy.164, ...), dimensions={0} | concatenate | bytes 4194304 | tf_op jit(solution)/shard_map/stack | solution.py:384
  254.4 1.2 fusion.2
  256.2 2.1 copy.170
  258.3 3.2 %convert_reduce_fusion = f32[8,128,256]{2,1,0:T(8,128)S(1)} fusion(bf16[8,8,128,256]{3,2,1,0:T(8,128)(2,1)} %all-to-all-done.1), kind=kLoop, calls=%fused_computation.2 | loop fusion | flops 3932160 | bytes 5242880 | tf_op jit(solution)/shard_map/reduce_sum | solution.py:371
  261.5 1.3 fusion.14
  265.3 27.6 %shard_map.141 = f32[16,32,128]{2,1,0:T(8,128)} custom-call(f32[16,32,128]{2,1,0:T(8,128)} %reshape.192.x_ref), custom_call_target="tpu_custom_call" | custom-call | tf_op jit(solution)/shard_map/pallas_call | solution.py:220
  (77 shorter events, 16.9 us)
Async XLA Ops:
  7.2 4.7 %copy-start = (bf16[1,1,16,128,128]{4,3,2,1,0:T(8,128)(2,1)S(1)}, bf16[1,1,16,128,128]{4,3,2,1,0:T(8,128)(2,1)}, u32[]{:S(2)}) copy-start(bf16[1,1,16,128,128]{4,3,2,1,0:T(8,128)(2,1)} %param.20) | copy-start | bytes 1572868
  7.2 4.6 %copy-start.11 = (s32[1,1,16]{2,1,0:T(1,128)S(1)}, s32[1,1,16]{2,1,0:T(1,128)}, u32[]{:S(2)}) copy-start(s32[1,1,16]{2,1,0:T(1,128)} %param.21) | copy-start | bytes 196
  7.2 97.4 %all-gather.2.cloned.1.call-start = ((), (), s32[]{:S(2)}) async-start(), calls=%async_computation.2 | async-start | bytes 8912896 | tf_op jit(solution)/shard_map/all_gather | solution.py:322
  11.8 2.3 copy-start.7
  22.3 6.4 %copy-start.8 = (s32[1,1,16,32]{3,2,1,0:T(8,128)S(1)}, s32[1,1,16,32]{3,2,1,0:T(8,128)}, u32[]{:S(2)}) copy-start(s32[1,1,16,32]{3,2,1,0:T(8,128)} %param.17) | copy-start | bytes 6148
  22.3 7.0 %copy-start.9 = (s32[1,1,16,32]{3,2,1,0:T(8,128)S(1)}, s32[1,1,16,32]{3,2,1,0:T(8,128)}, u32[]{:S(2)}) copy-start(s32[1,1,16,32]{3,2,1,0:T(8,128)} %param.18) | copy-start | bytes 6148
  22.3 7.7 %copy-start.10 = (s32[1024]{0:T(1024)S(1)}, s32[1024]{0:T(1024)}, u32[]{:S(2)}) copy-start(s32[1024]{0:T(1024)} %param.15) | copy-start | bytes 12292
  22.3 7.7 %copy-start.12 = (s32[8,1,16]{2,1,0:T(1,128)S(1)}, s32[8,1,16]{2,1,0:T(1,128)}, u32[]{:S(2)}) copy-start(s32[8,1,16]{2,1,0:T(1,128)} %param.23) | copy-start | bytes 1540
  22.3 33.4 %all-to-all-start = ((bf16[8,4,128,256]{3,1,2,0:T(4,128)(2,1)}), bf16[8,4,128,256]{3,1,2,0:T(4,128)(2,1)S(1)}, u32[]{:S(2)}, u32[]{:S(2)}) async-start(bf16[8,4,128,256]{3,1,2,0:T(4,128)(2,1)} %copy.155), calls=%async_computation | async-start | bytes 4194304 | tf_op jit(solution)/shard_map/all_to_all | solution.py:347
  104.6 20.2 %copy-start.4 = (f32[8,128,256]{2,0,1:T(8,128)S(1)}, f32[8,128,256]{2,0,1:T(8,128)}, u32[]{:S(2)}) copy-start(f32[8,128,256]{2,0,1:T(8,128)} %convolution_bitcast_fusion.1) | copy-start | bytes 3145732
  124.8 1.7 copy-start.5
  151.6 7.4 %collective-permute-start = (bf16[8,8,128,256]{3,2,1,0:T(8,128)(2,1)}, bf16[8,8,128,256]{3,2,1,0:T(8,128)(2,1)S(1)}, u32[]{:S(2)}, u32[]{:S(2)}) collective-permute-start(bf16[8,8,128,256]{3,2,1,0:T(8,128)(2,1)} %get-tuple-element.6), channel_id=1, source_target_pairs={{0,1},{1,0},{2,3},{3,2},{4,5},{5,4},{6,7},{7,6},{8,9},{9,8},{10,11... | collective-permute-start | bytes 12582920 | tf_op jit(solution)/shard_map/ppermute | solution.py:366
  165.7 5.4 %copy-start.2 = (bf16[1024,256]{1,0:T(8,128)(2,1)S(1)}, bf16[1024,256]{1,0:T(8,128)(2,1)}, u32[]{:S(2)}) copy-start(bf16[1024,256]{1,0:T(8,128)(2,1)} %get-tuple-element.15) | copy-start | bytes 1572868
  165.7 92.6 %all-to-all-start.1 = ((bf16[8,8,128,256]{3,2,1,0:T(8,128)(2,1)}), bf16[8,8,128,256]{3,2,1,0:T(8,128)(2,1)}, u32[]{:S(2)}, u32[]{:S(2)}) async-start(bf16[8,8,128,256]{3,2,1,0:T(8,128)(2,1)} %add_convert_fusion), calls=%async_computation.1 | async-start | bytes 8388608 | tf_op jit(solution)/shard_map/all_to_all | solution.py:368
  176.2 30.0 %collective-permute-start.1 = (bf16[4,128,256]{2,1,0:T(8,128)(2,1)S(1)}, bf16[4,128,256]{2,1,0:T(8,128)(2,1)S(1)}, u32[]{:S(2)}, u32[]{:S(2)}) collective-permute-start(bf16[4,128,256]{2,1,0:T(8,128)(2,1)S(1)} %bitcast.150), channel_id=1, source_target_pairs={{0,16},{16,32},{32,48},{48,64},{64,80},{80,96},{96,112},{112,0},{1... | collective-permute-start | bytes 786440 | tf_op jit(solution)/shard_map/ppermute | solution.py:381
  176.7 29.5 %collective-permute-start.2 = (bf16[4,128,256]{2,1,0:T(8,128)(2,1)S(1)}, bf16[4,128,256]{2,1,0:T(8,128)(2,1)S(1)}, u32[]{:S(2)}, u32[]{:S(2)}) collective-permute-start(bf16[4,128,256]{2,1,0:T(8,128)(2,1)S(1)} %bitcast.148), channel_id=1, source_target_pairs={{0,32},{16,48},{32,64},{48,80},{64,96},{80,112},{96,0},{112,16},{1... | collective-permute-start | bytes 786440 | tf_op jit(solution)/shard_map/ppermute | solution.py:381
  181.3 32.4 %collective-permute-start.3 = (bf16[4,128,256]{2,1,0:T(8,128)(2,1)S(1)}, bf16[4,128,256]{2,1,0:T(8,128)(2,1)S(1)}, u32[]{:S(2)}, u32[]{:S(2)}) collective-permute-start(bf16[4,128,256]{2,1,0:T(8,128)(2,1)S(1)} %bitcast.141), channel_id=1, source_target_pairs={{0,48},{16,64},{32,80},{48,96},{64,112},{80,0},{96,16},{112,32},{1... | collective-permute-start | bytes 786440 | tf_op jit(solution)/shard_map/ppermute | solution.py:381
  182.1 56.6 %collective-permute-start.4 = (bf16[4,128,256]{2,1,0:T(8,128)(2,1)S(1)}, bf16[4,128,256]{2,1,0:T(8,128)(2,1)S(1)}, u32[]{:S(2)}, u32[]{:S(2)}) collective-permute-start(bf16[4,128,256]{2,1,0:T(8,128)(2,1)S(1)} %bitcast.143), channel_id=1, source_target_pairs={{0,64},{16,80},{32,96},{48,112},{64,0},{80,16},{96,32},{112,48},{1... | collective-permute-start | bytes 786440 | tf_op jit(solution)/shard_map/ppermute | solution.py:381
  183.4 56.5 %collective-permute-start.5 = (bf16[4,128,256]{2,1,0:T(8,128)(2,1)S(1)}, bf16[4,128,256]{2,1,0:T(8,128)(2,1)S(1)}, u32[]{:S(2)}, u32[]{:S(2)}) collective-permute-start(bf16[4,128,256]{2,1,0:T(8,128)(2,1)S(1)} %bitcast.145), channel_id=1, source_target_pairs={{0,80},{16,96},{32,112},{48,0},{64,16},{80,32},{96,48},{112,64},{1... | collective-permute-start | bytes 786440 | tf_op jit(solution)/shard_map/ppermute | solution.py:381
  206.2 34.9 %collective-permute-start.6 = (bf16[4,128,256]{2,1,0:T(8,128)(2,1)S(1)}, bf16[4,128,256]{2,1,0:T(8,128)(2,1)S(1)}, u32[]{:S(2)}, u32[]{:S(2)}) collective-permute-start(bf16[4,128,256]{2,1,0:T(8,128)(2,1)S(1)} %bitcast.147), channel_id=1, source_target_pairs={{0,96},{16,112},{32,0},{48,16},{64,32},{80,48},{96,64},{112,80},{1... | collective-permute-start | bytes 786440 | tf_op jit(solution)/shard_map/ppermute | solution.py:381
  206.2 36.1 %collective-permute-start.7 = (bf16[4,128,256]{2,1,0:T(8,128)(2,1)S(1)}, bf16[4,128,256]{2,1,0:T(8,128)(2,1)S(1)}, u32[]{:S(2)}, u32[]{:S(2)}) collective-permute-start(bf16[4,128,256]{2,1,0:T(8,128)(2,1)S(1)} %bitcast.139), channel_id=1, source_target_pairs={{0,112},{16,0},{32,16},{48,32},{64,48},{80,64},{96,80},{112,96},{1... | collective-permute-start | bytes 786440 | tf_op jit(solution)/shard_map/ppermute | solution.py:381
  258.3 3.2 %copy-start.1 = (f32[16,128,256]{2,0,1:T(8,128)S(1)}, f32[16,128,256]{2,0,1:T(8,128)}, u32[]{:S(2)}) copy-start(f32[16,128,256]{2,0,1:T(8,128)} %copy.170) | copy-start | bytes 6291460
  261.5 1.5 copy-start.6
  261.5 2.6 copy-start.3
Sparse Core Ops, SparseCore 0:
  11.0 93.5 all-gather.1

commit v14 on v13

--- a/solution.py
+++ b/solution.py
@@ -381,17 +381,15 @@
         lax.ppermute(back_send[k], "grp", [(i, (i + k) % n_groups) for i in range(n_groups)])
         for k in range(1, n_groups)
     ]
-    back_flat = jnp.stack(pieces).reshape(n_groups * capacity, tile_size, width)
     back_slot = ((my_group - my_dest) % n_groups) * capacity + my_rank
-    back_place = (
-        back_slot[:, None] == jnp.arange(n_groups * capacity, dtype=jnp.int32)[None, :]
-    ).astype(jnp.bfloat16)
-    own_pick = jnp.einsum(
-        "hs,sif->hif",
-        back_place,
-        back_flat,
-        preferred_element_type=jnp.float32,
-    ).astype(jnp.bfloat16)
+    own_sum = None
+    for k, piece in enumerate(pieces):
+        place_k = (
+            back_slot[:, None] == (k * capacity + jnp.arange(capacity, dtype=jnp.int32))[None, :]
+        ).astype(jnp.bfloat16)
+        term = jnp.einsum("hc,cif->hif", place_k, piece, preferred_element_type=jnp.float32)
+        own_sum = term if own_sum is None else own_sum + term
+    own_pick = own_sum.astype(jnp.bfloat16)
     hub_back = jnp.einsum("hij,hif->hjf", hub_tiles, own_pick, preferred_element_type=jnp.float32)
     col_hot = (hub_cols[:, None] == tile_range[None, :]).astype(jnp.float32)
     grad_sum = grad_sum + jnp.einsum("hr,hjf->rjf", col_hot, hub_back, precision=highest)

time: 304 us -> 293 us (0.964)
  local copies, waits for them, and re-layouts: 38.9 us -> 22.1 us
  matrix products: 12.5 us -> 16.4 us
    another operation x9 -> x0, local copies, waits for them, and re-layouts: 19.3 us -> none  [local(): back_flat = jnp.stack(pieces).reshape(n_groups * capacity, tile_size, width)]
    dot_general x1 -> x8, matrix products: 1.25 us -> 5.14 us  [local(): jnp.einsum('hc,cif->hif', place_k, piece, preferred_element_type=jnp.floa...]
  transfers between devices with their start and end apart: 11 -> 11, of which waited for: 6 -> 5; matrix products, arithmetic and copies ran while one was open for 15% -> 11% of each run, Pallas kernels for 0% -> 0%
where the time goes in v14:
time: 293 us; the launch traced here: 291 us
  waiting for transfers between devices  130 us (44%)
  Pallas kernels  72.5 us (25%)
  local copies, waits for them, and re-layouts  22.1 us (8%)
  starting transfers between devices  19.3 us (7%)
  other arithmetic  16.5 us (6%)
  matrix products  16.4 us (6%)
  between operations  14.5 us (5%)
    ppermute x7, waiting for transfers between devices, local(): lax.ppermute(back_send[k], 'grp', [(i, (i + k) % n_groups) for i in range...  52.1 us
    all_gather x1, waiting for transfers between devices, local(): panels = lax.all_gather(proj, 'blk', axis=0, tiled=True)  46.6 us
    pallas_call x1, Pallas kernels, weight_sum(): pl.pallas_call(functools.partial(weight_sum_kernel, n_grp, n_blk), out_sh...  28.1 us
    all_to_all x1, waiting for transfers between devices, local(): lax.all_to_all(send_buf, 'grp', split_axis=0, concat_axis=0, tiled=True)  25.5 us
    pallas_call x1, Pallas kernels, tile_backward(): pl.pallas_call(backward_kernel, out_shape=(part, part_out), grid_spec=gri...  23.3 us
    pallas_call x1, Pallas kernels, tile_forward(): pl.pallas_call(forward_kernel, out_shape=jax.ShapeDtypeStruct((row_tiles,...  21 us
    convert_element_type x1, other arithmetic, local(): pair_sum = (keep + from_sibling.astype(jnp.float32)).astype(jnp.bfloat16)  8.1 us
    ppermute x7, starting transfers between devices, local(): lax.ppermute(back_send[k], 'grp', [(i, (i + k) % n_groups) for i in range...  7.58 us
  transfers between devices with their start and end apart: 11, of which 5 were waited for; matrix products, arithmetic and copies ran while one was open for 11% of the time, Pallas kernels for 0%

profile of v14, /device:TPU:1, one launch (start us, length us, event | category | flops | bytes accessed | tf_op | source)
XLA Modules:
  0.0 291.2 jit_solution(6201462272939234302)
XLA Ops:
  7.2 2.2 convolution_convert_fusion.4
  10.1 1.7 gather_fusion
  12.4 1.7 copy.68
  14.4 2.0 convolution_convert_fusion
  16.5 2.1 reshape.212
  18.6 3.7 %copy.69 = bf16[8,4,128,256]{3,1,2,0:T(4,128)(2,1)} copy(bf16[8,4,128,256]{3,1,0,2:T(4,128)(2,1)} %reshape.212) | data formatting | bytes 4194304 | tf_op jit(solution)/shard_map/reshape | solution.py:346
  22.3 6.3 %all-to-all-start = ((bf16[8,4,128,256]{3,1,2,0:T(4,128)(2,1)}), bf16[8,4,128,256]{3,1,2,0:T(4,128)(2,1)S(1)}, u32[]{:S(2)}, u32[]{:S(2)}) async-start(bf16[8,4,128,256]{3,1,2,0:T(4,128)(2,1)} %copy.69), calls=%async_computation | async-start | bytes 4194304 | tf_op jit(solution)/shard_map/all_to_all | solution.py:347
  30.1 25.5 %all-to-all-done = bf16[8,4,128,256]{3,1,2,0:T(4,128)(2,1)S(1)} async-done(((bf16[8,4,128,256]{3,1,2,0:T(4,128)(2,1)}), bf16[8,4,128,256]{3,1,2,0:T(4,128)(2,1)S(1)}, u32[]{:S(2)}, u32[]{:S(2)}) %all-to-all-start) | async-done | bytes 2097184 | tf_op jit(solution)/shard_map/all_to_all | solution.py:347
  55.7 2.3 convolution_bitcast_fusion.1
  58.0 46.6 %all-gather.2.cloned.1.call-done = bf16[16384,256]{1,0:T(8,128)(2,1)} async-done(((bf16[1024,256]{1,0:T(8,128)(2,1)}), bf16[16384,256]{1,0:T(8,128)(2,1)}) %all-gather.2.cloned.1.call-update) | async-done | bytes 8388624 | tf_op jit(solution)/shard_map/all_gather | solution.py:322
  104.6 21.0 %shard_map.139 = f32[8,128,256]{2,1,0:T(8,128)} custom-call(s32[512]{0:T(512)} %reshape_squeeze.6.rows_ref, s32[512]{0:T(512)} %reshape_squeeze.7.cols_ref, s32[16]{0:T(128)} %bitcast.171, bf16[16,32,128,128]{3,2,1,0:T(8,128)(2,1)} %bitcast.154, bf16[16,8,128,256]{3,2,1,0:T(8,128)(2,1)} %bitcast.157), custom_call_target="tpu_custom_call" | custom-call | flops 4294967296 | bytes 25165824 | tf_op jit(solution)/shard_map/pallas_call | solution.py:98
  125.6 1.7 copy_add_fusion.1
  127.3 1.4 fusion.8
  128.8 23.3 %shard_map.140 = (f32[8,8,128,256]{3,2,1,0:T(8,128)}, bf16[8,8,128,256]{3,2,1,0:T(8,128)(2,1)}) custom-call(s32[512]{0:T(512)} %reshape_squeeze.6.rows_ref, s32[512]{0:T(512)} %reshape_squeeze.7.cols_ref, s32[16]{0:T(128)} %bitcast.172, s32[1]{0:T(128)} %bitcast.18.core_ref, bf16[16,32,128,128]{3,2,1,0:T(8,128)(2,1)} %bitcast.155, bf16[8,128,256]{2,1,0:T(8,128)(2,1)} %bitcast.158), custom_call_target="tpu_custom_call" | custom-call | flops 4294967296 | bytes 33554432 | tf_op jit(solution)/shard_map/pallas_call | solution.py:132
  152.1 0.8 collective-permute-start
  154.4 5.7 %collective-permute-done = bf16[8,8,128,256]{3,2,1,0:T(8,128)(2,1)} collective-permute-done((bf16[8,8,128,256]{3,2,1,0:T(8,128)(2,1)}, bf16[8,8,128,256]{3,2,1,0:T(8,128)(2,1)}, u32[]{:S(2)}, u32[]{:S(2)}) %collective-permute-start) | collective-permute-done | bytes 4194336 | tf_op jit(solution)/shard_map/ppermute | solution.py:366
  160.0 8.1 %add_convert_fusion = bf16[8,8,128,256]{3,2,1,0:T(8,128)(2,1)} fusion(f32[8,8,128,256]{3,2,1,0:T(8,128)} %get-tuple-element.5, bf16[8,8,128,256]{3,2,1,0:T(8,128)(2,1)} %collective-permute-done), kind=kLoop, calls=%fused_computation.3 | loop fusion | flops 6291456 | bytes 16777216 | tf_op jit(solution)/shard_map/convert_element_type | solution.py:367
  168.1 4.6 %all-to-all-start.1 = ((bf16[8,8,128,256]{3,2,1,0:T(8,128)(2,1)}), bf16[8,8,128,256]{3,2,1,0:T(8,128)(2,1)}, u32[]{:S(2)}, u32[]{:S(2)}) async-start(bf16[8,8,128,256]{3,2,1,0:T(8,128)(2,1)} %add_convert_fusion), calls=%async_computation.1 | async-start | bytes 8388608 | tf_op jit(solution)/shard_map/all_to_all | solution.py:368
  172.7 4.8 %fusion.89 = (bf16[1,4,128,256]{3,0,2,1:T(2,128)(2,1)S(1)}, bf16[1,4,128,256]{3,0,2,1:T(2,128)(2,1)S(1)}, bf16[1,4,128,256]{3,0,2,1:T(2,128)(2,1)S(1)}, bf16[1,4...) fusion(bf16[8,4,128,256]{3,0,2,1:T(8,128)(2,1)S(1)} %convolutio, ...), kind=kLoop, calls=%fused_computation.146 | loop fusion | bytes 4194304 | tf_op jit(solution)/shard_map/slice | solution.py:381
  177.9 1.9 collective-permute-start.6
  180.1 2.8 collective-permute-start.5
  184.7 1.2 collective-permute-start.2
  187.2 0.9 collective-permute-start.1
  188.7 16.1 %collective-permute-done.5 = bf16[4,128,256]{2,0,1:T(4,128)(2,1)S(1)} collective-permute-done((bf16[4,128,256]{2,0,1:T(4,128)(2,1)S(1)}, bf16[4,128,256]{2,0,1:T(4,128)(2,1)S(1)}, u32[]{:S(2)}, u32[]{:S(2)}) %collective-permute-start.5) | collective-permute-done | bytes 262176 | tf_op jit(solution)/shard_map/ppermute | solution.py:381
  205.4 36.1 %collective-permute-done.4 = bf16[4,128,256]{2,0,1:T(4,128)(2,1)S(1)} collective-permute-done((bf16[4,128,256]{2,0,1:T(4,128)(2,1)S(1)}, bf16[4,128,256]{2,0,1:T(4,128)(2,1)S(1)}, u32[]{:S(2)}, u32[]{:S(2)}) %collective-permute-start.4) | collective-permute-done | bytes 262176 | tf_op jit(solution)/shard_map/ppermute | solution.py:381
  243.8 1.0 add_convert_fusion.1
  245.4 2.1 copy.83
  247.5 3.2 %convert_reduce_fusion = f32[8,128,256]{2,1,0:T(8,128)S(1)} fusion(bf16[8,8,128,256]{3,2,1,0:T(8,128)(2,1)} %all-to-all-done.1), kind=kLoop, calls=%fused_computation.2 | loop fusion | flops 3932160 | bytes 5242880 | tf_op jit(solution)/shard_map/reduce_sum | solution.py:371
  250.7 1.3 fusion.9
  252.2 1.1 convolution_convert_fusion.3
  254.5 28.1 %shard_map.141 = f32[16,32,128]{2,1,0:T(8,128)} custom-call(f32[16,32,128]{2,1,0:T(8,128)} %reshape.216.x_ref), custom_call_target="tpu_custom_call" | custom-call | tf_op jit(solution)/shard_map/pallas_call | solution.py:220
  282.6 1.0 broadcast_multiply_fusion
  (82 shorter events, 14.5 us)
Async XLA Ops:
  7.2 4.7 %copy-start = (bf16[1,1,16,128,128]{4,3,2,1,0:T(8,128)(2,1)S(1)}, bf16[1,1,16,128,128]{4,3,2,1,0:T(8,128)(2,1)}, u32[]{:S(2)}) copy-start(bf16[1,1,16,128,128]{4,3,2,1,0:T(8,128)(2,1)} %param.20) | copy-start | bytes 1572868
  7.2 4.6 %copy-start.11 = (s32[1,1,16]{2,1,0:T(1,128)S(1)}, s32[1,1,16]{2,1,0:T(1,128)}, u32[]{:S(2)}) copy-start(s32[1,1,16]{2,1,0:T(1,128)} %param.21) | copy-start | bytes 196
  7.2 97.4 %all-gather.2.cloned.1.call-start = ((), (), s32[]{:S(2)}) async-start(), calls=%async_computation.2 | async-start | bytes 8912896 | tf_op jit(solution)/shard_map/all_gather | solution.py:322
  11.8 2.3 copy-start.7
  22.3 6.4 %copy-start.8 = (s32[1,1,16,32]{3,2,1,0:T(8,128)S(1)}, s32[1,1,16,32]{3,2,1,0:T(8,128)}, u32[]{:S(2)}) copy-start(s32[1,1,16,32]{3,2,1,0:T(8,128)} %param.17) | copy-start | bytes 6148
  22.3 7.0 %copy-start.9 = (s32[1,1,16,32]{3,2,1,0:T(8,128)S(1)}, s32[1,1,16,32]{3,2,1,0:T(8,128)}, u32[]{:S(2)}) copy-start(s32[1,1,16,32]{3,2,1,0:T(8,128)} %param.18) | copy-start | bytes 6148
  22.3 7.7 %copy-start.10 = (s32[1024]{0:T(1024)S(1)}, s32[1024]{0:T(1024)}, u32[]{:S(2)}) copy-start(s32[1024]{0:T(1024)} %param.15) | copy-start | bytes 12292
  22.3 7.7 %copy-start.12 = (s32[8,1,16]{2,1,0:T(1,128)S(1)}, s32[8,1,16]{2,1,0:T(1,128)}, u32[]{:S(2)}) copy-start(s32[8,1,16]{2,1,0:T(1,128)} %param.23) | copy-start | bytes 1540
  22.3 33.4 %all-to-all-start = ((bf16[8,4,128,256]{3,1,2,0:T(4,128)(2,1)}), bf16[8,4,128,256]{3,1,2,0:T(4,128)(2,1)S(1)}, u32[]{:S(2)}, u32[]{:S(2)}) async-start(bf16[8,4,128,256]{3,1,2,0:T(4,128)(2,1)} %copy.69), calls=%async_computation | async-start | bytes 4194304 | tf_op jit(solution)/shard_map/all_to_all | solution.py:347
  104.6 21.0 %copy-start.4 = (f32[8,128,256]{2,0,1:T(8,128)S(1)}, f32[8,128,256]{2,0,1:T(8,128)}, u32[]{:S(2)}) copy-start(f32[8,128,256]{2,0,1:T(8,128)} %convolution_bitcast_fusion.1) | copy-start | bytes 3145732
  125.6 1.7 copy-start.5
  128.8 24.9 %copy-start.2 = (bf16[1024,256]{1,0:T(8,128)(2,1)S(1)}, bf16[1024,256]{1,0:T(8,128)(2,1)}, u32[]{:S(2)}) copy-start(bf16[1024,256]{1,0:T(8,128)(2,1)} %get-tuple-element.15) | copy-start | bytes 1572868
  152.1 8.0 %collective-permute-start = (bf16[8,8,128,256]{3,2,1,0:T(8,128)(2,1)}, bf16[8,8,128,256]{3,2,1,0:T(8,128)(2,1)}, u32[]{:S(2)}, u32[]{:S(2)}) collective-permute-start(bf16[8,8,128,256]{3,2,1,0:T(8,128)(2,1)} %get-tuple-element.6), channel_id=1, source_target_pairs={{0,1},{1,0},{2,3},{3,2},{4,5},{5,4},{6,7},{7,6},{8,9},{9,8},{10,11... | collective-permute-start | bytes 12582920 | tf_op jit(solution)/shard_map/ppermute | solution.py:366
  168.1 79.4 %all-to-all-start.1 = ((bf16[8,8,128,256]{3,2,1,0:T(8,128)(2,1)}), bf16[8,8,128,256]{3,2,1,0:T(8,128)(2,1)}, u32[]{:S(2)}, u32[]{:S(2)}) async-start(bf16[8,8,128,256]{3,2,1,0:T(8,128)(2,1)} %add_convert_fusion), calls=%async_computation.1 | async-start | bytes 8388608 | tf_op jit(solution)/shard_map/all_to_all | solution.py:368
  177.9 9.3 %collective-permute-start.6 = (bf16[4,128,256]{2,0,1:T(4,128)(2,1)S(1)}, bf16[4,128,256]{2,0,1:T(4,128)(2,1)S(1)}, u32[]{:S(2)}, u32[]{:S(2)}) collective-permute-start(bf16[4,128,256]{2,0,1:T(4,128)(2,1)S(1)} %bitcast.168), channel_id=1, source_target_pairs={{0,96},{16,112},{32,0},{48,16},{64,32},{80,48},{96,64},{112,80},{1... | collective-permute-start | bytes 786440 | tf_op jit(solution)/shard_map/ppermute | solution.py:381
  180.1 24.7 %collective-permute-start.5 = (bf16[4,128,256]{2,0,1:T(4,128)(2,1)S(1)}, bf16[4,128,256]{2,0,1:T(4,128)(2,1)S(1)}, u32[]{:S(2)}, u32[]{:S(2)}) collective-permute-start(bf16[4,128,256]{2,0,1:T(4,128)(2,1)S(1)} %bitcast.167), channel_id=1, source_target_pairs={{0,80},{16,96},{32,112},{48,0},{64,16},{80,32},{96,48},{112,64},{1... | collective-permute-start | bytes 786440 | tf_op jit(solution)/shard_map/ppermute | solution.py:381
  183.2 58.2 %collective-permute-start.4 = (bf16[4,128,256]{2,0,1:T(4,128)(2,1)S(1)}, bf16[4,128,256]{2,0,1:T(4,128)(2,1)S(1)}, u32[]{:S(2)}, u32[]{:S(2)}) collective-permute-start(bf16[4,128,256]{2,0,1:T(4,128)(2,1)S(1)} %bitcast.166), channel_id=1, source_target_pairs={{0,64},{16,80},{32,96},{48,112},{64,0},{80,16},{96,32},{112,48},{1... | collective-permute-start | bytes 786440 | tf_op jit(solution)/shard_map/ppermute | solution.py:381
  183.6 58.4 %collective-permute-start.3 = (bf16[4,128,256]{2,0,1:T(4,128)(2,1)S(1)}, bf16[4,128,256]{2,0,1:T(4,128)(2,1)S(1)}, u32[]{:S(2)}, u32[]{:S(2)}) collective-permute-start(bf16[4,128,256]{2,0,1:T(4,128)(2,1)S(1)} %bitcast.165), channel_id=1, source_target_pairs={{0,48},{16,64},{32,80},{48,96},{64,112},{80,0},{96,16},{112,32},{1... | collective-permute-start | bytes 786440 | tf_op jit(solution)/shard_map/ppermute | solution.py:381
  184.7 57.9 %collective-permute-start.2 = (bf16[4,128,256]{2,0,1:T(4,128)(2,1)S(1)}, bf16[4,128,256]{2,0,1:T(4,128)(2,1)S(1)}, u32[]{:S(2)}, u32[]{:S(2)}) collective-permute-start(bf16[4,128,256]{2,0,1:T(4,128)(2,1)S(1)} %bitcast.164), channel_id=1, source_target_pairs={{0,32},{16,48},{32,64},{48,80},{64,96},{80,112},{96,0},{112,16},{1... | collective-permute-start | bytes 786440 | tf_op jit(solution)/shard_map/ppermute | solution.py:381
  187.2 56.0 %collective-permute-start.1 = (bf16[4,128,256]{2,0,1:T(4,128)(2,1)S(1)}, bf16[4,128,256]{2,0,1:T(4,128)(2,1)S(1)}, u32[]{:S(2)}, u32[]{:S(2)}) collective-permute-start(bf16[4,128,256]{2,0,1:T(4,128)(2,1)S(1)} %bitcast.163), channel_id=1, source_target_pairs={{0,16},{16,32},{32,48},{48,64},{64,80},{80,96},{96,112},{112,0},{1... | collective-permute-start | bytes 786440 | tf_op jit(solution)/shard_map/ppermute | solution.py:381
  204.8 39.0 %collective-permute-start.7 = (bf16[4,128,256]{2,0,1:T(4,128)(2,1)S(1)}, bf16[4,128,256]{2,0,1:T(4,128)(2,1)S(1)}, u32[]{:S(2)}, u32[]{:S(2)}) collective-permute-start(bf16[4,128,256]{2,0,1:T(4,128)(2,1)S(1)} %bitcast.162), channel_id=1, source_target_pairs={{0,112},{16,0},{32,16},{48,32},{64,48},{80,64},{96,80},{112,96},{1... | collective-permute-start | bytes 786440 | tf_op jit(solution)/shard_map/ppermute | solution.py:381
  247.5 3.2 %copy-start.1 = (f32[16,128,256]{2,0,1:T(8,128)S(1)}, f32[16,128,256]{2,0,1:T(8,128)}, u32[]{:S(2)}) copy-start(f32[16,128,256]{2,0,1:T(8,128)} %copy.83) | copy-start | bytes 6291460
  250.7 1.5 copy-start.6
  250.7 2.6 copy-start.3
Sparse Core Ops, SparseCore 0:
  11.0 93.5 all-gather.1

commit v15 on v14

--- a/solution.py
+++ b/solution.py
@@ -54,7 +54,7 @@
     i = pl.program_id(0)
     half = pl.num_programs(0) // 2
     p = i // half
-    c = 2 * (i % half) + (p + core_ref[0]) % 2
+    c = 2 * ((i % half + core_ref[1]) % half) + (p + core_ref[0]) % 2
     slots = vals_ref.shape[1]
     row_tiles = grad_ref.shape[0]
     acc_ref[...] = jnp.zeros_like(acc_ref)
@@ -111,7 +111,7 @@
     half = n_src // 2
 
     def source(i, core_ref):
-        return 2 * (i % half) + (i // half + core_ref[0]) % 2
+        return 2 * ((i % half + core_ref[1]) % half) + (i // half + core_ref[0]) % 2
 
     grid_spec = pltpu.PrefetchScalarGridSpec(
         num_scalar_prefetch=4,
@@ -362,13 +362,15 @@
     grad_agg = (cotangent.astype(jnp.float32) * keep * slope).astype(jnp.bfloat16)
     grad_tiles = grad_agg.reshape(row_tiles, tile_size, width)
 
-    keep, send = tile_backward(dev_rows, dev_cols, dev_count, dev_vals, grad_tiles, core.reshape(1))
+    keep, send = tile_backward(
+        dev_rows, dev_cols, dev_count, dev_vals, grad_tiles, jnp.stack([core, lax.axis_index("blk") // 2])
+    )
     from_sibling = lax.ppermute(send, "blk", sibling)
     pair_sum = (keep + from_sibling.astype(jnp.float32)).astype(jnp.bfloat16)
-    received_parts = lax.all_to_all(
-        pair_sum, "blk", split_axis=0, concat_axis=0, tiled=True, axis_index_groups=core_groups
-    )
-    grad_sum = jnp.sum(received_parts.astype(jnp.float32), axis=0)
+    grad_sum = pair_sum[0].astype(jnp.float32)
+    for k in range(1, n_blocks // 2):
+        shift = [(i, (i + 2 * k) % n_blocks) for i in range(n_blocks)]
+        grad_sum = grad_sum + lax.ppermute(pair_sum[k], "blk", shift).astype(jnp.float32)
 
     rotation = (my_group + jnp.arange(n_groups, dtype=jnp.int32)) % n_groups
     back_send = jnp.einsum(

time: 293 us -> 313 us (1.068)
  starting transfers between devices: 19.3 us -> 30.9 us
  waiting for transfers between devices: 130 us -> 136 us
  matrix products: 16.4 us -> 21.9 us
  Pallas kernels: 72.5 us -> 67.5 us
  local copies, waits for them, and re-layouts: 22.1 us -> 26.5 us
    ppermute x0 -> x7, waiting for transfers between devices: none -> 37.2 us  [local(): lax.ppermute(pair_sum[k], 'blk', shift).astype(jnp.float32)]
    ppermute x7, waiting for transfers between devices: 52.1 us -> 27.5 us  [local(): lax.ppermute(back_send[k], 'grp', [(i, (i + k) % n_groups) for i in range...]
    ppermute x0 -> x7, starting transfers between devices: none -> 8.42 us  [local(): lax.ppermute(pair_sum[k], 'blk', shift).astype(jnp.float32)]
    ppermute x7, starting transfers between devices: 7.58 us -> 14.8 us  [local(): lax.ppermute(back_send[k], 'grp', [(i, (i + k) % n_groups) for i in range...]
    ppermute x1, waiting for transfers between devices: 5.65 us -> 0.01 us  [local(): from_sibling = lax.ppermute(send, 'blk', sibling)]
    all_to_all x1 -> x0, starting transfers between devices: 4.55 us -> none  [local(): lax.all_to_all(pair_sum, 'blk', split_axis=0, concat_axis=0, tiled=True,...]
    dot_general x8, matrix products: 5.14 us -> 9.48 us  [local(): jnp.einsum('hc,cif->hif', place_k, piece, preferred_element_type=jnp.floa...]
    reduce_sum x1 -> x0, other arithmetic: 3.16 us -> none  [local(): grad_sum = jnp.sum(received_parts.astype(jnp.float32), axis=0)]
  transfers between devices with their start and end apart: 11 -> 17, of which waited for: 5 -> 11; matrix products, arithmetic and copies ran while one was open for 11% -> 15% of each run, Pallas kernels for 0% -> 0%
where the time goes in v15:
time: 313 us; the launch traced here: 312 us
  waiting for transfers between devices  136 us (43%)
  Pallas kernels  67.5 us (22%)
  starting transfers between devices  30.9 us (10%)
  local copies, waits for them, and re-layouts  26.5 us (8%)
  matrix products  21.9 us (7%)
  other arithmetic  14.5 us (5%)
  between operations  14.5 us (5%)
    all_gather x1, waiting for transfers between devices, local(): panels = lax.all_gather(proj, 'blk', axis=0, tiled=True)  46.7 us
    ppermute x7, waiting for transfers between devices, local(): lax.ppermute(pair_sum[k], 'blk', shift).astype(jnp.float32)  37.2 us
    ppermute x7, waiting for transfers between devices, local(): lax.ppermute(back_send[k], 'grp', [(i, (i + k) % n_groups) for i in range...  27.5 us
    pallas_call x1, Pallas kernels, weight_sum(): pl.pallas_call(functools.partial(weight_sum_kernel, n_grp, n_blk), out_sh...  25.8 us
    all_to_all x1, waiting for transfers between devices, local(): lax.all_to_all(send_buf, 'grp', split_axis=0, concat_axis=0, tiled=True)  24.9 us
    pallas_call x1, Pallas kernels, tile_backward(): pl.pallas_call(backward_kernel, out_shape=(part, part_out), grid_spec=gri...  22.3 us
    pallas_call x1, Pallas kernels, tile_forward(): pl.pallas_call(forward_kernel, out_shape=jax.ShapeDtypeStruct((row_tiles,...  19.4 us
    ppermute x7, starting transfers between devices, local(): lax.ppermute(back_send[k], 'grp', [(i, (i + k) % n_groups) for i in range...  14.8 us
  transfers between devices with their start and end apart: 17, of which 11 were waited for; matrix products, arithmetic and copies ran while one was open for 15% of the time, Pallas kernels for 0%

profile of v15, /device:TPU:1, one launch (start us, length us, event | category | flops | bytes accessed | tf_op | source)
XLA Modules:
  0.0 312.2 jit_solution(11956994738783734794)
XLA Ops:
  7.2 2.2 convolution_convert_fusion.4
  14.4 2.0 convolution_convert_fusion
  16.5 2.1 reshape.211
  18.6 3.7 %copy.68 = bf16[8,4,128,256]{3,1,2,0:T(4,128)(2,1)} copy(bf16[8,4,128,256]{3,1,0,2:T(4,128)(2,1)} %reshape.211) | data formatting | bytes 4194304 | tf_op jit(solution)/shard_map/reshape | solution.py:346
  22.2 6.3 %all-to-all-start = ((bf16[8,4,128,256]{3,1,2,0:T(4,128)(2,1)}), bf16[8,4,128,256]{3,1,2,0:T(4,128)(2,1)S(1)}, u32[]{:S(2)}, u32[]{:S(2)}) async-start(bf16[8,4,128,256]{3,1,2,0:T(4,128)(2,1)} %copy.68), calls=%async_computation | async-start | bytes 4194304 | tf_op jit(solution)/shard_map/all_to_all | solution.py:347
  30.7 24.9 %all-to-all-done = bf16[8,4,128,256]{3,1,2,0:T(4,128)(2,1)S(1)} async-done(((bf16[8,4,128,256]{3,1,2,0:T(4,128)(2,1)}), bf16[8,4,128,256]{3,1,2,0:T(4,128)(2,1)S(1)}, u32[]{:S(2)}, u32[]{:S(2)}) %all-to-all-start) | async-done | bytes 2097184 | tf_op jit(solution)/shard_map/all_to_all | solution.py:347
  55.6 2.3 convolution_bitcast_fusion.1
  57.9 46.7 %all-gather.2.cloned.1.call-done = bf16[16384,256]{1,0:T(8,128)(2,1)} async-done(((bf16[1024,256]{1,0:T(8,128)(2,1)}), bf16[16384,256]{1,0:T(8,128)(2,1)}) %all-gather.2.cloned.1.call-update) | async-done | bytes 8388624 | tf_op jit(solution)/shard_map/all_gather | solution.py:322
  104.7 19.4 %shard_map.139 = f32[8,128,256]{2,1,0:T(8,128)} custom-call(s32[512]{0:T(512)} %reshape_squeeze.6.rows_ref, s32[512]{0:T(512)} %reshape_squeeze.7.cols_ref, s32[16]{0:T(128)} %bitcast.188, bf16[16,32,128,128]{3,2,1,0:T(8,128)(2,1)} %bitcast.172, bf16[16,8,128,256]{3,2,1,0:T(8,128)(2,1)} %bitcast.175), custom_call_target="tpu_custom_call" | custom-call | flops 4294967296 | bytes 25165824 | tf_op jit(solution)/shard_map/pallas_call | solution.py:98
  127.2 22.3 %shard_map.140 = (f32[8,8,128,256]{3,2,1,0:T(8,128)}, bf16[8,8,128,256]{3,2,1,0:T(8,128)(2,1)}) custom-call(s32[512]{0:T(512)} %reshape_squeeze.6.rows_ref, s32[512]{0:T(512)} %reshape_squeeze.7.cols_ref, s32[16]{0:T(128)} %bitcast.189, s32[2]{0:T(128)} %pad_add_fusion.core_ref, bf16[16,32,128,128]{3,2,1,0:T(8,128)(2,1)} %bitcast.173, ...), custom_call_target="tpu_custom_call" | custom-call | flops 4294967296 | bytes 33554432 | tf_op jit(solution)/shard_map/pallas_call | solution.py:132
  152.2 4.8 %fusion.94 = (bf16[1,4,128,256]{3,0,2,1:T(2,128)(2,1)S(1)}, bf16[1,4,128,256]{3,0,2,1:T(2,128)(2,1)S(1)}, bf16[1,4,128,256]{3,0,2,1:T(2,128)(2,1)S(1)}, bf16[1,4...) fusion(bf16[8,4,128,256]{3,0,2,1:T(8,128)(2,1)S(1)} %convolutio, ...), kind=kLoop, calls=%fused_computation.161 | loop fusion | bytes 4194304 | tf_op jit(solution)/shard_map/slice | solution.py:383
  160.1 2.4 collective-permute-start.8
  162.6 2.7 collective-permute-start.9
  168.6 15.1 %collective-permute-done.13 = bf16[4,128,256]{2,0,1:T(4,128)(2,1)S(1)} collective-permute-done((bf16[4,128,256]{2,0,1:T(4,128)(2,1)S(1)}, bf16[4,128,256]{2,0,1:T(4,128)(2,1)S(1)}, u32[]{:S(2)}, u32[]{:S(2)}) %collective-permute-start.13) | collective-permute-done | bytes 262176 | tf_op jit(solution)/shard_map/ppermute | solution.py:383
  183.7 2.2 collective-permute-start.12
  186.6 8.1 %collective-permute-done.12 = bf16[4,128,256]{2,0,1:T(4,128)(2,1)S(1)} collective-permute-done((bf16[4,128,256]{2,0,1:T(4,128)(2,1)S(1)}, bf16[4,128,256]{2,0,1:T(4,128)(2,1)S(1)}, u32[]{:S(2)}, u32[]{:S(2)}) %collective-permute-start.12) | collective-permute-done | bytes 262176 | tf_op jit(solution)/shard_map/ppermute | solution.py:383
  194.6 2.1 collective-permute-start.11
  197.3 4.3 %collective-permute-done.11 = bf16[4,128,256]{2,0,1:T(4,128)(2,1)S(1)} collective-permute-done((bf16[4,128,256]{2,0,1:T(4,128)(2,1)S(1)}, bf16[4,128,256]{2,0,1:T(4,128)(2,1)S(1)}, u32[]{:S(2)}, u32[]{:S(2)}) %collective-permute-start.11) | collective-permute-done | bytes 262176 | tf_op jit(solution)/shard_map/ppermute | solution.py:383
  201.6 2.6 collective-permute-start.14
  204.9 2.0 fusion.57
  208.7 2.0 fusion.61
  210.7 6.0 %add_convert_fusion = bf16[8,8,128,256]{3,2,1,0:T(8,128)(2,1)S(1)} fusion(f32[8,8,128,256]{3,2,1,0:T(8,128)} %get-tuple-element.5, bf16[8,8,128,256]{3,2,1,0:T(8,128)(2,1)} %collective-permute-done), kind=kLoop, calls=%fused_computation.2 | loop fusion | flops 6291456 | bytes 16777216 | tf_op jit(solution)/shard_map/convert_element_type | solution.py:369
  219.8 5.1 %collective-permute-start.7 = (bf16[8,128,256]{2,1,0:T(8,128)(2,1)S(1)}, bf16[8,128,256]{2,1,0:T(8,128)(2,1)S(1)}, u32[]{:S(2)}, u32[]{:S(2)}) collective-permute-start(bf16[8,128,256]{2,1,0:T(8,128)(2,1)S(1)} %get-tuple-element.8), channel_id=1, source_target_pairs={{0,14},{1,15},{2,0},{3,1},{4,2},{5,3},{6,4},{7,5},{8,6},{9,7},{10,... | collective-permute-start | bytes 1572872 | tf_op jit(solution)/shard_map/ppermute | solution.py:373
  227.4 2.3 collective-permute-start.4
  229.6 4.8 %collective-permute-done.1 = bf16[8,128,256]{2,1,0:T(8,128)(2,1)S(1)} collective-permute-done((bf16[8,128,256]{2,1,0:T(8,128)(2,1)S(1)}, bf16[8,128,256]{2,1,0:T(8,128)(2,1)S(1)}, u32[]{:S(2)}, u32[]{:S(2)}) %collective-permute-start.1) | collective-permute-done | bytes 524320 | tf_op jit(solution)/shard_map/ppermute | solution.py:373
  237.5 2.1 copy.82
  239.6 2.5 fusion.42
  242.2 12.3 %collective-permute-done.5 = bf16[8,128,256]{2,1,0:T(8,128)(2,1)} collective-permute-done((bf16[8,128,256]{2,1,0:T(8,128)(2,1)}, bf16[8,128,256]{2,1,0:T(8,128)(2,1)}, u32[]{:S(2)}, u32[]{:S(2)}) %collective-permute-start.5) | collective-permute-done | bytes 524320 | tf_op jit(solution)/shard_map/ppermute | solution.py:373
  254.5 7.8 %collective-permute-done.3 = bf16[8,128,256]{2,1,0:T(8,128)(2,1)} collective-permute-done((bf16[8,128,256]{2,1,0:T(8,128)(2,1)}, bf16[8,128,256]{2,1,0:T(8,128)(2,1)}, u32[]{:S(2)}, u32[]{:S(2)}) %collective-permute-start.3) | collective-permute-done | bytes 524320 | tf_op jit(solution)/shard_map/ppermute | solution.py:373
  262.4 10.4 %collective-permute-done.2 = bf16[8,128,256]{2,1,0:T(8,128)(2,1)} collective-permute-done((bf16[8,128,256]{2,1,0:T(8,128)(2,1)S(1)}, bf16[8,128,256]{2,1,0:T(8,128)(2,1)}, u32[]{:S(2)}, u32[]{:S(2)}) %collective-permute-start.2) | collective-permute-done | bytes 524320 | tf_op jit(solution)/shard_map/ppermute | solution.py:373
  272.8 2.6 fusion.8
  277.8 25.8 %shard_map.141 = f32[16,32,128]{2,1,0:T(8,128)} custom-call(f32[16,32,128]{2,1,0:T(8,128)} %reshape.214.x_ref), custom_call_target="tpu_custom_call" | custom-call | tf_op jit(solution)/shard_map/pallas_call | solution.py:220
  (109 shorter events, 35.7 us)
Async XLA Ops:
  7.2 4.7 %copy-start = (bf16[1,1,16,128,128]{4,3,2,1,0:T(8,128)(2,1)S(1)}, bf16[1,1,16,128,128]{4,3,2,1,0:T(8,128)(2,1)}, u32[]{:S(2)}) copy-start(bf16[1,1,16,128,128]{4,3,2,1,0:T(8,128)(2,1)} %param.20) | copy-start | bytes 1572868
  7.2 4.6 %copy-start.18 = (s32[1,1,16]{2,1,0:T(1,128)S(1)}, s32[1,1,16]{2,1,0:T(1,128)}, u32[]{:S(2)}) copy-start(s32[1,1,16]{2,1,0:T(1,128)} %param.21) | copy-start | bytes 196
  7.2 97.5 %all-gather.2.cloned.1.call-start = ((), (), s32[]{:S(2)}) async-start(), calls=%async_computation.1 | async-start | bytes 8912896 | tf_op jit(solution)/shard_map/all_gather | solution.py:322
  22.2 6.3 %copy-start.15 = (s32[1,1,16,32]{3,2,1,0:T(8,128)S(1)}, s32[1,1,16,32]{3,2,1,0:T(8,128)}, u32[]{:S(2)}) copy-start(s32[1,1,16,32]{3,2,1,0:T(8,128)} %param.17) | copy-start | bytes 6148
  22.2 7.0 %copy-start.16 = (s32[1,1,16,32]{3,2,1,0:T(8,128)S(1)}, s32[1,1,16,32]{3,2,1,0:T(8,128)}, u32[]{:S(2)}) copy-start(s32[1,1,16,32]{3,2,1,0:T(8,128)} %param.18) | copy-start | bytes 6148
  22.2 8.3 %copy-start.17 = (s32[1024]{0:T(1024)S(1)}, s32[1024]{0:T(1024)}, u32[]{:S(2)}) copy-start(s32[1024]{0:T(1024)} %param.15) | copy-start | bytes 12292
  22.2 8.3 %copy-start.19 = (s32[8,1,16]{2,1,0:T(1,128)S(1)}, s32[8,1,16]{2,1,0:T(1,128)}, u32[]{:S(2)}) copy-start(s32[8,1,16]{2,1,0:T(1,128)} %param.23) | copy-start | bytes 1540
  22.2 33.4 %all-to-all-start = ((bf16[8,4,128,256]{3,1,2,0:T(4,128)(2,1)}), bf16[8,4,128,256]{3,1,2,0:T(4,128)(2,1)S(1)}, u32[]{:S(2)}, u32[]{:S(2)}) async-start(bf16[8,4,128,256]{3,1,2,0:T(4,128)(2,1)} %copy.68), calls=%async_computation | async-start | bytes 4194304 | tf_op jit(solution)/shard_map/all_to_all | solution.py:347
  104.7 19.4 %copy-start.7 = (f32[8,128,256]{2,0,1:T(8,128)S(1)}, f32[8,128,256]{2,0,1:T(8,128)}, u32[]{:S(2)}) copy-start(f32[8,128,256]{2,0,1:T(8,128)} %convolution_bitcast_fusion.1) | copy-start | bytes 3145732
  127.2 24.3 %copy-start.5 = (bf16[1024,256]{1,0:T(8,128)(2,1)S(1)}, bf16[1024,256]{1,0:T(8,128)(2,1)}, u32[]{:S(2)}) copy-start(bf16[1024,256]{1,0:T(8,128)(2,1)} %get-tuple-element.22) | copy-start | bytes 1572868
  149.5 61.2 %collective-permute-start = (bf16[8,8,128,256]{3,2,1,0:T(8,128)(2,1)}, bf16[8,8,128,256]{3,2,1,0:T(8,128)(2,1)}, u32[]{:S(2)}, u32[]{:S(2)}) collective-permute-start(bf16[8,8,128,256]{3,2,1,0:T(8,128)(2,1)} %get-tuple-element.6), channel_id=1, source_target_pairs={{0,1},{1,0},{2,3},{3,2},{4,5},{5,4},{6,7},{7,6},{8,9},{9,8},{10,11... | collective-permute-start | bytes 12582920 | tf_op jit(solution)/shard_map/ppermute | solution.py:368
  160.1 48.6 %collective-permute-start.8 = (bf16[4,128,256]{2,0,1:T(4,128)(2,1)S(1)}, bf16[4,128,256]{2,0,1:T(4,128)(2,1)S(1)}, u32[]{:S(2)}, u32[]{:S(2)}) collective-permute-start(bf16[4,128,256]{2,0,1:T(4,128)(2,1)S(1)} %bitcast.180), channel_id=1, source_target_pairs={{0,16},{16,32},{32,48},{48,64},{64,80},{80,96},{96,112},{112,0},{1... | collective-permute-start | bytes 786440 | tf_op jit(solution)/shard_map/ppermute | solution.py:383
  162.6 44.3 %collective-permute-start.9 = (bf16[4,128,256]{2,0,1:T(4,128)(2,1)S(1)}, bf16[4,128,256]{2,0,1:T(4,128)(2,1)S(1)}, u32[]{:S(2)}, u32[]{:S(2)}) collective-permute-start(bf16[4,128,256]{2,0,1:T(4,128)(2,1)S(1)} %bitcast.181), channel_id=1, source_target_pairs={{0,32},{16,48},{32,64},{48,80},{64,96},{80,112},{96,0},{112,16},{1... | collective-permute-start | bytes 786440 | tf_op jit(solution)/shard_map/ppermute | solution.py:383
  165.3 39.6 %collective-permute-start.10 = (bf16[4,128,256]{2,0,1:T(4,128)(2,1)S(1)}, bf16[4,128,256]{2,0,1:T(4,128)(2,1)S(1)}, u32[]{:S(2)}, u32[]{:S(2)}) collective-permute-start(bf16[4,128,256]{2,0,1:T(4,128)(2,1)S(1)} %bitcast.182), channel_id=1, source_target_pairs={{0,48},{16,64},{32,80},{48,96},{64,112},{80,0},{96,16},{112,32},{1... | collective-permute-start | bytes 786440 | tf_op jit(solution)/shard_map/ppermute | solution.py:383
  166.2 17.5 %collective-permute-start.13 = (bf16[4,128,256]{2,0,1:T(4,128)(2,1)S(1)}, bf16[4,128,256]{2,0,1:T(4,128)(2,1)S(1)}, u32[]{:S(2)}, u32[]{:S(2)}) collective-permute-start(bf16[4,128,256]{2,0,1:T(4,128)(2,1)S(1)} %bitcast.185), channel_id=1, source_target_pairs={{0,96},{16,112},{32,0},{48,16},{64,32},{80,48},{96,64},{112,80},{1... | collective-permute-start | bytes 786440 | tf_op jit(solution)/shard_map/ppermute | solution.py:383
  183.7 10.9 %collective-permute-start.12 = (bf16[4,128,256]{2,0,1:T(4,128)(2,1)S(1)}, bf16[4,128,256]{2,0,1:T(4,128)(2,1)S(1)}, u32[]{:S(2)}, u32[]{:S(2)}) collective-permute-start(bf16[4,128,256]{2,0,1:T(4,128)(2,1)S(1)} %bitcast.184), channel_id=1, source_target_pairs={{0,80},{16,96},{32,112},{48,0},{64,16},{80,32},{96,48},{112,64},{1... | collective-permute-start | bytes 786440 | tf_op jit(solution)/shard_map/ppermute | solution.py:383
  194.6 7.0 %collective-permute-start.11 = (bf16[4,128,256]{2,0,1:T(4,128)(2,1)S(1)}, bf16[4,128,256]{2,0,1:T(4,128)(2,1)S(1)}, u32[]{:S(2)}, u32[]{:S(2)}) collective-permute-start(bf16[4,128,256]{2,0,1:T(4,128)(2,1)S(1)} %bitcast.183), channel_id=1, source_target_pairs={{0,64},{16,80},{32,96},{48,112},{64,0},{80,16},{96,32},{112,48},{1... | collective-permute-start | bytes 786440 | tf_op jit(solution)/shard_map/ppermute | solution.py:383
  201.6 23.3 %collective-permute-start.14 = (bf16[4,128,256]{2,0,1:T(4,128)(2,1)}, bf16[4,128,256]{2,0,1:T(4,128)(2,1)S(1)}, u32[]{:S(2)}, u32[]{:S(2)}) collective-permute-start(bf16[4,128,256]{2,0,1:T(4,128)(2,1)} %bitcast.165), channel_id=1, source_target_pairs={{0,112},{16,0},{32,16},{48,32},{64,48},{80,64},{96,80},{112,96},{1... | collective-permute-start | bytes 786440 | tf_op jit(solution)/shard_map/ppermute | solution.py:383
  216.7 8.2 %copy-start.2 = (f32[16,128,256]{2,0,1:T(8,128)S(1)}, f32[16,128,256]{2,0,1:T(8,128)}, u32[]{:S(2)}) copy-start(f32[16,128,256]{2,0,1:T(8,128)} %fusion.57) | copy-start | bytes 6291460
  216.7 8.2 %copy-start.3 = (f32[16,128,256]{2,0,1:T(8,128)S(1)}, f32[16,128,256]{2,0,1:T(8,128)}, u32[]{:S(2)}) copy-start(f32[16,128,256]{2,0,1:T(8,128)} %fusion.59) | copy-start | bytes 6291460
  216.7 8.2 %copy-start.4 = (f32[16,128,256]{2,0,1:T(8,128)S(1)}, f32[16,128,256]{2,0,1:T(8,128)}, u32[]{:S(2)}) copy-start(f32[16,128,256]{2,0,1:T(8,128)} %fusion.61) | copy-start | bytes 6291460
  219.8 14.6 %collective-permute-start.1 = (bf16[8,128,256]{2,1,0:T(8,128)(2,1)S(1)}, bf16[8,128,256]{2,1,0:T(8,128)(2,1)S(1)}, u32[]{:S(2)}, u32[]{:S(2)}) collective-permute-start(bf16[8,128,256]{2,1,0:T(8,128)(2,1)S(1)} %get-tuple-element.7), channel_id=1, source_target_pairs={{0,2},{1,3},{2,4},{3,5},{4,6},{5,7},{6,8},{7,9},{8,10},{9,11},{10,... | collective-permute-start | bytes 1572872 | tf_op jit(solution)/shard_map/ppermute | solution.py:373
  219.8 16.4 %collective-permute-start.7 = (bf16[8,128,256]{2,1,0:T(8,128)(2,1)S(1)}, bf16[8,128,256]{2,1,0:T(8,128)(2,1)S(1)}, u32[]{:S(2)}, u32[]{:S(2)}) collective-permute-start(bf16[8,128,256]{2,1,0:T(8,128)(2,1)S(1)} %get-tuple-element.8), channel_id=1, source_target_pairs={{0,14},{1,15},{2,0},{3,1},{4,2},{5,3},{6,4},{7,5},{8,6},{9,7},{10,... | collective-permute-start | bytes 1572872 | tf_op jit(solution)/shard_map/ppermute | solution.py:373
  226.3 15.9 %collective-permute-start.6 = (bf16[8,128,256]{2,1,0:T(8,128)(2,1)}, bf16[8,128,256]{2,1,0:T(8,128)(2,1)}, u32[]{:S(2)}, u32[]{:S(2)}) collective-permute-start(bf16[8,128,256]{2,1,0:T(8,128)(2,1)} %get-tuple-element.9), channel_id=1, source_target_pairs={{0,12},{1,13},{2,14},{3,15},{4,0},{5,1},{6,2},{7,3},{8,4},{9,5},{1... | collective-permute-start | bytes 1572872 | tf_op jit(solution)/shard_map/ppermute | solution.py:373
  226.4 28.2 %collective-permute-start.5 = (bf16[8,128,256]{2,1,0:T(8,128)(2,1)}, bf16[8,128,256]{2,1,0:T(8,128)(2,1)}, u32[]{:S(2)}, u32[]{:S(2)}) collective-permute-start(bf16[8,128,256]{2,1,0:T(8,128)(2,1)} %get-tuple-element.10), channel_id=1, source_target_pairs={{0,10},{1,11},{2,12},{3,13},{4,14},{5,15},{6,0},{7,1},{8,2},{9,3},... | collective-permute-start | bytes 1572872 | tf_op jit(solution)/shard_map/ppermute | solution.py:373
  227.4 27.2 %collective-permute-start.4 = (bf16[8,128,256]{2,1,0:T(8,128)(2,1)}, bf16[8,128,256]{2,1,0:T(8,128)(2,1)}, u32[]{:S(2)}, u32[]{:S(2)}) collective-permute-start(bf16[8,128,256]{2,1,0:T(8,128)(2,1)} %get-tuple-element.11), channel_id=1, source_target_pairs={{0,8},{1,9},{2,10},{3,11},{4,12},{5,13},{6,14},{7,15},{8,0},{9,1},... | collective-permute-start | bytes 1572872 | tf_op jit(solution)/shard_map/ppermute | solution.py:373
  234.4 27.9 %collective-permute-start.3 = (bf16[8,128,256]{2,1,0:T(8,128)(2,1)}, bf16[8,128,256]{2,1,0:T(8,128)(2,1)}, u32[]{:S(2)}, u32[]{:S(2)}) collective-permute-start(bf16[8,128,256]{2,1,0:T(8,128)(2,1)} %get-tuple-element.12), channel_id=1, source_target_pairs={{0,6},{1,7},{2,8},{3,9},{4,10},{5,11},{6,12},{7,13},{8,14},{9,15},... | collective-permute-start | bytes 1572872 | tf_op jit(solution)/shard_map/ppermute | solution.py:373
  236.2 36.6 %collective-permute-start.2 = (bf16[8,128,256]{2,1,0:T(8,128)(2,1)S(1)}, bf16[8,128,256]{2,1,0:T(8,128)(2,1)}, u32[]{:S(2)}, u32[]{:S(2)}) collective-permute-start(bf16[8,128,256]{2,1,0:T(8,128)(2,1)S(1)} %get-tuple-element.13), channel_id=1, source_target_pairs={{0,4},{1,5},{2,6},{3,7},{4,8},{5,9},{6,10},{7,11},{8,12},{9,13},{1... | collective-permute-start | bytes 1572872 | tf_op jit(solution)/shard_map/ppermute | solution.py:373
  239.6 33.2 %copy-start.11 = (bf16[8,128,256]{2,1,0:T(8,128)(2,1)S(1)}, bf16[8,128,256]{2,1,0:T(8,128)(2,1)}, u32[]{:S(2)}) copy-start(bf16[8,128,256]{2,1,0:T(8,128)(2,1)} %copy-done.10) | copy-start | bytes 1572868
  239.6 33.2 %copy-start.13 = (bf16[8,128,256]{2,1,0:T(8,128)(2,1)S(1)}, bf16[8,128,256]{2,1,0:T(8,128)(2,1)}, u32[]{:S(2)}) copy-start(bf16[8,128,256]{2,1,0:T(8,128)(2,1)} %copy-done.12) | copy-start | bytes 1572868
  242.1 33.3 %copy-start.6 = (bf16[1024,256]{1,0:T(8,128)(2,1)S(1)}, bf16[1024,256]{1,0:T(8,128)(2,1)}, u32[]{:S(2)}) copy-start(bf16[1024,256]{1,0:T(8,128)(2,1)} %param.12) | copy-start | bytes 1572868
  242.1 33.6 %copy-start.9 = (bf16[256,256]{1,0:T(8,128)(2,1)S(1)}, bf16[256,256]{1,0:T(8,128)(2,1)}, u32[]{:S(2)}) copy-start(bf16[256,256]{1,0:T(8,128)(2,1)} %param.13) | copy-start | bytes 393220
  (5 other events, 9.7 us)
Sparse Core Ops, SparseCore 0:
  11.0 93.5 all-gather.1

commit v16 on v14

--- a/solution.py
+++ b/solution.py
@@ -75,7 +75,7 @@
 
     @pl.when(p == 0)
     def _():
-        keep_ref[0] = acc_ref[...]
+        keep_ref[0] = acc_ref[...].astype(keep_ref.dtype)
 
     @pl.when(p == 1)
     def _():
@@ -127,11 +127,10 @@
         scratch_shapes=[pltpu.VMEM((row_tiles, tile, width), jnp.float32)],
     )
     flops = 2 * n_src * slots * tile * tile * width
-    part = jax.ShapeDtypeStruct((half, row_tiles, tile, width), jnp.float32)
     part_out = jax.ShapeDtypeStruct((half, row_tiles, tile, width), jnp.bfloat16)
     return pl.pallas_call(
         backward_kernel,
-        out_shape=(part, part_out),
+        out_shape=(part_out, part_out),
         grid_spec=grid_spec,
         cost_estimate=pl.CostEstimate(
             flops=flops, transcendentals=0, bytes_accessed=vals.size * 2 + n_src * row_tiles * tile * width * 4
@@ -364,7 +363,7 @@
 
     keep, send = tile_backward(dev_rows, dev_cols, dev_count, dev_vals, grad_tiles, core.reshape(1))
     from_sibling = lax.ppermute(send, "blk", sibling)
-    pair_sum = (keep + from_sibling.astype(jnp.float32)).astype(jnp.bfloat16)
+    pair_sum = (keep.astype(jnp.float32) + from_sibling.astype(jnp.float32)).astype(jnp.bfloat16)
     received_parts = lax.all_to_all(
         pair_sum, "blk", split_axis=0, concat_axis=0, tiled=True, axis_index_groups=core_groups
     )

time: 293 us -> 289 us (0.986)
  starting transfers between devices: 19.3 us -> 39 us
  waiting for transfers between devices: 130 us -> 111 us
  Pallas kernels: 72.5 us -> 68.3 us
    ppermute x7, starting transfers between devices: 7.58 us -> 26.4 us  [local(): lax.ppermute(back_send[k], 'grp', [(i, (i + k) % n_groups) for i in range...]
    ppermute x7, waiting for transfers between devices: 52.1 us -> 33.5 us  [local(): lax.ppermute(back_send[k], 'grp', [(i, (i + k) % n_groups) for i in range...]
  transfers between devices with their start and end apart: 11 -> 11, of which waited for: 5 -> 6; matrix products, arithmetic and copies ran while one was open for 11% -> 11% of each run, Pallas kernels for 0% -> 0%
where the time goes in v16:
time: 289 us; the launch traced here: 288 us
  waiting for transfers between devices  111 us (38%)
  Pallas kernels  68.3 us (24%)
  starting transfers between devices  39 us (13%)
  local copies, waits for them, and re-layouts  22.5 us (8%)
  matrix products  16.4 us (6%)
  other arithmetic  15.7 us (5%)
  between operations  14.5 us (5%)
    all_gather x1, waiting for transfers between devices, local(): panels = lax.all_gather(proj, 'blk', axis=0, tiled=True)  46.6 us
    ppermute x7, waiting for transfers between devices, local(): lax.ppermute(back_send[k], 'grp', [(i, (i + k) % n_groups) for i in range...  33.5 us
    pallas_call x1, Pallas kernels, weight_sum(): pl.pallas_call(functools.partial(weight_sum_kernel, n_grp, n_blk), out_sh...  26.7 us
    ppermute x7, starting transfers between devices, local(): lax.ppermute(back_send[k], 'grp', [(i, (i + k) % n_groups) for i in range...  26.4 us
    all_to_all x1, waiting for transfers between devices, local(): lax.all_to_all(send_buf, 'grp', split_axis=0, concat_axis=0, tiled=True)  25.5 us
    pallas_call x1, Pallas kernels, tile_backward(): pl.pallas_call(backward_kernel, out_shape=(part_out, part_out), grid_spec...  21.8 us
    pallas_call x1, Pallas kernels, tile_forward(): pl.pallas_call(forward_kernel, out_shape=jax.ShapeDtypeStruct((row_tiles,...  19.7 us
    convert_element_type x1, other arithmetic, local(): (keep.astype(jnp.float32) + from_sibling.astype(jnp.float32)).astype(jnp....  7.33 us
  transfers between devices with their start and end apart: 11, of which 6 were waited for; matrix products, arithmetic and copies ran while one was open for 11% of the time, Pallas kernels for 0%

profile of v16, /device:TPU:1, one launch (start us, length us, event | category | flops | bytes accessed | tf_op | source)
XLA Modules:
  0.0 287.6 jit_solution(8700232135548631502)
XLA Ops:
  7.2 2.2 convolution_convert_fusion.4
  10.1 1.7 gather_fusion
  12.4 1.7 copy.68
  14.4 2.0 convolution_convert_fusion
  16.5 2.1 reshape.212
  18.6 3.7 %copy.69 = bf16[8,4,128,256]{3,1,2,0:T(4,128)(2,1)} copy(bf16[8,4,128,256]{3,1,0,2:T(4,128)(2,1)} %reshape.212) | data formatting | bytes 4194304 | tf_op jit(solution)/shard_map/reshape | solution.py:345
  22.3 6.3 %all-to-all-start = ((bf16[8,4,128,256]{3,1,2,0:T(4,128)(2,1)}), bf16[8,4,128,256]{3,1,2,0:T(4,128)(2,1)S(1)}, u32[]{:S(2)}, u32[]{:S(2)}) async-start(bf16[8,4,128,256]{3,1,2,0:T(4,128)(2,1)} %copy.69), calls=%async_computation | async-start | bytes 4194304 | tf_op jit(solution)/shard_map/all_to_all | solution.py:346
  30.1 25.5 %all-to-all-done = bf16[8,4,128,256]{3,1,2,0:T(4,128)(2,1)S(1)} async-done(((bf16[8,4,128,256]{3,1,2,0:T(4,128)(2,1)}), bf16[8,4,128,256]{3,1,2,0:T(4,128)(2,1)S(1)}, u32[]{:S(2)}, u32[]{:S(2)}) %all-to-all-start) | async-done | bytes 2097184 | tf_op jit(solution)/shard_map/all_to_all | solution.py:346
  55.7 2.3 convolution_bitcast_fusion.1
  58.0 46.6 %all-gather.2.cloned.1.call-done = bf16[16384,256]{1,0:T(8,128)(2,1)} async-done(((bf16[1024,256]{1,0:T(8,128)(2,1)}), bf16[16384,256]{1,0:T(8,128)(2,1)}) %all-gather.2.cloned.1.call-update) | async-done | bytes 8388624 | tf_op jit(solution)/shard_map/all_gather | solution.py:321
  104.6 19.7 %shard_map.139 = f32[8,128,256]{2,1,0:T(8,128)} custom-call(s32[512]{0:T(512)} %reshape_squeeze.6.rows_ref, s32[512]{0:T(512)} %reshape_squeeze.7.cols_ref, s32[16]{0:T(128)} %bitcast.171, bf16[16,32,128,128]{3,2,1,0:T(8,128)(2,1)} %bitcast.154, bf16[16,8,128,256]{3,2,1,0:T(8,128)(2,1)} %bitcast.157), custom_call_target="tpu_custom_call" | custom-call | flops 4294967296 | bytes 25165824 | tf_op jit(solution)/shard_map/pallas_call | solution.py:98
  124.3 1.7 copy_add_fusion.1
  126.0 1.4 fusion.8
  127.5 21.8 %shard_map.140 = (bf16[8,8,128,256]{3,2,1,0:T(8,128)(2,1)}, bf16[8,8,128,256]{3,2,1,0:T(8,128)(2,1)}) custom-call(s32[512]{0:T(512)} %reshape_squeeze.6.rows_ref, s32[512]{0:T(512)} %reshape_squeeze.7.cols_ref, s32[16]{0:T(128)} %bitcast.172, s32[1]{0:T(128)} %bitcast.18.core_ref, bf16[16,32,128,128]{3,2,1,0:T(8,128)(2,1)} %bitcast.155, ...), custom_call_target="tpu_custom_call" | custom-call | flops 4294967296 | bytes 33554432 | tf_op jit(solution)/shard_map/pallas_call | solution.py:131
  149.3 1.4 collective-permute-start
  152.2 5.7 %collective-permute-done = bf16[8,8,128,256]{3,2,1,0:T(8,128)(2,1)} collective-permute-done((bf16[8,8,128,256]{3,2,1,0:T(8,128)(2,1)}, bf16[8,8,128,256]{3,2,1,0:T(8,128)(2,1)}, u32[]{:S(2)}, u32[]{:S(2)}) %collective-permute-start) | collective-permute-done | bytes 4194336 | tf_op jit(solution)/shard_map/ppermute | solution.py:365
  157.8 7.3 %add_convert_fusion = bf16[8,8,128,256]{3,2,1,0:T(8,128)(2,1)} fusion(bf16[8,8,128,256]{3,2,1,0:T(8,128)(2,1)} %collective-permute-done, bf16[8,8,128,256]{3,2,1,0:T(8,128)(2,1)} %get-tuple-element.5), kind=kLoop, calls=%fused_computation.3 | loop fusion | flops 8388608 | bytes 12582912 | tf_op jit(solution)/shard_map/convert_element_type | solution.py:366
  165.2 4.7 %all-to-all-start.1 = ((bf16[8,8,128,256]{3,2,1,0:T(8,128)(2,1)}), bf16[8,8,128,256]{3,2,1,0:T(8,128)(2,1)}, u32[]{:S(2)}, u32[]{:S(2)}) async-start(bf16[8,8,128,256]{3,2,1,0:T(8,128)(2,1)} %add_convert_fusion), calls=%async_computation.1 | async-start | bytes 8388608 | tf_op jit(solution)/shard_map/all_to_all | solution.py:367
  169.9 4.8 %fusion.89 = (bf16[1,4,128,256]{3,0,2,1:T(2,128)(2,1)S(1)}, bf16[1,4,128,256]{3,0,2,1:T(2,128)(2,1)S(1)}, bf16[1,4,128,256]{3,0,2,1:T(2,128)(2,1)S(1)}, bf16[1,4...) fusion(bf16[8,4,128,256]{3,0,2,1:T(8,128)(2,1)S(1)} %convolutio, ...), kind=kLoop, calls=%fused_computation.146 | loop fusion | bytes 4194304 | tf_op jit(solution)/shard_map/slice | solution.py:380
  177.1 2.1 collective-permute-start.1
  179.3 2.1 collective-permute-start.2
  182.0 2.3 collective-permute-start.4
  184.9 23.4 %collective-permute-done.6 = bf16[4,128,256]{2,0,1:T(4,128)(2,1)S(1)} collective-permute-done((bf16[4,128,256]{2,0,1:T(4,128)(2,1)S(1)}, bf16[4,128,256]{2,0,1:T(4,128)(2,1)S(1)}, u32[]{:S(2)}, u32[]{:S(2)}) %collective-permute-start.6) | collective-permute-done | bytes 262176 | tf_op jit(solution)/shard_map/ppermute | solution.py:380
  208.3 18.3 %collective-permute-start.5 = (bf16[4,128,256]{2,0,1:T(4,128)(2,1)S(1)}, bf16[4,128,256]{2,0,1:T(4,128)(2,1)S(1)}, u32[]{:S(2)}, u32[]{:S(2)}) collective-permute-start(bf16[4,128,256]{2,0,1:T(4,128)(2,1)S(1)} %bitcast.167), channel_id=1, source_target_pairs={{0,80},{16,96},{32,112},{48,0},{64,16},{80,32},{96,48},{112,64},{1... | collective-permute-start | bytes 786440 | tf_op jit(solution)/shard_map/ppermute | solution.py:380
  227.2 3.7 %collective-permute-done.5 = bf16[4,128,256]{2,0,1:T(4,128)(2,1)S(1)} collective-permute-done((bf16[4,128,256]{2,0,1:T(4,128)(2,1)S(1)}, bf16[4,128,256]{2,0,1:T(4,128)(2,1)S(1)}, u32[]{:S(2)}, u32[]{:S(2)}) %collective-permute-start.5) | collective-permute-done | bytes 262176 | tf_op jit(solution)/shard_map/ppermute | solution.py:380
  232.5 6.3 %collective-permute-done.4 = bf16[4,128,256]{2,0,1:T(4,128)(2,1)S(1)} collective-permute-done((bf16[4,128,256]{2,0,1:T(4,128)(2,1)S(1)}, bf16[4,128,256]{2,0,1:T(4,128)(2,1)S(1)}, u32[]{:S(2)}, u32[]{:S(2)}) %collective-permute-start.4) | collective-permute-done | bytes 262176 | tf_op jit(solution)/shard_map/ppermute | solution.py:380
  241.2 1.1 add_convert_fusion.1
  242.8 2.0 copy.83
  244.9 3.2 %convert_reduce_fusion = f32[8,128,256]{2,1,0:T(8,128)S(1)} fusion(bf16[8,8,128,256]{3,2,1,0:T(8,128)(2,1)} %all-to-all-done.1), kind=kLoop, calls=%fused_computation.2 | loop fusion | flops 3932160 | bytes 5242880 | tf_op jit(solution)/shard_map/reduce_sum | solution.py:370
  248.0 1.3 fusion.9
  250.3 1.1 convolution_convert_fusion.3
  252.3 26.7 %shard_map.141 = f32[16,32,128]{2,1,0:T(8,128)} custom-call(f32[16,32,128]{2,1,0:T(8,128)} %reshape.216.x_ref), custom_call_target="tpu_custom_call" | custom-call | tf_op jit(solution)/shard_map/pallas_call | solution.py:219
  (82 shorter events, 16.7 us)
Async XLA Ops:
  7.2 4.7 %copy-start = (bf16[1,1,16,128,128]{4,3,2,1,0:T(8,128)(2,1)S(1)}, bf16[1,1,16,128,128]{4,3,2,1,0:T(8,128)(2,1)}, u32[]{:S(2)}) copy-start(bf16[1,1,16,128,128]{4,3,2,1,0:T(8,128)(2,1)} %param.20) | copy-start | bytes 1572868
  7.2 4.6 %copy-start.11 = (s32[1,1,16]{2,1,0:T(1,128)S(1)}, s32[1,1,16]{2,1,0:T(1,128)}, u32[]{:S(2)}) copy-start(s32[1,1,16]{2,1,0:T(1,128)} %param.21) | copy-start | bytes 196
  7.2 97.4 %all-gather.2.cloned.1.call-start = ((), (), s32[]{:S(2)}) async-start(), calls=%async_computation.2 | async-start | bytes 8912896 | tf_op jit(solution)/shard_map/all_gather | solution.py:321
  11.8 2.3 copy-start.7
  22.3 6.3 %copy-start.8 = (s32[1,1,16,32]{3,2,1,0:T(8,128)S(1)}, s32[1,1,16,32]{3,2,1,0:T(8,128)}, u32[]{:S(2)}) copy-start(s32[1,1,16,32]{3,2,1,0:T(8,128)} %param.17) | copy-start | bytes 6148
  22.3 7.0 %copy-start.9 = (s32[1,1,16,32]{3,2,1,0:T(8,128)S(1)}, s32[1,1,16,32]{3,2,1,0:T(8,128)}, u32[]{:S(2)}) copy-start(s32[1,1,16,32]{3,2,1,0:T(8,128)} %param.18) | copy-start | bytes 6148
  22.3 7.7 %copy-start.10 = (s32[1024]{0:T(1024)S(1)}, s32[1024]{0:T(1024)}, u32[]{:S(2)}) copy-start(s32[1024]{0:T(1024)} %param.15) | copy-start | bytes 12292
  22.3 7.7 %copy-start.12 = (s32[8,1,16]{2,1,0:T(1,128)S(1)}, s32[8,1,16]{2,1,0:T(1,128)}, u32[]{:S(2)}) copy-start(s32[8,1,16]{2,1,0:T(1,128)} %param.23) | copy-start | bytes 1540
  22.3 33.4 %all-to-all-start = ((bf16[8,4,128,256]{3,1,2,0:T(4,128)(2,1)}), bf16[8,4,128,256]{3,1,2,0:T(4,128)(2,1)S(1)}, u32[]{:S(2)}, u32[]{:S(2)}) async-start(bf16[8,4,128,256]{3,1,2,0:T(4,128)(2,1)} %copy.69), calls=%async_computation | async-start | bytes 4194304 | tf_op jit(solution)/shard_map/all_to_all | solution.py:346
  104.6 19.7 %copy-start.4 = (f32[8,128,256]{2,0,1:T(8,128)S(1)}, f32[8,128,256]{2,0,1:T(8,128)}, u32[]{:S(2)}) copy-start(f32[8,128,256]{2,0,1:T(8,128)} %convolution_bitcast_fusion.1) | copy-start | bytes 3145732
  124.3 1.7 copy-start.5
  127.5 24.0 %copy-start.2 = (bf16[1024,256]{1,0:T(8,128)(2,1)S(1)}, bf16[1024,256]{1,0:T(8,128)(2,1)}, u32[]{:S(2)}) copy-start(bf16[1024,256]{1,0:T(8,128)(2,1)} %get-tuple-element.15) | copy-start | bytes 1572868
  149.3 8.6 %collective-permute-start = (bf16[8,8,128,256]{3,2,1,0:T(8,128)(2,1)}, bf16[8,8,128,256]{3,2,1,0:T(8,128)(2,1)}, u32[]{:S(2)}, u32[]{:S(2)}) collective-permute-start(bf16[8,8,128,256]{3,2,1,0:T(8,128)(2,1)} %get-tuple-element.6), channel_id=1, source_target_pairs={{0,1},{1,0},{2,3},{3,2},{4,5},{5,4},{6,7},{7,6},{8,9},{9,8},{10,11... | collective-permute-start | bytes 12582920 | tf_op jit(solution)/shard_map/ppermute | solution.py:365
  165.2 79.7 %all-to-all-start.1 = ((bf16[8,8,128,256]{3,2,1,0:T(8,128)(2,1)}), bf16[8,8,128,256]{3,2,1,0:T(8,128)(2,1)}, u32[]{:S(2)}, u32[]{:S(2)}) async-start(bf16[8,8,128,256]{3,2,1,0:T(8,128)(2,1)} %add_convert_fusion), calls=%async_computation.1 | async-start | bytes 8388608 | tf_op jit(solution)/shard_map/all_to_all | solution.py:367
  177.1 63.5 %collective-permute-start.1 = (bf16[4,128,256]{2,0,1:T(4,128)(2,1)S(1)}, bf16[4,128,256]{2,0,1:T(4,128)(2,1)S(1)}, u32[]{:S(2)}, u32[]{:S(2)}) collective-permute-start(bf16[4,128,256]{2,0,1:T(4,128)(2,1)S(1)} %bitcast.163), channel_id=1, source_target_pairs={{0,16},{16,32},{32,48},{48,64},{64,80},{80,96},{96,112},{112,0},{1... | collective-permute-start | bytes 786440 | tf_op jit(solution)/shard_map/ppermute | solution.py:380
  179.3 60.8 %collective-permute-start.2 = (bf16[4,128,256]{2,0,1:T(4,128)(2,1)S(1)}, bf16[4,128,256]{2,0,1:T(4,128)(2,1)S(1)}, u32[]{:S(2)}, u32[]{:S(2)}) collective-permute-start(bf16[4,128,256]{2,0,1:T(4,128)(2,1)S(1)} %bitcast.164), channel_id=1, source_target_pairs={{0,32},{16,48},{32,64},{48,80},{64,96},{80,112},{96,0},{112,16},{1... | collective-permute-start | bytes 786440 | tf_op jit(solution)/shard_map/ppermute | solution.py:380
  181.3 58.1 %collective-permute-start.3 = (bf16[4,128,256]{2,0,1:T(4,128)(2,1)S(1)}, bf16[4,128,256]{2,0,1:T(4,128)(2,1)S(1)}, u32[]{:S(2)}, u32[]{:S(2)}) collective-permute-start(bf16[4,128,256]{2,0,1:T(4,128)(2,1)S(1)} %bitcast.165), channel_id=1, source_target_pairs={{0,48},{16,64},{32,80},{48,96},{64,112},{80,0},{96,16},{112,32},{1... | collective-permute-start | bytes 786440 | tf_op jit(solution)/shard_map/ppermute | solution.py:380
  182.0 56.8 %collective-permute-start.4 = (bf16[4,128,256]{2,0,1:T(4,128)(2,1)S(1)}, bf16[4,128,256]{2,0,1:T(4,128)(2,1)S(1)}, u32[]{:S(2)}, u32[]{:S(2)}) collective-permute-start(bf16[4,128,256]{2,0,1:T(4,128)(2,1)S(1)} %bitcast.166), channel_id=1, source_target_pairs={{0,64},{16,80},{32,96},{48,112},{64,0},{80,16},{96,32},{112,48},{1... | collective-permute-start | bytes 786440 | tf_op jit(solution)/shard_map/ppermute | solution.py:380
  184.3 24.0 %collective-permute-start.6 = (bf16[4,128,256]{2,0,1:T(4,128)(2,1)S(1)}, bf16[4,128,256]{2,0,1:T(4,128)(2,1)S(1)}, u32[]{:S(2)}, u32[]{:S(2)}) collective-permute-start(bf16[4,128,256]{2,0,1:T(4,128)(2,1)S(1)} %bitcast.168), channel_id=1, source_target_pairs={{0,96},{16,112},{32,0},{48,16},{64,32},{80,48},{96,64},{112,80},{1... | collective-permute-start | bytes 786440 | tf_op jit(solution)/shard_map/ppermute | solution.py:380
  208.3 22.6 %collective-permute-start.5 = (bf16[4,128,256]{2,0,1:T(4,128)(2,1)S(1)}, bf16[4,128,256]{2,0,1:T(4,128)(2,1)S(1)}, u32[]{:S(2)}, u32[]{:S(2)}) collective-permute-start(bf16[4,128,256]{2,0,1:T(4,128)(2,1)S(1)} %bitcast.167), channel_id=1, source_target_pairs={{0,80},{16,96},{32,112},{48,0},{64,16},{80,32},{96,48},{112,64},{1... | collective-permute-start | bytes 786440 | tf_op jit(solution)/shard_map/ppermute | solution.py:380
  231.0 10.3 %collective-permute-start.7 = (bf16[4,128,256]{2,0,1:T(4,128)(2,1)S(1)}, bf16[4,128,256]{2,0,1:T(4,128)(2,1)S(1)}, u32[]{:S(2)}, u32[]{:S(2)}) collective-permute-start(bf16[4,128,256]{2,0,1:T(4,128)(2,1)S(1)} %bitcast.162), channel_id=1, source_target_pairs={{0,112},{16,0},{32,16},{48,32},{64,48},{80,64},{96,80},{112,96},{1... | collective-permute-start | bytes 786440 | tf_op jit(solution)/shard_map/ppermute | solution.py:380
  244.9 3.2 %copy-start.1 = (f32[16,128,256]{2,0,1:T(8,128)S(1)}, f32[16,128,256]{2,0,1:T(8,128)}, u32[]{:S(2)}) copy-start(f32[16,128,256]{2,0,1:T(8,128)} %copy.83) | copy-start | bytes 6291460
  248.0 1.5 copy-start.3
  249.4 0.9 copy-start.6
Sparse Core Ops, SparseCore 0:
  11.0 93.5 all-gather.1
